TPU v7x, 512 devices: a whole 4x8x8 slice. The times are simulated.
512 devices in a mesh: dp: 32 (over y_hi, x, core), tensor: 16 (over z, y_lo).
Axes of the slice: x: 4, y: 8 (y_hi: 4, y_lo: 2; y = y_hi * 2 + y_lo), z: 8, core: 2. Of those that a mesh axis runs over, the one named last changes fastest.
Arguments:
- tokens: bfloat16 [12288, 2048], P('dp'), may hold values from -6 to 6
- out_grad: bfloat16 [12288, 7168], P('dp', 'tensor'), may hold values from -6 to 6
- gate_weight: bfloat16 [2048, 7168], P('dp', 'tensor'), may hold values from -0.1875 to 0.1875
- up_weight: bfloat16 [2048, 7168], P('dp', 'tensor'), may hold values from -0.1875 to 0.1875
- gate_mask: int32 [32, 112], P('dp', 'tensor'), may hold values 0 or 1
- up_mask: int32 [32, 112], P('dp', 'tensor'), may hold values 0 or 1
Outputs:
- hidden: float32 [12288, 7168], P('dp', 'tensor')
- grad_tokens: bfloat16 [12288, 2048], P('dp')
- grad_gate: float32 [2048, 7168], P('dp', 'tensor')
- grad_up: float32 [2048, 7168], P('dp', 'tensor')
All inputs are finite; a program needn't handle non-finite values. No bound on the sum of `gate_mask` or of `up_mask` on one device may be relied on, other than what follows from the above.
Results may differ from a plain program's by a relative error of at most 0.014.
Values may be sent and summed in bfloat16 or wider, within the bound.
No kernel may reach another device: no remote copies, remote signals or barrier semaphores. Data moves between devices by JAX's collectives and lax.ppermute only.
A program may use at most 64 MiB of HBM per device.

v0:
```python
import jax
import jax.numpy as jnp
from jax import lax
from jax.sharding import PartitionSpec as P

BLOCK = 64


def expand(block_mask):
    height, breadth = block_mask.shape
    values = block_mask.astype(jnp.float32)
    return jnp.broadcast_to(values[:, None, :, None], (height, BLOCK, breadth, BLOCK)).reshape(
        height * BLOCK, breadth * BLOCK
    )


def local(tokens, out_grad, gate_weight, up_weight, gate_mask, up_mask):
    gate_keep = expand(gate_mask)
    up_keep = expand(up_mask)
    gate_eff = gate_weight * gate_keep.astype(jnp.bfloat16)
    up_eff = up_weight * up_keep.astype(jnp.bfloat16)
    local_both = jnp.concatenate([gate_eff, up_eff], axis=1)
    hidden_width = gate_weight.shape[1]
    gathered = lax.all_gather(local_both, "dp", axis=0, tiled=True)
    preact = jnp.dot(tokens, gathered, preferred_element_type=jnp.float32)
    gate = preact[:, :hidden_width]
    up = preact[:, hidden_width:]
    sigmoid_gate = jax.nn.sigmoid(gate)
    activation = gate * sigmoid_gate
    hidden = activation * up
    grad_float = out_grad.astype(jnp.float32)
    d_gate = (grad_float * up * sigmoid_gate * (1.0 + gate * (1.0 - sigmoid_gate))).astype(
        jnp.bfloat16
    )
    d_up = (grad_float * activation).astype(jnp.bfloat16)
    d_both = jnp.concatenate([d_gate, d_up], axis=1)
    partial_input = lax.dot_general(
        d_both, gathered, (((1,), (1,)), ((), ())), preferred_element_type=jnp.float32
    )
    grad_tokens = lax.psum(partial_input, "tensor").astype(jnp.bfloat16)
    summed = lax.psum_scatter(
        lax.dot_general(
            tokens, d_both, (((0,), (0,)), ((), ())), preferred_element_type=jnp.float32
        ).astype(jnp.bfloat16),
        "dp",
        scatter_dimension=0,
        tiled=True,
    ).astype(jnp.float32)
    grad_gate = summed[:, :hidden_width] * gate_keep
    grad_up = summed[:, hidden_width:] * up_keep
    return (hidden, grad_tokens, grad_gate, grad_up)


def solution(mesh):
    placed = (
        P("dp", None),
        P("dp", "tensor"),
        P("dp", "tensor"),
        P("dp", "tensor"),
        P("dp", "tensor"),
        P("dp", "tensor"),
    )
    return jax.shard_map(
        local,
        mesh=mesh,
        in_specs=placed,
        out_specs=(P("dp", "tensor"), P("dp", None), P("dp", "tensor"), P("dp", "tensor")),
        check_vma=False,
    )
```

profile of v0, /device:TPU:2, one launch (start us, length us, event | category | flops | bytes accessed | tf_op | source)
XLA Modules:
  0.0 270.0 jit_solution(18201012500881110290)
XLA Ops:
  7.2 0.0 copy-start
  7.2 0.0 all-gather.2.cloned.1.call-start
  7.2 0.8 convert_bitcast_fusion.2
  8.0 0.7 convert_bitcast_fusion.1
  8.7 0.1 broadcast_in_dim.33
  8.7 0.1 broadcast_in_dim.34
  8.8 0.1 broadcast_in_dim.29
  8.9 0.1 broadcast_in_dim.30
  9.0 0.9 broadcast_multiply_fusion
  9.9 0.7 pad_maximum_fusion.3
  10.6 0.0 all-gather.2.cloned.1.call-update
  10.6 0.0 copy-start.1
  10.6 0.0 reduce-scatter.4.cloned.1.call-start
  10.7 69.7 %all-gather.2.cloned.1.call-done = bf16[2048,896]{1,0:T(8,128)(2,1)} async-done(((bf16[64,896]{1,0:T(8,128)(2,1)}), bf16[2048,896]{1,0:T(8,128)(2,1)}) %all-gather.2.cloned.1.call-update) | async-done | bytes 3670032 | tf_op jit(solution)/shard_map/all_gather | solution.py:24
  80.3 0.0 copy-done
  80.3 4.1 %convolution_bitcast_fusion = f32[384,896]{0,1:T(8,128)S(1)} fusion(bf16[2048,896]{1,0:T(8,128)(2,1)} %all-gather.2.cloned.1.call-done, bf16[384,2048]{1,0:T(8,128)(2,1)S(1)} %copy-done), kind=kOutput, calls=%fused_computation.1 | convolution fusion | flops 1409286144 | bytes 6619136 | tf_op jit(solution)/shard_map/dot_general | solution.py:25
  84.5 0.0 copy-done.1
  84.5 1.3 fusion.2
  85.7 4.0 %convert_bitcast_fusion = bf16[2048,896]{0,1:T(8,128)(2,1)} fusion(bf16[384,2048]{1,0:T(8,128)(2,1)S(1)} %copy-done, bf16[384,448]{0,1:T(8,128)(2,1)S(1)} %get-tuple-element.13, bf16[384,448]{0,1:T(8,128)(2,1)S(1)} %get-tuple-element.12), kind=kOutput, calls=%fused_computation | convolution fusion | flops 1412497408 | bytes 5931008 | tf_op jit(solution)/shard_map/dot_general | solution.py:42
  89.7 6.1 %copy.14 = bf16[2048,896]{1,0:T(8,128)(2,1)} copy(bf16[2048,896]{0,1:T(8,128)(2,1)} %convert_bitcast_fusion) | data formatting | bytes 7340032
  95.8 0.0 reduce-scatter.4.cloned.1.call-update
  95.8 5.6 %fusion.5 = f32[384,2048]{1,0:T(8,128)} fusion(bf16[2048,896]{1,0:T(8,128)(2,1)} %all-gather.2.cloned.1.call-done, bf16[384,448]{0,1:T(8,128)(2,1)S(1)} %get-tuple-element.13, bf16[384,448]{0,1:T(8,128)(2,1)S(1)} %get-tuple-element.12), kind=kOutput, calls=%fused_computation.12 | convolution fusion | flops 1410662400 | bytes 7503872 | tf_op jit(solution)/shard_map/dot_general | solution.py:37
  101.4 158.8 %all-reduce.1 = bf16[384,2048]{1,0:T(8,128)(2,1)} all-reduce(f32[384,2048]{1,0:T(8,128)} %fusion.5), channel_id=1, replica_groups=mesh['dp'=32,'tensor'=16] {'tensor'}, use_global_device_ids=true, to_apply=%region_0.0 | all-reduce | flops 786432 | bytes 4718592 | tf_op jit(solution)/shard_map/psum | solution.py:40
  260.3 0.0 reduce-scatter.4.cloned.1.call-done
  260.3 1.1 copy.15
  261.4 0.2 slice_multiply_fusion.1
  261.6 0.8 copy.13
  262.4 0.8 copy.12
  (3 shorter events, 0.0 us)
Async XLA Ops:
  7.2 73.2 %copy-start = (bf16[384,2048]{1,0:T(8,128)(2,1)S(1)}, bf16[384,2048]{1,0:T(8,128)(2,1)}, u32[]{:S(2)}) copy-start(bf16[384,2048]{1,0:T(8,128)(2,1)} %param.6) | copy-start | bytes 4718596
  7.2 73.1 %all-gather.2.cloned.1.call-start = ((), (), s32[]{:S(2)}) async-start(), calls=%async_computation.1 | async-start | bytes 3784704 | tf_op jit(solution)/shard_map/all_gather | solution.py:24
  10.6 73.9 %copy-start.1 = (bf16[384,448]{0,1:T(8,128)(2,1)S(1)}, bf16[384,448]{0,1:T(8,128)(2,1)}, u32[]{:S(2)}) copy-start(bf16[384,448]{0,1:T(8,128)(2,1)} %param.7) | copy-start | bytes 1032196
  10.6 249.7 %reduce-scatter.4.cloned.1.call-start = ((), (), s32[]{:S(2)}) async-start(), calls=%async_computation.2 | async-start | bytes 3784704
Sparse Core Ops, SparseCore 0:
  11.7 68.5 all-gather.1
  96.0 108.4 reduce-scatter.3
where the time goes:
time: 270 us
  blocking collectives  159 us (59%)
  waiting for transfers between devices  69.7 us (26%)
  between operations  14.1 us (5%)
  matrix products  13.7 us (5%)
  local copies, waits for them, and re-layouts  8.99 us (3%)
  other arithmetic  4.54 us (2%)
    psum x1, blocking collectives, local(): grad_tokens = lax.psum(partial_input, 'tensor').astype(jnp.bfloat16)  159 us
    all_gather x1, waiting for transfers between devices, local(): gathered = lax.all_gather(local_both, 'dp', axis=0, tiled=True)  69.7 us
    unnamed x8, local copies, waits for them, and re-layouts  8.7 us
    dot_general x1, matrix products, local(): lax.dot_general(d_both, gathered, (((1,), (1,)), ((), ())), preferred_ele...  5.62 us
  transfers between devices with their start and end apart: 2, of which 1 were waited for; matrix products, arithmetic and copies ran while one was open for 2% of the time, Pallas kernels for 0%

commit v1 on v0

v1 whole, which is shorter than its diff:
```python
import jax
import jax.numpy as jnp
import numpy as np
from jax import lax
from jax.experimental import pallas as pl
from jax.experimental.pallas import tpu as pltpu
from jax.sharding import Mesh
from jax.sharding import PartitionSpec as P

BLOCK = 64
BF16 = jnp.bfloat16
F32 = jnp.float32
YH, X, CORE, Z, YL = 4, 4, 2, 8, 2
VM = pl.BlockSpec(memory_space=pltpu.VMEM)
SM = pl.BlockSpec(memory_space=pltpu.SMEM)


def keep_row(mask_ref, width):
    column = lax.broadcasted_iota(jnp.int32, (1, width), 1) // BLOCK
    keep = jnp.zeros((1, width), F32)
    for block in range(width // BLOCK):
        keep = jnp.where(column == block, mask_ref[0, block].astype(F32), keep)
    return keep


def mask_kernel(gm, um, gw, uw, out):
    width = gw.shape[1]
    gate = gw[...].astype(F32) * keep_row(gm, width)
    up = uw[...].astype(F32) * keep_row(um, width)
    both = jnp.concatenate([gate, up], axis=1).astype(BF16)
    for copy in range(YH):
        out[copy] = both


def forward_kernel(place, tokens, ogt, mine, other, hidden_t, d_both, send, keep, w):
    core = place[0]
    half = place[1]
    width = ogt.shape[0]
    for yh in range(YH):
        for x in range(X):
            w[yh * X + x, core] = mine[x, yh]
            w[yh * X + x, 1 - core] = other[x, yh]
    weights = w[...].reshape(YH * X * CORE * BLOCK, 2 * width)
    preact = jnp.dot(tokens[...], weights, preferred_element_type=F32)
    gate = preact[:, :width]
    up = preact[:, width:]
    sigmoid = jax.nn.sigmoid(gate)
    activation = gate * sigmoid
    hidden_t[...] = (activation * up).T
    grad = ogt[...].astype(F32).T
    d_gate = grad * up * sigmoid * (1.0 + gate * (1.0 - sigmoid))
    d_up = grad * activation
    d_both[...] = jnp.concatenate([d_gate, d_up], axis=1).astype(BF16)
    rows = send.shape[0]

    def partial(index):
        part = d_both[pl.ds(pl.multiple_of(index * rows, rows), rows), :]
        return lax.dot_general(
            part, weights, (((1,), (1,)), ((), ())), preferred_element_type=F32
        ).astype(BF16)

    send[...] = partial(1 - half)
    keep[...] = partial(half)


def weight_kernel(place, tokens, d_both, keep, send):
    core = place[0]
    rows = CORE * BLOCK * 2
    for step in range(YH * X // 2):
        both = lax.dot_general(
            tokens[:, step * rows : (step + 1) * rows],
            d_both[...],
            (((0,), (0,)), ((), ())),
            preferred_element_type=F32,
        ).astype(BF16)
        for pair in range(2):
            yh, x = divmod(step * 2 + pair, X)
            low = both[pair * 128 : pair * 128 + 64]
            high = both[pair * 128 + 64 : pair * 128 + 128]
            first = core == 0
            keep[x, yh] = jnp.where(first, low, high)
            send[x, yh] = jnp.where(first, high, low)


def final_kernel(gm, um, parts, grad_gate, grad_up):
    width = grad_gate.shape[1]
    total = parts[0].astype(F32)
    for source in range(1, YH):
        total = total + parts[source].astype(F32)
    grad_gate[...] = total[:, :width] * keep_row(gm, width)
    grad_up[...] = total[:, width:] * keep_row(um, width)


def shape(dims, dtype=BF16):
    return jax.ShapeDtypeStruct(dims, dtype)


def params():
    return pltpu.CompilerParams(vmem_limit_bytes=40 << 20)


def swap(array, axis):
    return lax.ppermute(array, axis, [(0, 1), (1, 0)])


def local(tokens, out_grad, gate_weight, up_weight, gate_mask, up_mask):
    width = gate_weight.shape[1]
    count, features = tokens.shape
    half = count // YL
    chunk = half // Z
    place = jnp.stack([lax.axis_index("core"), lax.axis_index("yl")]).astype(jnp.int32)
    with jax.named_scope("mask"):
        copies = pl.pallas_call(
            mask_kernel,
            in_specs=[SM, SM, VM, VM],
            out_specs=VM,
            out_shape=shape((YH, BLOCK, 2 * width)),
        )(gate_mask, up_mask, gate_weight, up_weight)
    with jax.named_scope("gather_yh"):
        rows = lax.all_to_all(copies, "yh", 0, 0, tiled=True)
    with jax.named_scope("gather_x"):
        rows = jnp.broadcast_to(rows[None], (X,) + rows.shape)
        mine = lax.all_to_all(rows, "x", 0, 0, tiled=True)
    with jax.named_scope("gather_core"):
        other = swap(mine, "core")
    with jax.named_scope("forward"):
        hidden_t, d_both, send, keep = pl.pallas_call(
            forward_kernel,
            in_specs=[SM, VM, VM, VM, VM],
            out_specs=[VM] * 4,
            out_shape=[
                shape((width, count), F32),
                shape((count, 2 * width)),
                shape((half, features)),
                shape((half, features)),
            ],
            scratch_shapes=[pltpu.VMEM((YH * X, CORE, BLOCK, 2 * width), BF16)],
            compiler_params=params(),
        )(place, tokens, out_grad.T, mine, other)
    with jax.named_scope("tensor_yl"):
        received = swap(send, "yl")
    with jax.named_scope("weights"):
        w_keep, w_send = pl.pallas_call(
            weight_kernel,
            in_specs=[SM, VM, VM],
            out_specs=[VM] * 2,
            out_shape=[shape((X, YH, BLOCK, 2 * width))] * 2,
            compiler_params=params(),
        )(place, tokens, d_both)
    with jax.named_scope("scatter_core"):
        w_received = swap(w_send, "core")
    w_sum = (w_keep.astype(F32) + w_received.astype(F32)).astype(BF16)
    x_sum = (keep.astype(F32) + received.astype(F32)).astype(BF16)
    with jax.named_scope("scatter_x"):
        w_parts = lax.all_to_all(w_sum, "x", 0, 0, tiled=True)
    with jax.named_scope("tensor_z"):
        x_parts = lax.all_to_all(x_sum.reshape(Z, chunk, features), "z", 0, 0, tiled=True)
    w_sum = w_parts.astype(F32).sum(axis=0).astype(BF16)
    x_own = x_parts.astype(F32).sum(axis=0).astype(BF16)
    with jax.named_scope("scatter_yh"):
        w_parts = lax.all_to_all(w_sum, "yh", 0, 0, tiled=True)
    with jax.named_scope("tensor_back_z"):
        x_own = jnp.broadcast_to(x_own[None], (Z, chunk, features))
        x_half = lax.all_to_all(x_own, "z", 0, 0, tiled=True).reshape(half, features)
    with jax.named_scope("tensor_back_yl"):
        x_other = swap(x_half, "yl")
    with jax.named_scope("final"):
        grad_gate, grad_up = pl.pallas_call(
            final_kernel,
            in_specs=[SM, SM, VM],
            out_specs=[VM] * 2,
            out_shape=[shape((BLOCK, width), F32)] * 2,
        )(gate_mask, up_mask, w_parts)
    first = place[1] == 0
    grad_tokens = jnp.concatenate(
        [jnp.where(first, x_half, x_other), jnp.where(first, x_other, x_half)], axis=0
    )
    return (hidden_t.T, grad_tokens, grad_gate, grad_up)


def solution(mesh):
    fine = Mesh(
        np.asarray(mesh.devices).reshape(YH, X, CORE, Z, YL), ("yh", "x", "core", "z", "yl")
    )
    dp = ("yh", "x", "core")
    tensor = ("z", "yl")
    both = P(dp, tensor)
    return jax.shard_map(
        local,
        mesh=fine,
        in_specs=(P(dp, None), both, both, both, both, both),
        out_specs=(both, P(dp, None), both, both),
        check_vma=False,
    )
```

time: 270 us -> 202 us (0.75)
  the two profiles are of different devices: /device:TPU:2 before, /device:TPU:16 now
where the time goes in v1:
time: 202 us; the launch traced here: 201 us
  waiting for transfers between devices  93.5 us (46%)
  blocking collectives  48.7 us (24%)
  starting transfers between devices  30 us (15%)
  Pallas kernels  14.8 us (7%)
  other arithmetic  8.35 us (4%)
  local copies, waits for them, and re-layouts  4.95 us (2%)
    all_to_all x1, blocking collectives, local(): mine = lax.all_to_all(rows, 'x', 0, 0, tiled=True)  27.8 us
    ppermute x4, waiting for transfers between devices, swap(): return lax.ppermute(array, axis, [(0, 1), (1, 0)])  23.3 us
    all_to_all x1, waiting for transfers between devices, local(): w_parts = lax.all_to_all(w_sum, 'x', 0, 0, tiled=True)  21.3 us
    all_to_all x1, blocking collectives, local(): rows = lax.all_to_all(copies, 'yh', 0, 0, tiled=True)  20.9 us
    all_to_all x1, waiting for transfers between devices, local(): lax.all_to_all(x_own, 'z', 0, 0, tiled=True).reshape(half, features)  20.2 us
    all_to_all x1, waiting for transfers between devices, local(): lax.all_to_all(x_sum.reshape(Z, chunk, features), 'z', 0, 0, tiled=True)  15.6 us
    all_to_all x1, waiting for transfers between devices, local(): w_parts = lax.all_to_all(w_sum, 'yh', 0, 0, tiled=True)  13 us
    all_to_all x1, starting transfers between devices, local(): lax.all_to_all(x_sum.reshape(Z, chunk, features), 'z', 0, 0, tiled=True)  10.3 us
  transfers between devices with their start and end apart: 8, of which 6 were waited for; matrix products, arithmetic and copies ran while one was open for 3% of the time, Pallas kernels for 3%

profile of v1, /device:TPU:16, one launch (start us, length us, event | category | flops | bytes accessed | tf_op | source)
XLA Modules:
  0.0 201.1 jit_solution(3199923444754700980)
XLA Ops:
  0.6 1.8 mask.1
  2.4 20.9 %all_to_all.30 = bf16[4,64,896]{2,1,0:T(8,128)(2,1)S(1)} all-to-all(bf16[4,64,896]{2,1,0:T(8,128)(2,1)} %mask.1), channel_id=1, replica_groups=mesh['yh'=4,'x'=4,'core'=2,'z'=8,'yl'=2] {'yh'}, dimensions={0} | all-to-all | bytes 917504 | tf_op jit(solution)/shard_map/gather_yh/all_to_all | solution.py:120
  23.3 0.2 broadcast_in_dim.4
  23.6 0.0 copy-start
  23.6 27.8 %all_to_all.31.mine = bf16[4,4,64,896]{3,2,1,0:T(8,128)(2,1)S(1)} all-to-all(bf16[4,4,64,896]{3,2,1,0:T(8,128)(2,1)S(1)} %broadcast_in_dim.4), channel_id=1, replica_groups=mesh['yh'=4,'x'=4,'core'=2,'z'=8,'yl'=2] {'x'}, dimensions={0} | all-to-all | bytes 3670016 | tf_op jit(solution)/shard_map/gather_x/all_to_all | solution.py:123
  51.4 1.9 collective-permute-start
  53.3 0.1 pad_add_fusion.place
  53.4 3.8 %collective-permute-done.other = bf16[4,4,64,896]{3,2,1,0:T(8,128)(2,1)} collective-permute-done((bf16[4,4,64,896]{3,2,1,0:T(8,128)(2,1)S(1)}, bf16[4,4,64,896]{3,2,1,0:T(8,128)(2,1)}, u32[]{:S(2)}, u32[]{:S(2)}) %collective-permute-start) | collective-permute-done | bytes 1835040 | tf_op jit(solution)/shard_map/gather_core/ppermute | solution.py:103
  57.2 0.0 copy-done
  57.2 0.0 copy-start.3
  57.2 1.0 copy-done.3
  58.2 7.2 %forward.1 = (f32[448,384]{1,0:T(8,128)}, bf16[384,896]{1,0:T(8,128)(2,1)S(1)}, bf16[192,2048]{1,0:T(8,128)(2,1)S(1)}, bf16[192,2048]{1,0:T(8,128)(2,1)S(1)}) custom-call(s32[2]{0:T(128)S(1)} %pad_add_fusion.place, bf16[384,2048]{1,0:T(8,128)(2,1)S(1)} %copy-done, bf16[448,384]{1,0:T(8,128)(2,1)S(1)} %bitcast.8, ...), custom_call_target="tpu_custom_call" | custom-call | tf_op jit(solution)/shard_map/forward/pallas_call | solution.py:127
  65.4 0.0 copy-start.1
  65.4 1.9 collective-permute-start.1
  67.3 19.5 %collective-permute-done.1 = bf16[192,2048]{1,0:T(8,128)(2,1)S(1)} collective-permute-done((bf16[192,2048]{1,0:T(8,128)(2,1)S(1)}, bf16[192,2048]{1,0:T(8,128)(2,1)S(1)}, u32[]{:S(2)}, u32[]{:S(2)}) %collective-permute-start.1) | collective-permute-done | bytes 786464 | tf_op jit(solution)/shard_map/tensor_yl/ppermute | solution.py:103
  86.8 1.2 add_convert_fusion.1
  88.0 0.0 copy-done.1
  88.0 10.3 %all-to-all-start.2 = ((bf16[8,24,2048]{2,1,0:T(8,128)(2,1)}), bf16[8,24,2048]{2,1,0:T(8,128)(2,1)}, u32[]{:S(2)}, u32[]{:S(2)}) async-start(bf16[8,24,2048]{2,1,0:T(8,128)(2,1)} %bitcast.4), calls=%async_computation.2 | async-start | bytes 1572864 | tf_op jit(solution)/shard_map/tensor_z/all_to_all | solution.py:157
  98.3 0.0 copy-start.2
  98.3 1.1 copy-done.2
  99.4 4.0 %weights.1 = (bf16[4,4,64,896]{3,2,1,0:T(8,128)(2,1)S(1)}, bf16[4,4,64,896]{3,2,1,0:T(8,128)(2,1)}) custom-call(s32[2]{0:T(128)S(1)} %pad_add_fusion.place, bf16[384,2048]{1,0:T(8,128)(2,1)S(1)} %copy-done, bf16[384,896]{1,0:T(8,128)(2,1)S(1)} %copy-done.2), custom_call_target="tpu_custom_call" | custom-call | tf_op jit(solution)/shard_map/weights/pallas_call | solution.py:143
  103.4 1.9 collective-permute-start.3
  105.3 15.6 %all-to-all-done.2 = bf16[8,24,2048]{2,1,0:T(8,128)(2,1)} async-done(((bf16[8,24,2048]{2,1,0:T(8,128)(2,1)}), bf16[8,24,2048]{2,1,0:T(8,128)(2,1)}, u32[]{:S(2)}, u32[]{:S(2)}) %all-to-all-start.2) | async-done | bytes 786464 | tf_op jit(solution)/shard_map/tensor_z/all_to_all | solution.py:157
  121.0 1.2 reduce_sum.24
  122.2 1.0 broadcast_in_dim.5
  123.2 3.5 %all-to-all-start.3 = ((bf16[8,24,2048]{2,1,0:T(8,128)(2,1)}), bf16[8,24,2048]{2,1,0:T(8,128)(2,1)S(1)}, u32[]{:S(2)}, u32[]{:S(2)}) async-start(bf16[8,24,2048]{2,1,0:T(8,128)(2,1)} %broadcast_in_dim.5), calls=%async_computation.3 | async-start | bytes 1572864 | tf_op jit(solution)/shard_map/tensor_back_z/all_to_all | solution.py:164
  126.7 0.0 collective-permute-done.3
  126.8 3.3 %add_convert_fusion = bf16[4,4,64,896]{3,2,1,0:T(8,128)(2,1)} fusion(bf16[4,4,64,896]{3,2,1,0:T(8,128)(2,1)} %collective-permute-done.3, bf16[4,4,64,896]{3,2,1,0:T(8,128)(2,1)S(1)} %get-tuple-element.16), kind=kLoop, calls=%fused_computation | loop fusion | flops 3670016 | bytes 5505024 | tf_op jit(solution)/shard_map/convert_element_type | solution.py:152
  130.1 20.2 %all-to-all-done.3 = bf16[8,24,2048]{2,1,0:T(8,128)(2,1)S(1)} async-done(((bf16[8,24,2048]{2,1,0:T(8,128)(2,1)}), bf16[8,24,2048]{2,1,0:T(8,128)(2,1)S(1)}, u32[]{:S(2)}, u32[]{:S(2)}) %all-to-all-start.3) | async-done | bytes 786464 | tf_op jit(solution)/shard_map/tensor_back_z/all_to_all | solution.py:164
  150.2 0.0 copy-start.4
  150.2 0.9 copy-done.4
  151.1 3.6 %all-to-all-start.4 = ((bf16[4,4,64,896]{3,2,1,0:T(8,128)(2,1)}), bf16[4,4,64,896]{3,2,1,0:T(8,128)(2,1)S(1)}, u32[]{:S(2)}, u32[]{:S(2)}) async-start(bf16[4,4,64,896]{3,2,1,0:T(8,128)(2,1)} %add_convert_fusion), calls=%async_computation.4 | async-start | bytes 3670016 | tf_op jit(solution)/shard_map/scatter_x/all_to_all | solution.py:155
  154.7 0.0 copy-start.5
  154.7 2.6 %collective-permute-start.2 = (bf16[192,2048]{1,0:T(8,128)(2,1)}, bf16[192,2048]{1,0:T(8,128)(2,1)S(1)}, u32[]{:S(2)}, u32[]{:S(2)}) collective-permute-start(bf16[192,2048]{1,0:T(8,128)(2,1)} %bitcast.9), channel_id=1, source_target_pairs={{0,1},{1,0},{2,3},{3,2},{4,5},{5,4},{6,7},{7,6},{8,9},{9,8},{10,11... | collective-permute-start | bytes 2359304 | tf_op jit(solution)/shard_map/tensor_back_yl/ppermute | solution.py:103
  157.3 21.3 %all-to-all-done.4 = bf16[4,4,64,896]{3,2,1,0:T(8,128)(2,1)S(1)} async-done(((bf16[4,4,64,896]{3,2,1,0:T(8,128)(2,1)}), bf16[4,4,64,896]{3,2,1,0:T(8,128)(2,1)S(1)}, u32[]{:S(2)}, u32[]{:S(2)}) %all-to-all-start.4) | async-done | bytes 1835040 | tf_op jit(solution)/shard_map/scatter_x/all_to_all | solution.py:155
  178.7 1.2 reduce_sum.25
  179.8 4.2 %all-to-all-start.5 = ((bf16[4,64,896]{2,1,0:T(8,128)(2,1)}), bf16[4,64,896]{2,1,0:T(8,128)(2,1)S(1)}, u32[]{:S(2)}, u32[]{:S(2)}) async-start(bf16[4,64,896]{2,1,0:T(8,128)(2,1)} %reduce_sum.25), calls=%async_computation.5 | async-start | bytes 917504 | tf_op jit(solution)/shard_map/scatter_yh/all_to_all | solution.py:161
  184.0 13.0 %all-to-all-done.5.parts = bf16[4,64,896]{2,1,0:T(8,128)(2,1)S(1)} async-done(((bf16[4,64,896]{2,1,0:T(8,128)(2,1)}), bf16[4,64,896]{2,1,0:T(8,128)(2,1)S(1)}, u32[]{:S(2)}, u32[]{:S(2)}) %all-to-all-start.5) | async-done | bytes 458784 | tf_op jit(solution)/shard_map/scatter_yh/all_to_all | solution.py:161
  197.0 0.0 copy-start.6
  197.0 0.8 copy-done.6
  197.8 1.9 final.1
  199.7 0.0 collective-permute-done.2
  199.7 0.0 copy-done.5
  199.7 0.2 broadcast_select_fusion.1
  199.8 1.2 pad_maximum_fusion
Async XLA Ops:
  23.6 33.6 %copy-start = (bf16[384,2048]{1,0:T(8,128)(2,1)S(1)}, bf16[384,2048]{1,0:T(8,128)(2,1)}, u32[]{:S(2)}) copy-start(bf16[384,2048]{1,0:T(8,128)(2,1)} %tokens.3) | copy-start | bytes 4718596
  51.4 5.8 %collective-permute-start = (bf16[4,4,64,896]{3,2,1,0:T(8,128)(2,1)S(1)}, bf16[4,4,64,896]{3,2,1,0:T(8,128)(2,1)}, u32[]{:S(2)}, u32[]{:S(2)}) collective-permute-start(bf16[4,4,64,896]{3,2,1,0:T(8,128)(2,1)S(1)} %all_to_all.31.mine), channel_id=1, source_target_pairs={{0,16},{16,0},{1,17},{17,1},{2,18},{18,2},{3,19},{19,3},{4,20},{20... | collective-permute-start | bytes 5505032 | tf_op jit(solution)/shard_map/gather_core/ppermute | solution.py:103
  57.2 1.0 copy-start.3
  65.4 22.6 %copy-start.1 = (bf16[384,896]{1,0:T(8,128)(2,1)}, bf16[384,896]{1,0:T(8,128)(2,1)S(1)}, u32[]{:S(2)}) copy-start(bf16[384,896]{1,0:T(8,128)(2,1)S(1)} %get-tuple-element.15.d_both) | copy-start | bytes 2064388
  65.4 21.5 %collective-permute-start.1 = (bf16[192,2048]{1,0:T(8,128)(2,1)S(1)}, bf16[192,2048]{1,0:T(8,128)(2,1)S(1)}, u32[]{:S(2)}, u32[]{:S(2)}) collective-permute-start(bf16[192,2048]{1,0:T(8,128)(2,1)S(1)} %get-tuple-element.14), channel_id=1, source_target_pairs={{0,1},{1,0},{2,3},{3,2},{4,5},{5,4},{6,7},{7,6},{8,9},{9,8},{10,11... | collective-permute-start | bytes 2359304 | tf_op jit(solution)/shard_map/tensor_yl/ppermute | solution.py:103
  88.0 33.0 %all-to-all-start.2 = ((bf16[8,24,2048]{2,1,0:T(8,128)(2,1)}), bf16[8,24,2048]{2,1,0:T(8,128)(2,1)}, u32[]{:S(2)}, u32[]{:S(2)}) async-start(bf16[8,24,2048]{2,1,0:T(8,128)(2,1)} %bitcast.4), calls=%async_computation.2 | async-start | bytes 1572864 | tf_op jit(solution)/shard_map/tensor_z/all_to_all | solution.py:157
  98.3 1.1 copy-start.2
  103.4 23.3 %collective-permute-start.3 = (bf16[4,4,64,896]{3,2,1,0:T(8,128)(2,1)}, bf16[4,4,64,896]{3,2,1,0:T(8,128)(2,1)}, u32[]{:S(2)}, u32[]{:S(2)}) collective-permute-start(bf16[4,4,64,896]{3,2,1,0:T(8,128)(2,1)} %get-tuple-element.17), channel_id=1, source_target_pairs={{0,16},{16,0},{1,17},{17,1},{2,18},{18,2},{3,19},{19,3},{4,20},{20... | collective-permute-start | bytes 5505032 | tf_op jit(solution)/shard_map/scatter_core/ppermute | solution.py:103
  123.2 27.0 %all-to-all-start.3 = ((bf16[8,24,2048]{2,1,0:T(8,128)(2,1)}), bf16[8,24,2048]{2,1,0:T(8,128)(2,1)S(1)}, u32[]{:S(2)}, u32[]{:S(2)}) async-start(bf16[8,24,2048]{2,1,0:T(8,128)(2,1)} %broadcast_in_dim.5), calls=%async_computation.3 | async-start | bytes 1572864 | tf_op jit(solution)/shard_map/tensor_back_z/all_to_all | solution.py:164
  150.2 0.9 copy-start.4
  151.1 27.5 %all-to-all-start.4 = ((bf16[4,4,64,896]{3,2,1,0:T(8,128)(2,1)}), bf16[4,4,64,896]{3,2,1,0:T(8,128)(2,1)S(1)}, u32[]{:S(2)}, u32[]{:S(2)}) async-start(bf16[4,4,64,896]{3,2,1,0:T(8,128)(2,1)} %add_convert_fusion), calls=%async_computation.4 | async-start | bytes 3670016 | tf_op jit(solution)/shard_map/scatter_x/all_to_all | solution.py:155
  154.7 45.0 %copy-start.5 = (bf16[8,24,2048]{2,1,0:T(8,128)(2,1)S(1)}, bf16[8,24,2048]{2,1,0:T(8,128)(2,1)}, u32[]{:S(2)}) copy-start(bf16[8,24,2048]{2,1,0:T(8,128)(2,1)} %copy-done.4) | copy-start | bytes 2359300
  154.7 45.0 %collective-permute-start.2 = (bf16[192,2048]{1,0:T(8,128)(2,1)}, bf16[192,2048]{1,0:T(8,128)(2,1)S(1)}, u32[]{:S(2)}, u32[]{:S(2)}) collective-permute-start(bf16[192,2048]{1,0:T(8,128)(2,1)} %bitcast.9), channel_id=1, source_target_pairs={{0,1},{1,0},{2,3},{3,2},{4,5},{5,4},{6,7},{7,6},{8,9},{9,8},{10,11... | collective-permute-start | bytes 2359304 | tf_op jit(solution)/shard_map/tensor_back_yl/ppermute | solution.py:103
  179.8 17.2 %all-to-all-start.5 = ((bf16[4,64,896]{2,1,0:T(8,128)(2,1)}), bf16[4,64,896]{2,1,0:T(8,128)(2,1)S(1)}, u32[]{:S(2)}, u32[]{:S(2)}) async-start(bf16[4,64,896]{2,1,0:T(8,128)(2,1)} %reduce_sum.25), calls=%async_computation.5 | async-start | bytes 917504 | tf_op jit(solution)/shard_map/scatter_yh/all_to_all | solution.py:161
  197.0 0.8 copy-start.6

commit v2 on v1

v2 whole, which is shorter than its diff:
```python
import jax
import jax.numpy as jnp
import numpy as np
from jax import lax
from jax.experimental import pallas as pl
from jax.experimental.pallas import tpu as pltpu
from jax.sharding import Mesh
from jax.sharding import PartitionSpec as P


BLOCK = 64
BF16 = jnp.bfloat16
F32 = jnp.float32
YH, X, CORE, Z, YL = 4, 4, 2, 8, 2
PIECES = 2
VM = pl.BlockSpec(memory_space=pltpu.VMEM)
SM = pl.BlockSpec(memory_space=pltpu.SMEM)


def keep_row(mask_ref, width):
    column = lax.broadcasted_iota(jnp.int32, (1, width), 1) // BLOCK
    keep = jnp.zeros((1, width), F32)
    for block in range(width // BLOCK):
        keep = jnp.where(column == block, mask_ref[0, block].astype(F32), keep)
    return keep


def mask_kernel(gm, um, gw, uw, out):
    width = gw.shape[1]
    gate = gw[...].astype(F32) * keep_row(gm, width)
    up = uw[...].astype(F32) * keep_row(um, width)
    both = jnp.concatenate([gate, up], axis=1).astype(BF16)
    for copy in range(YH):
        out[copy] = both


def forward_kernel(place, tokens, ogt, *rest):
    mine, other = rest[:X], rest[X : 2 * X]
    hidden_t, d_both, *rest = rest[2 * X :]
    sends, keeps, w = rest[:PIECES], rest[PIECES:-1], rest[-1]
    core, half, own_x = place[0], place[1], place[2]
    width = ogt.shape[0]
    for yh in range(YH):
        for back in range(X):
            x = lax.rem(own_x + (X - back), X)
            w[yh * X + x, core] = mine[back][yh]
            w[yh * X + x, 1 - core] = other[back][yh]
    weights = w[...].reshape(YH * X * CORE * BLOCK, 2 * width)
    preact = jnp.dot(tokens[...], weights, preferred_element_type=F32)
    gate = preact[:, :width]
    up = preact[:, width:]
    sigmoid = jax.nn.sigmoid(gate)
    activation = gate * sigmoid
    hidden_t[...] = (activation * up).T
    grad = ogt[...].astype(F32).T
    d_gate = grad * up * sigmoid * (1.0 + gate * (1.0 - sigmoid))
    d_up = grad * activation
    d_both[...] = jnp.concatenate([d_gate, d_up], axis=1).astype(BF16)
    rows, columns = sends[0].shape
    for index, outs in ((1 - half, sends), (half, keeps)):
        part = d_both[pl.ds(pl.multiple_of(index * rows, rows), rows), :]
        for piece, out in enumerate(outs):
            out[...] = lax.dot_general(
                part,
                weights[piece * columns : (piece + 1) * columns],
                (((1,), (1,)), ((), ())),
                preferred_element_type=F32,
            ).astype(BF16)


def weight_kernel(place, tokens, d_both, keep, send):
    core, own_x, own_yh = place[0], place[2], place[3]
    rows = CORE * BLOCK * 2
    for step in range(YH * X // 2):
        both = lax.dot_general(
            tokens[:, step * rows : (step + 1) * rows],
            d_both[...],
            (((0,), (0,)), ((), ())),
            preferred_element_type=F32,
        ).astype(BF16)
        for pair in range(2):
            yh, x = divmod(step * 2 + pair, X)
            ahead = lax.rem(x + X - own_x, X), lax.rem(yh + YH - own_yh, YH)
            low = both[pair * 128 : pair * 128 + 64]
            high = both[pair * 128 + 64 : pair * 128 + 128]
            first = core == 0
            keep[ahead] = jnp.where(first, low, high)
            send[ahead] = jnp.where(first, high, low)


def final_kernel(gm, um, *refs):
    parts, (grad_gate, grad_up) = refs[:-2], refs[-2:]
    width = grad_gate.shape[1]
    total = parts[0][...].astype(F32)
    for part in parts[1:]:
        total = total + part[...].astype(F32)
    grad_gate[...] = total[:, :width] * keep_row(gm, width)
    grad_up[...] = total[:, width:] * keep_row(um, width)


def pair_kernel(first, second, *outs):
    for index, out in enumerate(outs):
        out[...] = (first[index].astype(F32) + second[index].astype(F32)).astype(BF16)


def rows_kernel(*refs):
    parts, outs = refs[:X], refs[X:]
    for index, out in enumerate(outs):
        total = parts[0][index].astype(F32)
        for part in parts[1:]:
            total = total + part[index].astype(F32)
        out[...] = total.astype(BF16)


def add_kernel(first, second, out):
    out[...] = (first[...].astype(F32) + second[...].astype(F32)).astype(BF16)


def total_of(parts):
    total = parts[0].astype(F32)
    for source in range(1, parts.shape[0]):
        total = total + parts[source].astype(F32)
    return total.astype(BF16)


def sum_copies_kernel(parts, out):
    total = total_of(parts)
    for copy in range(out.shape[0]):
        out[copy] = total


def join_kernel(place, *refs):
    mine, other, out = refs[:PIECES], refs[PIECES:-1], refs[-1]
    half = place[1]
    rows, columns = mine[0].shape
    for piece in range(PIECES):
        span = slice(piece * columns, (piece + 1) * columns)
        out[pl.ds(pl.multiple_of(half * rows, rows), rows), span] = mine[piece][...]
        out[pl.ds(pl.multiple_of((1 - half) * rows, rows), rows), span] = other[piece][...]


def shape(dims, dtype=BF16):
    return jax.ShapeDtypeStruct(dims, dtype)


def params():
    return pltpu.CompilerParams(vmem_limit_bytes=40 << 20)


def swap(array, axis):
    return lax.ppermute(array, axis, [(0, 1), (1, 0)])


def shift(array, axis, size, steps):
    return lax.ppermute(array, axis, [(i, (i + steps) % size) for i in range(size)])


def call(kernel, out_shape, *operands, scalars=0, scratch=()):
    many = isinstance(out_shape, list)
    results = pl.pallas_call(
        kernel,
        in_specs=[SM] * scalars + [VM] * (len(operands) - scalars),
        out_specs=[VM] * len(out_shape) if many else VM,
        out_shape=out_shape,
        scratch_shapes=list(scratch),
        compiler_params=params(),
    )(*operands)
    return list(results) if many else results


def compute(tokens, out_grad, gate_weight, up_weight, gate_mask, up_mask):
    width = gate_weight.shape[1]
    count, features = tokens.shape
    half = count // YL
    chunk = half // Z
    columns = features // PIECES
    place = jnp.stack([lax.axis_index(name) for name in ("core", "yl", "x", "yh")])
    copies = call(
        mask_kernel,
        shape((YH, BLOCK, 2 * width)),
        gate_mask,
        up_mask,
        gate_weight,
        up_weight,
        scalars=2,
    )
    rows = lax.all_to_all(copies, "yh", 0, 0, tiled=True)
    mine, other = [rows], []
    for steps in range(1, X):
        mine.append(shift(rows, "x", X, steps))
    for steps in range(X):
        other.append(swap(mine[steps], "core"))
    hidden_t, d_both, *partials = call(
        forward_kernel,
        [shape((width, count), F32), shape((count, 2 * width))]
        + [shape((half, columns))] * (2 * PIECES),
        place,
        tokens,
        out_grad.T,
        *mine,
        *other,
        scalars=1,
        scratch=[pltpu.VMEM((YH * X, CORE, BLOCK, 2 * width), BF16)],
    )
    sends, keeps = partials[:PIECES], partials[PIECES:]
    received = []
    for piece in range(PIECES):
        received.append(swap(sends[piece], "yl"))
    w_keep, w_send = call(
        weight_kernel,
        [shape((X, YH, BLOCK, 2 * width))] * 2,
        place,
        tokens,
        d_both,
        scalars=1,
    )
    w_received = swap(w_send, "core")
    w_parts = call(
        pair_kernel, [shape((YH, BLOCK, 2 * width))] * X, w_keep, w_received
    )
    for steps in range(1, X):
        w_parts[steps] = shift(w_parts[steps], "x", X, steps)
    w_parts = call(rows_kernel, [shape((BLOCK, 2 * width))] * YH, *w_parts)
    for steps in range(1, YH):
        w_parts[steps] = shift(w_parts[steps], "yh", YH, steps)
    grad_gate, grad_up = call(
        final_kernel,
        [shape((BLOCK, width), F32)] * 2,
        gate_mask,
        up_mask,
        *w_parts,
        scalars=2,
    )
    own, others = [], []
    for piece in range(PIECES):
        x_sum = call(add_kernel, shape((half, columns)), keeps[piece], received[piece])
        x_parts = lax.all_to_all(x_sum.reshape(Z, chunk, columns), "z", 0, 0, tiled=True)
        x_copies = call(sum_copies_kernel, shape((Z, chunk, columns)), x_parts)
        x_half = lax.all_to_all(x_copies, "z", 0, 0, tiled=True).reshape(half, columns)
        own.append(x_half)
        others.append(swap(x_half, "yl"))
    grad_tokens = call(
        join_kernel, shape((count, features)), place, *own, *others, scalars=1
    )
    return (hidden_t.T, grad_tokens, grad_gate, grad_up)


def solution(mesh):
    fine = Mesh(
        np.asarray(mesh.devices).reshape(YH, X, CORE, Z, YL), ("yh", "x", "core", "z", "yl")
    )
    dp = ("yh", "x", "core")
    tensor = ("z", "yl")
    both = P(dp, tensor)
    return jax.shard_map(
        compute,
        mesh=fine,
        in_specs=(P(dp, None), both, both, both, both, both),
        out_specs=(both, P(dp, None), both, both),
        check_vma=False,
    )
```

time: 202 us -> 200 us (0.990)
  the two profiles are of different devices: /device:TPU:16 before, /device:TPU:1 now
where the time goes in v2:
time: 200 us; the launch traced here: 198 us
  starting transfers between devices  92.8 us (46%)
  waiting for transfers between devices  54.5 us (27%)
  Pallas kernels  21.9 us (11%)
  blocking collectives  20.2 us (10%)
  local copies, waits for them, and re-layouts  8.1 us (4%)
    ppermute x9, starting transfers between devices, swap(): return lax.ppermute(array, axis, [(0, 1), (1, 0)])  36.1 us
    ppermute x9, starting transfers between devices, shift(): lax.ppermute(array, axis, [(i, (i + steps) % size) for i in range(size)])  31.4 us
    pallas_call x11, Pallas kernels, call(): pl.pallas_call(kernel, in_specs=[SM] * scalars + [VM] * (len(operands) -...  21.9 us
    ppermute x9, waiting for transfers between devices, swap(): return lax.ppermute(array, axis, [(0, 1), (1, 0)])  20.8 us
    ppermute x9, waiting for transfers between devices, shift(): lax.ppermute(array, axis, [(i, (i + steps) % size) for i in range(size)])  20.6 us
    all_to_all x1, blocking collectives, compute(): rows = lax.all_to_all(copies, 'yh', 0, 0, tiled=True)  20.2 us
    all_to_all x2, starting transfers between devices, compute(): lax.all_to_all(x_sum.reshape(Z, chunk, columns), 'z', 0, 0, tiled=True)  15.5 us
    all_to_all x2, waiting for transfers between devices, compute(): lax.all_to_all(x_copies, 'z', 0, 0, tiled=True).reshape(half, columns)  11.6 us
  transfers between devices with their start and end apart: 22, of which 11 were waited for; matrix products, arithmetic and copies ran while one was open for 0% of the time, Pallas kernels for 6%

profile of v2, /device:TPU:1, one launch (start us, length us, event | category | flops | bytes accessed | tf_op | source)
XLA Modules:
  0.0 198.5 jit_solution(14673269412895758614)
XLA Ops:
  0.6 0.8 copy-done.9
  1.5 0.8 copy-done.10
  2.3 0.7 copy-done.11
  3.0 0.7 copy-done.13
  3.6 0.6 shard_map.93
  4.3 20.2 %all_to_all.25.rest_0_ = bf16[4,64,896]{2,1,0:T(8,128)(2,1)S(1)} all-to-all(bf16[4,64,896]{2,1,0:T(8,128)(2,1)S(1)} %shard_map.93), channel_id=1, replica_groups=mesh['yh'=4,'x'=4,'core'=2,'z'=8,'yl'=2] {'yh'}, dimensions={0} | all-to-all | bytes 917504 | tf_op jit(solution)/shard_map/all_to_all | solution.py:187
  24.5 5.2 %collective-permute-start.2 = (bf16[4,64,896]{2,1,0:T(8,128)(2,1)S(1)}, bf16[4,64,896]{2,1,0:T(8,128)(2,1)S(1)}, u32[]{:S(2)}, u32[]{:S(2)}) collective-permute-start(bf16[4,64,896]{2,1,0:T(8,128)(2,1)S(1)} %all_to_all.25.rest_0_), channel_id=1, source_target_pairs={{0,96},{32,0},{64,32},{96,64},{1,97},{33,1},{65,33},{97,65},{2,98}... | collective-permute-start | bytes 1376264 | tf_op jit(solution)/shard_map/ppermute | solution.py:155
  29.7 2.4 %collective-permute-start.1 = (bf16[4,64,896]{2,1,0:T(8,128)(2,1)S(1)}, bf16[4,64,896]{2,1,0:T(8,128)(2,1)S(1)}, u32[]{:S(2)}, u32[]{:S(2)}) collective-permute-start(bf16[4,64,896]{2,1,0:T(8,128)(2,1)S(1)} %all_to_all.25.rest_0_), channel_id=1, source_target_pairs={{0,64},{32,96},{64,0},{96,32},{1,65},{33,97},{65,1},{97,33},{2,66}... | collective-permute-start | bytes 1376264 | tf_op jit(solution)/shard_map/ppermute | solution.py:155
  32.1 2.5 %collective-permute-start = (bf16[4,64,896]{2,1,0:T(8,128)(2,1)S(1)}, bf16[4,64,896]{2,1,0:T(8,128)(2,1)S(1)}, u32[]{:S(2)}, u32[]{:S(2)}) collective-permute-start(bf16[4,64,896]{2,1,0:T(8,128)(2,1)S(1)} %all_to_all.25.rest_0_), channel_id=1, source_target_pairs={{0,32},{32,64},{64,96},{96,0},{1,33},{33,65},{65,97},{97,1},{2,34}... | collective-permute-start | bytes 1376264 | tf_op jit(solution)/shard_map/ppermute | solution.py:155
  34.6 5.2 %collective-permute-start.3 = (bf16[4,64,896]{2,1,0:T(8,128)(2,1)S(1)}, bf16[4,64,896]{2,1,0:T(8,128)(2,1)S(1)}, u32[]{:S(2)}, u32[]{:S(2)}) collective-permute-start(bf16[4,64,896]{2,1,0:T(8,128)(2,1)S(1)} %all_to_all.25.rest_0_), channel_id=1, source_target_pairs={{0,16},{16,0},{1,17},{17,1},{2,18},{18,2},{3,19},{19,3},{4,20},{20... | collective-permute-start | bytes 1376264 | tf_op jit(solution)/shard_map/ppermute | solution.py:151
  39.9 12.2 %collective-permute-start.6 = (bf16[4,64,896]{2,1,0:T(8,128)(2,1)S(1)}, bf16[4,64,896]{2,1,0:T(8,128)(2,1)S(1)}, u32[]{:S(2)}, u32[]{:S(2)}) collective-permute-start(bf16[4,64,896]{2,1,0:T(8,128)(2,1)S(1)} %collective-permute-done.2.rest_3_), channel_id=1, source_target_pairs={{0,16},{16,0},{1,17},{17,1},{2,18},{18,2},{3,19},{19,3},{4,20},{20... | collective-permute-start | bytes 1376264 | tf_op jit(solution)/shard_map/ppermute | solution.py:151
  52.1 1.9 collective-permute-start.5
  54.1 1.3 collective-permute-done.rest_1_
  55.4 2.4 %collective-permute-start.4 = (bf16[4,64,896]{2,1,0:T(8,128)(2,1)S(1)}, bf16[4,64,896]{2,1,0:T(8,128)(2,1)}, u32[]{:S(2)}, u32[]{:S(2)}) collective-permute-start(bf16[4,64,896]{2,1,0:T(8,128)(2,1)S(1)} %collective-permute-done.rest_1_), channel_id=1, source_target_pairs={{0,16},{16,0},{1,17},{17,1},{2,18},{18,2},{3,19},{19,3},{4,20},{20... | collective-permute-start | bytes 1376264 | tf_op jit(solution)/shard_map/ppermute | solution.py:151
  57.8 0.1 pad_add_fusion.place
  57.8 0.0 collective-permute-done.6.rest_7_
  57.8 0.0 collective-permute-done.5.rest_6_
  57.9 1.5 collective-permute-done.4.rest_5_
  59.3 1.4 copy-done
  60.7 1.0 copy-done.8
  61.7 6.8 %shard_map.94 = (f32[448,384]{1,0:T(8,128)}, bf16[384,896]{1,0:T(8,128)(2,1)S(1)}, bf16[192,1024]{1,0:T(8,128)(2,1)S(1)}, bf16[192,1024]{1,0:T(8,128)(2,1)S(1)},...) custom-call(s32[4]{0:T(128)S(1)} %pad_add_fusion.place, bf16[384,2048]{1,0:T(8,128)(2,1)S(1)} %copy-done, ...), custom_call_target="tpu_custom_call" | custom-call | tf_op jit(solution)/shard_map/pallas_call | solution.py:160
  68.4 0.8 copy-done.4
  69.3 0.8 copy-done.6
  70.1 2.0 %collective-permute-start.7 = (bf16[192,1024]{1,0:T(8,128)(2,1)S(1)}, bf16[192,1024]{1,0:T(8,128)(2,1)S(1)}, u32[]{:S(2)}, u32[]{:S(2)}) collective-permute-start(bf16[192,1024]{1,0:T(8,128)(2,1)S(1)} %get-tuple-element.24), channel_id=1, source_target_pairs={{0,1},{1,0},{2,3},{3,2},{4,5},{5,4},{6,7},{7,6},{8,9},{9,8},{10,11... | collective-permute-start | bytes 1179656 | tf_op jit(solution)/shard_map/ppermute | solution.py:151
  72.1 10.3 %collective-permute-done.7.second = bf16[192,1024]{1,0:T(8,128)(2,1)S(1)} collective-permute-done((bf16[192,1024]{1,0:T(8,128)(2,1)S(1)}, bf16[192,1024]{1,0:T(8,128)(2,1)S(1)}, u32[]{:S(2)}, u32[]{:S(2)}) %collective-permute-start.7) | collective-permute-done | bytes 393248 | tf_op jit(solution)/shard_map/ppermute | solution.py:151
  82.4 0.8 shard_map.95
  83.2 10.0 %all-to-all-start.1 = ((bf16[8,24,1024]{2,1,0:T(8,128)(2,1)}), bf16[8,24,1024]{2,1,0:T(8,128)(2,1)S(1)}, u32[]{:S(2)}, u32[]{:S(2)}) async-start(bf16[8,24,1024]{2,1,0:T(8,128)(2,1)} %bitcast.6), calls=%async_computation.1 | async-start | bytes 786432 | tf_op jit(solution)/shard_map/all_to_all | solution.py:237
  93.3 2.2 %collective-permute-start.8 = (bf16[192,1024]{1,0:T(8,128)(2,1)}, bf16[192,1024]{1,0:T(8,128)(2,1)S(1)}, u32[]{:S(2)}, u32[]{:S(2)}) collective-permute-start(bf16[192,1024]{1,0:T(8,128)(2,1)} %copy-done.15), channel_id=1, source_target_pairs={{0,1},{1,0},{2,3},{3,2},{4,5},{5,4},{6,7},{7,6},{8,9},{9,8},{10,11... | collective-permute-start | bytes 1179656 | tf_op jit(solution)/shard_map/ppermute | solution.py:151
  95.4 9.1 %collective-permute-done.8.second = bf16[192,1024]{1,0:T(8,128)(2,1)S(1)} collective-permute-done((bf16[192,1024]{1,0:T(8,128)(2,1)}, bf16[192,1024]{1,0:T(8,128)(2,1)S(1)}, u32[]{:S(2)}, u32[]{:S(2)}) %collective-permute-start.8) | collective-permute-done | bytes 393248 | tf_op jit(solution)/shard_map/ppermute | solution.py:151
  104.5 0.9 shard_map.97
  105.4 0.9 all-to-all-done.1.parts
  106.3 5.5 %all-to-all-start.3 = ((bf16[8,24,1024]{2,1,0:T(8,128)(2,1)}), bf16[8,24,1024]{2,1,0:T(8,128)(2,1)}, u32[]{:S(2)}, u32[]{:S(2)}) async-start(bf16[8,24,1024]{2,1,0:T(8,128)(2,1)} %bitcast.8), calls=%async_computation.3 | async-start | bytes 786432 | tf_op jit(solution)/shard_map/all_to_all | solution.py:237
  111.8 0.0 copy-start.5
  111.8 1.1 copy-done.5
  112.9 4.1 %shard_map.100 = (bf16[4,4,64,896]{3,2,1,0:T(8,128)(2,1)S(1)}, bf16[4,4,64,896]{3,2,1,0:T(8,128)(2,1)}) custom-call(s32[4]{0:T(128)S(1)} %pad_add_fusion.place, bf16[384,2048]{1,0:T(8,128)(2,1)S(1)} %copy-done.1, bf16[384,896]{1,0:T(8,128)(2,1)S(1)} %copy-done.5), custom_call_target="tpu_custom_call" | custom-call | tf_op jit(solution)/shard_map/pallas_call | solution.py:160
  116.9 4.8 %collective-permute-start.11 = (bf16[4,4,64,896]{3,2,1,0:T(8,128)(2,1)}, bf16[4,4,64,896]{3,2,1,0:T(8,128)(2,1)}, u32[]{:S(2)}, u32[]{:S(2)}) collective-permute-start(bf16[4,4,64,896]{3,2,1,0:T(8,128)(2,1)} %get-tuple-element.29), channel_id=1, source_target_pairs={{0,16},{16,0},{1,17},{17,1},{2,18},{18,2},{3,19},{19,3},{4,20},{20... | collective-permute-start | bytes 5505032 | tf_op jit(solution)/shard_map/ppermute | solution.py:151
  121.8 0.8 shard_map.96
  122.6 0.6 all-to-all-done.3.parts
  123.2 6.3 %all-to-all-start.2 = ((bf16[8,24,1024]{2,1,0:T(8,128)(2,1)}), bf16[8,24,1024]{2,1,0:T(8,128)(2,1)S(1)}, u32[]{:S(2)}, u32[]{:S(2)}) async-start(bf16[8,24,1024]{2,1,0:T(8,128)(2,1)} %shard_map.96), calls=%async_computation.2 | async-start | bytes 786432 | tf_op jit(solution)/shard_map/all_to_all | solution.py:239
  129.5 1.8 shard_map.98
  131.3 11.6 %all-to-all-done.2 = bf16[8,24,1024]{2,1,0:T(8,128)(2,1)S(1)} async-done(((bf16[8,24,1024]{2,1,0:T(8,128)(2,1)}), bf16[8,24,1024]{2,1,0:T(8,128)(2,1)S(1)}, u32[]{:S(2)}, u32[]{:S(2)}) %all-to-all-start.2) | async-done | bytes 393248 | tf_op jit(solution)/shard_map/all_to_all | solution.py:239
  142.9 3.5 %all-to-all-start.4 = ((bf16[8,24,1024]{2,1,0:T(8,128)(2,1)}), bf16[8,24,1024]{2,1,0:T(8,128)(2,1)S(1)}, u32[]{:S(2)}, u32[]{:S(2)}) async-start(bf16[8,24,1024]{2,1,0:T(8,128)(2,1)} %shard_map.98), calls=%async_computation.4 | async-start | bytes 786432 | tf_op jit(solution)/shard_map/all_to_all | solution.py:239
  146.4 0.0 collective-permute-done.11.second
  146.4 2.7 %shard_map.101 = (bf16[4,64,896]{2,1,0:T(8,128)(2,1)S(1)}, bf16[4,64,896]{2,1,0:T(8,128)(2,1)}, bf16[4,64,896]{2,1,0:T(8,128)(2,1)}, bf16[4,64,896]{2,1,0:T(8,128)(2,1)}) custom-call(bf16[4,4,64,896]{3,2,1,0:T(8,128)(2,1)S(1)} %get-tuple-element.28.first, bf16[4,4,64,896]{3,2,1,0:T(8,128)(2,1)} %collective-permute-done.11.second), custom_call_target="tpu_custom_call" | custom-call | tf_op jit(solution)/shard_map/pallas_call | solution.py:160
  149.1 1.9 collective-permute-start.12
  151.0 5.2 %collective-permute-start.13 = (bf16[4,64,896]{2,1,0:T(8,128)(2,1)}, bf16[4,64,896]{2,1,0:T(8,128)(2,1)S(1)}, u32[]{:S(2)}, u32[]{:S(2)}) collective-permute-start(bf16[4,64,896]{2,1,0:T(8,128)(2,1)} %get-tuple-element.32), channel_id=1, source_target_pairs={{0,64},{32,96},{64,0},{96,32},{1,65},{33,97},{65,1},{97,33},{2,66}... | collective-permute-start | bytes 1376264 | tf_op jit(solution)/shard_map/ppermute | solution.py:155
  156.2 1.9 collective-permute-start.14
  158.1 1.9 collective-permute-start.9
  160.1 3.4 %collective-permute-start.10 = (bf16[192,1024]{1,0:T(8,128)(2,1)S(1)}, bf16[192,1024]{1,0:T(8,128)(2,1)S(1)}, u32[]{:S(2)}, u32[]{:S(2)}) collective-permute-start(bf16[192,1024]{1,0:T(8,128)(2,1)S(1)} %bitcast.12), channel_id=1, source_target_pairs={{0,1},{1,0},{2,3},{3,2},{4,5},{5,4},{6,7},{7,6},{8,9},{9,8},{10,11... | collective-permute-start | bytes 1179656 | tf_op jit(solution)/shard_map/ppermute | solution.py:151
  163.4 0.0 collective-permute-done.12.refs_1_
  163.4 9.2 %collective-permute-done.13.refs_2_ = bf16[4,64,896]{2,1,0:T(8,128)(2,1)S(1)} collective-permute-done((bf16[4,64,896]{2,1,0:T(8,128)(2,1)}, bf16[4,64,896]{2,1,0:T(8,128)(2,1)S(1)}, u32[]{:S(2)}, u32[]{:S(2)}) %collective-permute-start.13) | collective-permute-done | bytes 458784 | tf_op jit(solution)/shard_map/ppermute | solution.py:155
  172.6 3.6 %collective-permute-done.14.refs_3_ = bf16[4,64,896]{2,1,0:T(8,128)(2,1)S(1)} collective-permute-done((bf16[4,64,896]{2,1,0:T(8,128)(2,1)}, bf16[4,64,896]{2,1,0:T(8,128)(2,1)S(1)}, u32[]{:S(2)}, u32[]{:S(2)}) %collective-permute-start.14) | collective-permute-done | bytes 458784 | tf_op jit(solution)/shard_map/ppermute | solution.py:155
  176.2 0.2 shard_map.102
  176.5 0.0 copy-start.12
  176.5 0.0 copy-start.14
  176.5 4.8 %collective-permute-start.15 = (bf16[64,896]{1,0:T(8,128)(2,1)S(1)}, bf16[64,896]{1,0:T(8,128)(2,1)S(1)}, u32[]{:S(2)}, u32[]{:S(2)}) collective-permute-start(bf16[64,896]{1,0:T(8,128)(2,1)S(1)} %get-tuple-element.35), channel_id=1, source_target_pairs={{0,128},{128,256},{256,384},{384,0},{1,129},{129,257},{257,385},{3... | collective-permute-start | bytes 344072 | tf_op jit(solution)/shard_map/ppermute | solution.py:155
  181.3 2.5 %collective-permute-start.16 = (bf16[64,896]{1,0:T(8,128)(2,1)S(1)}, bf16[64,896]{1,0:T(8,128)(2,1)S(1)}, u32[]{:S(2)}, u32[]{:S(2)}) collective-permute-start(bf16[64,896]{1,0:T(8,128)(2,1)S(1)} %get-tuple-element.36), channel_id=1, source_target_pairs={{0,256},{128,384},{256,0},{384,128},{1,257},{129,385},{257,1},{385... | collective-permute-start | bytes 344072 | tf_op jit(solution)/shard_map/ppermute | solution.py:155
  183.8 4.9 %collective-permute-start.17 = (bf16[64,896]{1,0:T(8,128)(2,1)S(1)}, bf16[64,896]{1,0:T(8,128)(2,1)S(1)}, u32[]{:S(2)}, u32[]{:S(2)}) collective-permute-start(bf16[64,896]{1,0:T(8,128)(2,1)S(1)} %get-tuple-element.37), channel_id=1, source_target_pairs={{0,384},{128,0},{256,128},{384,256},{1,385},{129,1},{257,129},{385... | collective-permute-start | bytes 344072 | tf_op jit(solution)/shard_map/ppermute | solution.py:155
  188.7 0.0 collective-permute-done.9.refs_2_
  188.7 0.0 collective-permute-done.10.refs_3_
  188.7 1.8 shard_map.99
  190.5 0.5 collective-permute-done.16.refs_2_
  191.1 6.0 %collective-permute-done.17.refs_3_ = bf16[64,896]{1,0:T(8,128)(2,1)S(1)} collective-permute-done((bf16[64,896]{1,0:T(8,128)(2,1)S(1)}, bf16[64,896]{1,0:T(8,128)(2,1)S(1)}, u32[]{:S(2)}, u32[]{:S(2)}) %collective-permute-start.17) | collective-permute-done | bytes 114720 | tf_op jit(solution)/shard_map/ppermute | solution.py:155
  197.1 1.4 shard_map.103
  (25 shorter events, 0.0 us)
Async XLA Ops:
  0.6 0.8 copy-start.9
  1.5 0.8 copy-start.10
  2.3 0.7 copy-start.11
  3.0 0.7 copy-start.13
  24.5 15.4 %collective-permute-start.2 = (bf16[4,64,896]{2,1,0:T(8,128)(2,1)S(1)}, bf16[4,64,896]{2,1,0:T(8,128)(2,1)S(1)}, u32[]{:S(2)}, u32[]{:S(2)}) collective-permute-start(bf16[4,64,896]{2,1,0:T(8,128)(2,1)S(1)} %all_to_all.25.rest_0_), channel_id=1, source_target_pairs={{0,96},{32,0},{64,32},{96,64},{1,97},{33,1},{65,33},{97,65},{2,98}... | collective-permute-start | bytes 1376264 | tf_op jit(solution)/shard_map/ppermute | solution.py:155
  29.7 22.4 %collective-permute-start.1 = (bf16[4,64,896]{2,1,0:T(8,128)(2,1)S(1)}, bf16[4,64,896]{2,1,0:T(8,128)(2,1)S(1)}, u32[]{:S(2)}, u32[]{:S(2)}) collective-permute-start(bf16[4,64,896]{2,1,0:T(8,128)(2,1)S(1)} %all_to_all.25.rest_0_), channel_id=1, source_target_pairs={{0,64},{32,96},{64,0},{96,32},{1,65},{33,97},{65,1},{97,33},{2,66}... | collective-permute-start | bytes 1376264 | tf_op jit(solution)/shard_map/ppermute | solution.py:155
  32.1 23.2 %collective-permute-start = (bf16[4,64,896]{2,1,0:T(8,128)(2,1)S(1)}, bf16[4,64,896]{2,1,0:T(8,128)(2,1)S(1)}, u32[]{:S(2)}, u32[]{:S(2)}) collective-permute-start(bf16[4,64,896]{2,1,0:T(8,128)(2,1)S(1)} %all_to_all.25.rest_0_), channel_id=1, source_target_pairs={{0,32},{32,64},{64,96},{96,0},{1,33},{33,65},{65,97},{97,1},{2,34}... | collective-permute-start | bytes 1376264 | tf_op jit(solution)/shard_map/ppermute | solution.py:155
  34.6 23.2 %collective-permute-start.3 = (bf16[4,64,896]{2,1,0:T(8,128)(2,1)S(1)}, bf16[4,64,896]{2,1,0:T(8,128)(2,1)S(1)}, u32[]{:S(2)}, u32[]{:S(2)}) collective-permute-start(bf16[4,64,896]{2,1,0:T(8,128)(2,1)S(1)} %all_to_all.25.rest_0_), channel_id=1, source_target_pairs={{0,16},{16,0},{1,17},{17,1},{2,18},{18,2},{3,19},{19,3},{4,20},{20... | collective-permute-start | bytes 1376264 | tf_op jit(solution)/shard_map/ppermute | solution.py:151
  39.9 17.9 %collective-permute-start.6 = (bf16[4,64,896]{2,1,0:T(8,128)(2,1)S(1)}, bf16[4,64,896]{2,1,0:T(8,128)(2,1)S(1)}, u32[]{:S(2)}, u32[]{:S(2)}) collective-permute-start(bf16[4,64,896]{2,1,0:T(8,128)(2,1)S(1)} %collective-permute-done.2.rest_3_), channel_id=1, source_target_pairs={{0,16},{16,0},{1,17},{17,1},{2,18},{18,2},{3,19},{19,3},{4,20},{20... | collective-permute-start | bytes 1376264 | tf_op jit(solution)/shard_map/ppermute | solution.py:151
  52.1 5.7 %collective-permute-start.5 = (bf16[4,64,896]{2,1,0:T(8,128)(2,1)S(1)}, bf16[4,64,896]{2,1,0:T(8,128)(2,1)S(1)}, u32[]{:S(2)}, u32[]{:S(2)}) collective-permute-start(bf16[4,64,896]{2,1,0:T(8,128)(2,1)S(1)} %collective-permute-done.1.rest_2_), channel_id=1, source_target_pairs={{0,16},{16,0},{1,17},{17,1},{2,18},{18,2},{3,19},{19,3},{4,20},{20... | collective-permute-start | bytes 1376264 | tf_op jit(solution)/shard_map/ppermute | solution.py:151
  55.4 4.0 %collective-permute-start.4 = (bf16[4,64,896]{2,1,0:T(8,128)(2,1)S(1)}, bf16[4,64,896]{2,1,0:T(8,128)(2,1)}, u32[]{:S(2)}, u32[]{:S(2)}) collective-permute-start(bf16[4,64,896]{2,1,0:T(8,128)(2,1)S(1)} %collective-permute-done.rest_1_), channel_id=1, source_target_pairs={{0,16},{16,0},{1,17},{17,1},{2,18},{18,2},{3,19},{19,3},{4,20},{20... | collective-permute-start | bytes 1376264 | tf_op jit(solution)/shard_map/ppermute | solution.py:151
  59.3 1.4 copy-start
  60.7 1.0 copy-start.8
  68.4 0.8 copy-start.4
  69.3 0.8 copy-start.6
  70.1 13.2 %copy-start.15 = (bf16[192,1024]{1,0:T(8,128)(2,1)}, bf16[192,1024]{1,0:T(8,128)(2,1)S(1)}, u32[]{:S(2)}) copy-start(bf16[192,1024]{1,0:T(8,128)(2,1)S(1)} %get-tuple-element.26) | copy-start | bytes 1179652
  70.1 34.4 %copy-start.7 = (bf16[192,1024]{1,0:T(8,128)(2,1)S(1)}, bf16[192,1024]{1,0:T(8,128)(2,1)}, u32[]{:S(2)}) copy-start(bf16[192,1024]{1,0:T(8,128)(2,1)} %copy-done.6) | copy-start | bytes 1179652
  70.1 12.3 %collective-permute-start.7 = (bf16[192,1024]{1,0:T(8,128)(2,1)S(1)}, bf16[192,1024]{1,0:T(8,128)(2,1)S(1)}, u32[]{:S(2)}, u32[]{:S(2)}) collective-permute-start(bf16[192,1024]{1,0:T(8,128)(2,1)S(1)} %get-tuple-element.24), channel_id=1, source_target_pairs={{0,1},{1,0},{2,3},{3,2},{4,5},{5,4},{6,7},{7,6},{8,9},{9,8},{10,11... | collective-permute-start | bytes 1179656 | tf_op jit(solution)/shard_map/ppermute | solution.py:151
  82.4 29.4 %copy-start.1 = (bf16[384,2048]{1,0:T(8,128)(2,1)S(1)}, bf16[384,2048]{1,0:T(8,128)(2,1)}, u32[]{:S(2)}) copy-start(bf16[384,2048]{1,0:T(8,128)(2,1)} %tokens.3) | copy-start | bytes 4718596
  83.2 23.1 %all-to-all-start.1 = ((bf16[8,24,1024]{2,1,0:T(8,128)(2,1)}), bf16[8,24,1024]{2,1,0:T(8,128)(2,1)S(1)}, u32[]{:S(2)}, u32[]{:S(2)}) async-start(bf16[8,24,1024]{2,1,0:T(8,128)(2,1)} %bitcast.6), calls=%async_computation.1 | async-start | bytes 786432 | tf_op jit(solution)/shard_map/all_to_all | solution.py:237
  93.3 11.3 %collective-permute-start.8 = (bf16[192,1024]{1,0:T(8,128)(2,1)}, bf16[192,1024]{1,0:T(8,128)(2,1)S(1)}, u32[]{:S(2)}, u32[]{:S(2)}) collective-permute-start(bf16[192,1024]{1,0:T(8,128)(2,1)} %copy-done.15), channel_id=1, source_target_pairs={{0,1},{1,0},{2,3},{3,2},{4,5},{5,4},{6,7},{7,6},{8,9},{9,8},{10,11... | collective-permute-start | bytes 1179656 | tf_op jit(solution)/shard_map/ppermute | solution.py:151
  106.3 5.5 %copy-start.2 = (bf16[8,24,1024]{2,1,0:T(8,128)(2,1)}, bf16[8,24,1024]{2,1,0:T(8,128)(2,1)S(1)}, u32[]{:S(2)}) copy-start(bf16[8,24,1024]{2,1,0:T(8,128)(2,1)S(1)} %all-to-all-done.1.parts) | copy-start | bytes 1179652
  106.3 16.9 %all-to-all-start.3 = ((bf16[8,24,1024]{2,1,0:T(8,128)(2,1)}), bf16[8,24,1024]{2,1,0:T(8,128)(2,1)}, u32[]{:S(2)}, u32[]{:S(2)}) async-start(bf16[8,24,1024]{2,1,0:T(8,128)(2,1)} %bitcast.8), calls=%async_computation.3 | async-start | bytes 786432 | tf_op jit(solution)/shard_map/all_to_all | solution.py:237
  111.8 1.1 copy-start.5
  112.9 8.9 %copy-start.3 = (bf16[8,24,1024]{2,1,0:T(8,128)(2,1)S(1)}, bf16[8,24,1024]{2,1,0:T(8,128)(2,1)}, u32[]{:S(2)}) copy-start(bf16[8,24,1024]{2,1,0:T(8,128)(2,1)} %copy-done.2) | copy-start | bytes 1179652
  116.9 29.5 %collective-permute-start.11 = (bf16[4,4,64,896]{3,2,1,0:T(8,128)(2,1)}, bf16[4,4,64,896]{3,2,1,0:T(8,128)(2,1)}, u32[]{:S(2)}, u32[]{:S(2)}) collective-permute-start(bf16[4,4,64,896]{3,2,1,0:T(8,128)(2,1)} %get-tuple-element.29), channel_id=1, source_target_pairs={{0,16},{16,0},{1,17},{17,1},{2,18},{18,2},{3,19},{19,3},{4,20},{20... | collective-permute-start | bytes 5505032 | tf_op jit(solution)/shard_map/ppermute | solution.py:151
  123.2 19.7 %all-to-all-start.2 = ((bf16[8,24,1024]{2,1,0:T(8,128)(2,1)}), bf16[8,24,1024]{2,1,0:T(8,128)(2,1)S(1)}, u32[]{:S(2)}, u32[]{:S(2)}) async-start(bf16[8,24,1024]{2,1,0:T(8,128)(2,1)} %shard_map.96), calls=%async_computation.2 | async-start | bytes 786432 | tf_op jit(solution)/shard_map/all_to_all | solution.py:239
  142.9 17.1 %all-to-all-start.4 = ((bf16[8,24,1024]{2,1,0:T(8,128)(2,1)}), bf16[8,24,1024]{2,1,0:T(8,128)(2,1)S(1)}, u32[]{:S(2)}, u32[]{:S(2)}) async-start(bf16[8,24,1024]{2,1,0:T(8,128)(2,1)} %shard_map.98), calls=%async_computation.4 | async-start | bytes 786432 | tf_op jit(solution)/shard_map/all_to_all | solution.py:239
  149.1 14.4 %collective-permute-start.12 = (bf16[4,64,896]{2,1,0:T(8,128)(2,1)}, bf16[4,64,896]{2,1,0:T(8,128)(2,1)S(1)}, u32[]{:S(2)}, u32[]{:S(2)}) collective-permute-start(bf16[4,64,896]{2,1,0:T(8,128)(2,1)} %get-tuple-element.31), channel_id=1, source_target_pairs={{0,32},{32,64},{64,96},{96,0},{1,33},{33,65},{65,97},{97,1},{2,34}... | collective-permute-start | bytes 1376264 | tf_op jit(solution)/shard_map/ppermute | solution.py:155
  151.0 21.6 %collective-permute-start.13 = (bf16[4,64,896]{2,1,0:T(8,128)(2,1)}, bf16[4,64,896]{2,1,0:T(8,128)(2,1)S(1)}, u32[]{:S(2)}, u32[]{:S(2)}) collective-permute-start(bf16[4,64,896]{2,1,0:T(8,128)(2,1)} %get-tuple-element.32), channel_id=1, source_target_pairs={{0,64},{32,96},{64,0},{96,32},{1,65},{33,97},{65,1},{97,33},{2,66}... | collective-permute-start | bytes 1376264 | tf_op jit(solution)/shard_map/ppermute | solution.py:155
  156.2 20.0 %collective-permute-start.14 = (bf16[4,64,896]{2,1,0:T(8,128)(2,1)}, bf16[4,64,896]{2,1,0:T(8,128)(2,1)S(1)}, u32[]{:S(2)}, u32[]{:S(2)}) collective-permute-start(bf16[4,64,896]{2,1,0:T(8,128)(2,1)} %get-tuple-element.33), channel_id=1, source_target_pairs={{0,96},{32,0},{64,32},{96,64},{1,97},{33,1},{65,33},{97,65},{2,98}... | collective-permute-start | bytes 1376264 | tf_op jit(solution)/shard_map/ppermute | solution.py:155
  158.1 30.6 %collective-permute-start.9 = (bf16[192,1024]{1,0:T(8,128)(2,1)S(1)}, bf16[192,1024]{1,0:T(8,128)(2,1)S(1)}, u32[]{:S(2)}, u32[]{:S(2)}) collective-permute-start(bf16[192,1024]{1,0:T(8,128)(2,1)S(1)} %bitcast.10), channel_id=1, source_target_pairs={{0,1},{1,0},{2,3},{3,2},{4,5},{5,4},{6,7},{7,6},{8,9},{9,8},{10,11... | collective-permute-start | bytes 1179656 | tf_op jit(solution)/shard_map/ppermute | solution.py:151
  160.1 28.7 %collective-permute-start.10 = (bf16[192,1024]{1,0:T(8,128)(2,1)S(1)}, bf16[192,1024]{1,0:T(8,128)(2,1)S(1)}, u32[]{:S(2)}, u32[]{:S(2)}) collective-permute-start(bf16[192,1024]{1,0:T(8,128)(2,1)S(1)} %bitcast.12), channel_id=1, source_target_pairs={{0,1},{1,0},{2,3},{3,2},{4,5},{5,4},{6,7},{7,6},{8,9},{9,8},{10,11... | collective-permute-start | bytes 1179656 | tf_op jit(solution)/shard_map/ppermute | solution.py:151
  176.5 20.6 %copy-start.12 = (s32[1,7]{1,0:T(1,128)S(1)}, s32[1,7]{1,0:T(1,128)}, u32[]{:S(2)}) copy-start(s32[1,7]{1,0:T(1,128)} %gm.3) | copy-start | bytes 88
  176.5 20.6 %copy-start.14 = (s32[1,7]{1,0:T(1,128)S(1)}, s32[1,7]{1,0:T(1,128)}, u32[]{:S(2)}) copy-start(s32[1,7]{1,0:T(1,128)} %um.3) | copy-start | bytes 88
  176.5 14.1 %collective-permute-start.15 = (bf16[64,896]{1,0:T(8,128)(2,1)S(1)}, bf16[64,896]{1,0:T(8,128)(2,1)S(1)}, u32[]{:S(2)}, u32[]{:S(2)}) collective-permute-start(bf16[64,896]{1,0:T(8,128)(2,1)S(1)} %get-tuple-element.35), channel_id=1, source_target_pairs={{0,128},{128,256},{256,384},{384,0},{1,129},{129,257},{257,385},{3... | collective-permute-start | bytes 344072 | tf_op jit(solution)/shard_map/ppermute | solution.py:155
  181.3 9.8 %collective-permute-start.16 = (bf16[64,896]{1,0:T(8,128)(2,1)S(1)}, bf16[64,896]{1,0:T(8,128)(2,1)S(1)}, u32[]{:S(2)}, u32[]{:S(2)}) collective-permute-start(bf16[64,896]{1,0:T(8,128)(2,1)S(1)} %get-tuple-element.36), channel_id=1, source_target_pairs={{0,256},{128,384},{256,0},{384,128},{1,257},{129,385},{257,1},{385... | collective-permute-start | bytes 344072 | tf_op jit(solution)/shard_map/ppermute | solution.py:155
  183.8 13.3 %collective-permute-start.17 = (bf16[64,896]{1,0:T(8,128)(2,1)S(1)}, bf16[64,896]{1,0:T(8,128)(2,1)S(1)}, u32[]{:S(2)}, u32[]{:S(2)}) collective-permute-start(bf16[64,896]{1,0:T(8,128)(2,1)S(1)} %get-tuple-element.37), channel_id=1, source_target_pairs={{0,384},{128,0},{256,128},{384,256},{1,385},{129,1},{257,129},{385... | collective-permute-start | bytes 344072 | tf_op jit(solution)/shard_map/ppermute | solution.py:155

commit v3 on v2

--- a/solution.py
+++ b/solution.py
@@ -12,8 +12,9 @@
 BF16 = jnp.bfloat16
 F32 = jnp.float32
 YH, X, CORE, Z, YL = 4, 4, 2, 8, 2
-PIECES = 2
+PIECES = 1
 VM = pl.BlockSpec(memory_space=pltpu.VMEM)
+HB = pl.BlockSpec(memory_space=pltpu.HBM)
 SM = pl.BlockSpec(memory_space=pltpu.SMEM)
 
 
@@ -25,7 +26,17 @@
     return keep
 
 
-def mask_kernel(gm, um, gw, uw, out):
+def mask_kernel(gm_hbm, um_hbm, gw_hbm, uw_hbm, out, gm, um, gw, uw, sems):
+    moves = [
+        pltpu.make_async_copy(source, target, sems.at[index])
+        for index, (source, target) in enumerate(
+            ((gw_hbm, gw), (uw_hbm, uw), (gm_hbm, gm), (um_hbm, um))
+        )
+    ]
+    for move in moves:
+        move.start()
+    for move in moves:
+        move.wait()
     width = gw.shape[1]
     gate = gw[...].astype(F32) * keep_row(gm, width)
     up = uw[...].astype(F32) * keep_row(um, width)
@@ -34,12 +45,17 @@
         out[copy] = both
 
 
-def forward_kernel(place, tokens, ogt, *rest):
+def prepare_kernel(tokens, ogt, tokens_out, grad_out):
+    tokens_out[...] = tokens[...]
+    grad_out[...] = ogt[...].astype(F32).T
+
+
+def forward_kernel(place, tokens, grad_ref, *rest):
     mine, other = rest[:X], rest[X : 2 * X]
     hidden_t, d_both, *rest = rest[2 * X :]
     sends, keeps, w = rest[:PIECES], rest[PIECES:-1], rest[-1]
     core, half, own_x = place[0], place[1], place[2]
-    width = ogt.shape[0]
+    width = grad_ref.shape[1]
     for yh in range(YH):
         for back in range(X):
             x = lax.rem(own_x + (X - back), X)
@@ -52,7 +68,7 @@
     sigmoid = jax.nn.sigmoid(gate)
     activation = gate * sigmoid
     hidden_t[...] = (activation * up).T
-    grad = ogt[...].astype(F32).T
+    grad = grad_ref[...]
     d_gate = grad * up * sigmoid * (1.0 + gate * (1.0 - sigmoid))
     d_up = grad * activation
     d_both[...] = jnp.concatenate([d_gate, d_up], axis=1).astype(BF16)
@@ -175,28 +191,35 @@
     chunk = half // Z
     columns = features // PIECES
     place = jnp.stack([lax.axis_index(name) for name in ("core", "yl", "x", "yh")])
-    copies = call(
+    copies = pl.pallas_call(
         mask_kernel,
-        shape((YH, BLOCK, 2 * width)),
-        gate_mask,
-        up_mask,
-        gate_weight,
-        up_weight,
-        scalars=2,
-    )
+        in_specs=[HB] * 4,
+        out_specs=VM,
+        out_shape=shape((YH, BLOCK, 2 * width)),
+        scratch_shapes=[
+            pltpu.SMEM(gate_mask.shape, jnp.int32),
+            pltpu.SMEM(up_mask.shape, jnp.int32),
+            pltpu.VMEM(gate_weight.shape, BF16),
+            pltpu.VMEM(up_weight.shape, BF16),
+            pltpu.SemaphoreType.DMA((4,)),
+        ],
+    )(gate_mask, up_mask, gate_weight, up_weight)
     rows = lax.all_to_all(copies, "yh", 0, 0, tiled=True)
     mine, other = [rows], []
     for steps in range(1, X):
         mine.append(shift(rows, "x", X, steps))
     for steps in range(X):
         other.append(swap(mine[steps], "core"))
+    tokens, grad = call(
+        prepare_kernel, [shape(tokens.shape), shape((count, width), F32)], tokens, out_grad.T
+    )
     hidden_t, d_both, *partials = call(
         forward_kernel,
         [shape((width, count), F32), shape((count, 2 * width))]
         + [shape((half, columns))] * (2 * PIECES),
         place,
         tokens,
-        out_grad.T,
+        grad,
         *mine,
         *other,
         scalars=1,

time: 200 us -> 207 us (1.035)
  the two profiles are of different devices: /device:TPU:1 before, /device:TPU:23 now
where the time goes in v3:
time: 207 us; the launch traced here: 206 us
  waiting for transfers between devices  79.8 us (39%)
  starting transfers between devices  53.1 us (26%)
  blocking collectives  47 us (23%)
  Pallas kernels  19.8 us (10%)
  local copies, waits for them, and re-layouts  5.66 us (3%)
    ppermute x9, waiting for transfers between devices, shift(): lax.ppermute(array, axis, [(i, (i + steps) % size) for i in range(size)])  45.5 us
    all_to_all x1, blocking collectives, compute(): lax.all_to_all(x_copies, 'z', 0, 0, tiled=True).reshape(half, columns)  26 us
    ppermute x9, starting transfers between devices, shift(): lax.ppermute(array, axis, [(i, (i + steps) % size) for i in range(size)])  24.8 us
    all_to_all x1, blocking collectives, compute(): rows = lax.all_to_all(copies, 'yh', 0, 0, tiled=True)  21 us
    ppermute x7, waiting for transfers between devices, swap(): return lax.ppermute(array, axis, [(0, 1), (1, 0)])  19.1 us
    ppermute x7, starting transfers between devices, swap(): return lax.ppermute(array, axis, [(0, 1), (1, 0)])  18.2 us
    pallas_call x9, Pallas kernels, call(): pl.pallas_call(kernel, in_specs=[SM] * scalars + [VM] * (len(operands) -...  18 us
    all_to_all x1, waiting for transfers between devices, compute(): lax.all_to_all(x_sum.reshape(Z, chunk, columns), 'z', 0, 0, tiled=True)  15.2 us
  transfers between devices with their start and end apart: 17, of which 8 were waited for; matrix products, arithmetic and copies ran while one was open for 0% of the time, Pallas kernels for 4%

profile of v3, /device:TPU:23, one launch (start us, length us, event | category | flops | bytes accessed | tf_op | source)
XLA Modules:
  0.0 206.3 jit_solution(13293446939997448650)
XLA Ops:
  0.6 1.8 shard_map.94
  2.4 21.0 %all_to_all.15.rest_0_ = bf16[4,64,896]{2,1,0:T(8,128)(2,1)S(1)} all-to-all(bf16[4,64,896]{2,1,0:T(8,128)(2,1)} %shard_map.94), channel_id=1, replica_groups=mesh['yh'=4,'x'=4,'core'=2,'z'=8,'yl'=2] {'yh'}, dimensions={0} | all-to-all | bytes 917504 | tf_op jit(solution)/shard_map/all_to_all | solution.py:207
  23.4 2.4 %collective-permute-start.2 = (bf16[4,64,896]{2,1,0:T(8,128)(2,1)S(1)}, bf16[4,64,896]{2,1,0:T(8,128)(2,1)S(1)}, u32[]{:S(2)}, u32[]{:S(2)}) collective-permute-start(bf16[4,64,896]{2,1,0:T(8,128)(2,1)S(1)} %all_to_all.15.rest_0_), channel_id=1, source_target_pairs={{0,96},{32,0},{64,32},{96,64},{1,97},{33,1},{65,33},{97,65},{2,98}... | collective-permute-start | bytes 1376264 | tf_op jit(solution)/shard_map/ppermute | solution.py:171
  25.9 2.6 %collective-permute-start.1 = (bf16[4,64,896]{2,1,0:T(8,128)(2,1)S(1)}, bf16[4,64,896]{2,1,0:T(8,128)(2,1)S(1)}, u32[]{:S(2)}, u32[]{:S(2)}) collective-permute-start(bf16[4,64,896]{2,1,0:T(8,128)(2,1)S(1)} %all_to_all.15.rest_0_), channel_id=1, source_target_pairs={{0,64},{32,96},{64,0},{96,32},{1,65},{33,97},{65,1},{97,33},{2,66}... | collective-permute-start | bytes 1376264 | tf_op jit(solution)/shard_map/ppermute | solution.py:171
  28.5 3.8 %collective-permute-start = (bf16[4,64,896]{2,1,0:T(8,128)(2,1)S(1)}, bf16[4,64,896]{2,1,0:T(8,128)(2,1)S(1)}, u32[]{:S(2)}, u32[]{:S(2)}) collective-permute-start(bf16[4,64,896]{2,1,0:T(8,128)(2,1)S(1)} %all_to_all.15.rest_0_), channel_id=1, source_target_pairs={{0,32},{32,64},{64,96},{96,0},{1,33},{33,65},{65,97},{97,1},{2,34}... | collective-permute-start | bytes 1376264 | tf_op jit(solution)/shard_map/ppermute | solution.py:171
  32.4 3.4 %collective-permute-start.3 = (bf16[4,64,896]{2,1,0:T(8,128)(2,1)S(1)}, bf16[4,64,896]{2,1,0:T(8,128)(2,1)}, u32[]{:S(2)}, u32[]{:S(2)}) collective-permute-start(bf16[4,64,896]{2,1,0:T(8,128)(2,1)S(1)} %all_to_all.15.rest_0_), channel_id=1, source_target_pairs={{0,16},{16,0},{1,17},{17,1},{2,18},{18,2},{3,19},{19,3},{4,20},{20... | collective-permute-start | bytes 1376264 | tf_op jit(solution)/shard_map/ppermute | solution.py:167
  35.8 12.1 %collective-permute-done.2.rest_3_ = bf16[4,64,896]{2,1,0:T(8,128)(2,1)S(1)} collective-permute-done((bf16[4,64,896]{2,1,0:T(8,128)(2,1)S(1)}, bf16[4,64,896]{2,1,0:T(8,128)(2,1)S(1)}, u32[]{:S(2)}, u32[]{:S(2)}) %collective-permute-start.2) | collective-permute-done | bytes 458784 | tf_op jit(solution)/shard_map/ppermute | solution.py:171
  47.8 3.4 %collective-permute-start.6 = (bf16[4,64,896]{2,1,0:T(8,128)(2,1)S(1)}, bf16[4,64,896]{2,1,0:T(8,128)(2,1)}, u32[]{:S(2)}, u32[]{:S(2)}) collective-permute-start(bf16[4,64,896]{2,1,0:T(8,128)(2,1)S(1)} %collective-permute-done.2.rest_3_), channel_id=1, source_target_pairs={{0,16},{16,0},{1,17},{17,1},{2,18},{18,2},{3,19},{19,3},{4,20},{20... | collective-permute-start | bytes 1376264 | tf_op jit(solution)/shard_map/ppermute | solution.py:167
  51.2 0.0 collective-permute-done.1.rest_2_
  51.2 0.0 copy-start.3
  51.2 1.9 collective-permute-start.5
  53.2 0.0 collective-permute-done.rest_1_
  53.2 0.0 copy-start.5
  53.2 2.4 %collective-permute-start.4 = (bf16[4,64,896]{2,1,0:T(8,128)(2,1)S(1)}, bf16[4,64,896]{2,1,0:T(8,128)(2,1)}, u32[]{:S(2)}, u32[]{:S(2)}) collective-permute-start(bf16[4,64,896]{2,1,0:T(8,128)(2,1)S(1)} %collective-permute-done.rest_1_), channel_id=1, source_target_pairs={{0,16},{16,0},{1,17},{17,1},{2,18},{18,2},{3,19},{19,3},{4,20},{20... | collective-permute-start | bytes 1376264 | tf_op jit(solution)/shard_map/ppermute | solution.py:167
  55.6 0.0 copy-start.2
  55.6 1.4 copy-done.2
  57.0 0.0 copy-start.7
  57.0 1.0 copy-done.7
  58.0 0.2 shard_map.93
  58.3 0.1 pad_add_fusion.place
  58.3 0.0 collective-permute-done.3.rest_4_
  58.3 0.0 collective-permute-done.6.rest_7_
  58.3 0.0 collective-permute-done.5.rest_6_
  58.3 0.0 collective-permute-done.4.rest_5_
  58.4 0.0 copy-done.3
  58.4 0.0 copy-done.5
  58.4 0.0 copy-start.4
  58.4 1.0 copy-done.4
  59.4 1.0 copy-done.6
  60.4 7.2 %shard_map.95 = (f32[448,384]{1,0:T(8,128)}, bf16[384,896]{1,0:T(8,128)(2,1)S(1)}, bf16[192,2048]{1,0:T(8,128)(2,1)S(1)}, bf16[192,2048]{1,0:T(8,128)(2,1)S(1)}) custom-call(s32[4]{0:T(128)S(1)} %pad_add_fusion.place, bf16[384,2048]{1,0:T(8,128)(2,1)S(1)} %get-tuple-element.22.tokens, f32[384,448]{1,0:T(8,128)S(1)} %get-tuple-element.23.grad_ref, ...), custom_call_target="tpu_custom_call" | custom-call | tf_op jit(solution)/shard_map/pallas_call | solution.py:176
  67.6 1.9 collective-permute-start.7
  69.5 19.1 %collective-permute-done.7.second = bf16[192,2048]{1,0:T(8,128)(2,1)S(1)} collective-permute-done((bf16[192,2048]{1,0:T(8,128)(2,1)S(1)}, bf16[192,2048]{1,0:T(8,128)(2,1)S(1)}, u32[]{:S(2)}, u32[]{:S(2)}) %collective-permute-start.7) | collective-permute-done | bytes 786464 | tf_op jit(solution)/shard_map/ppermute | solution.py:167
  88.5 1.1 shard_map.96
  89.6 10.1 %all-to-all-start.1 = ((bf16[8,24,2048]{2,1,0:T(8,128)(2,1)}), bf16[8,24,2048]{2,1,0:T(8,128)(2,1)S(1)}, u32[]{:S(2)}, u32[]{:S(2)}) async-start(bf16[8,24,2048]{2,1,0:T(8,128)(2,1)} %bitcast.6), calls=%async_computation.1 | async-start | bytes 1572864 | tf_op jit(solution)/shard_map/all_to_all | solution.py:260
  99.7 4.1 %shard_map.99 = (bf16[4,4,64,896]{3,2,1,0:T(8,128)(2,1)S(1)}, bf16[4,4,64,896]{3,2,1,0:T(8,128)(2,1)}) custom-call(s32[4]{0:T(128)S(1)} %pad_add_fusion.place, bf16[384,2048]{1,0:T(8,128)(2,1)S(1)} %get-tuple-element.22.tokens, bf16[384,896]{1,0:T(8,128)(2,1)S(1)} %get-tuple-element.27.d_both), custom_call_target="tpu_custom_call" | custom-call | tf_op jit(solution)/shard_map/pallas_call | solution.py:176
  103.7 1.2 copy-done
  105.0 3.0 %collective-permute-start.9 = (bf16[4,4,64,896]{3,2,1,0:T(8,128)(2,1)}, bf16[4,4,64,896]{3,2,1,0:T(8,128)(2,1)}, u32[]{:S(2)}, u32[]{:S(2)}) collective-permute-start(bf16[4,4,64,896]{3,2,1,0:T(8,128)(2,1)} %get-tuple-element.29), channel_id=1, source_target_pairs={{0,16},{16,0},{1,17},{17,1},{2,18},{18,2},{3,19},{19,3},{4,20},{20... | collective-permute-start | bytes 5505032 | tf_op jit(solution)/shard_map/ppermute | solution.py:167
  108.0 15.2 %all-to-all-done.1.parts = bf16[8,24,2048]{2,1,0:T(8,128)(2,1)S(1)} async-done(((bf16[8,24,2048]{2,1,0:T(8,128)(2,1)}), bf16[8,24,2048]{2,1,0:T(8,128)(2,1)S(1)}, u32[]{:S(2)}, u32[]{:S(2)}) %all-to-all-start.1) | async-done | bytes 786464 | tf_op jit(solution)/shard_map/all_to_all | solution.py:260
  123.2 0.1 shard_map.97
  123.3 26.0 %all_to_all.16 = bf16[8,24,2048]{2,1,0:T(8,128)(2,1)S(1)} all-to-all(bf16[8,24,2048]{2,1,0:T(8,128)(2,1)S(1)} %shard_map.97), channel_id=1, replica_groups=mesh['yh'=4,'x'=4,'core'=2,'z'=8,'yl'=2] {'z'}, dimensions={0} | all-to-all | bytes 1572864 | tf_op jit(solution)/shard_map/all_to_all | solution.py:262
  149.3 2.2 %collective-permute-start.8 = (bf16[192,2048]{1,0:T(8,128)(2,1)S(1)}, bf16[192,2048]{1,0:T(8,128)(2,1)S(1)}, u32[]{:S(2)}, u32[]{:S(2)}) collective-permute-start(bf16[192,2048]{1,0:T(8,128)(2,1)S(1)} %bitcast.8), channel_id=1, source_target_pairs={{0,1},{1,0},{2,3},{3,2},{4,5},{5,4},{6,7},{7,6},{8,9},{9,8},{10,11... | collective-permute-start | bytes 2359304 | tf_op jit(solution)/shard_map/ppermute | solution.py:167
  151.5 0.0 collective-permute-done.9.second
  151.5 0.0 copy-done.1
  151.5 1.9 shard_map.100
  153.5 0.0 copy-start.8
  153.5 0.0 copy-start.9
  153.5 2.4 %collective-permute-start.10 = (bf16[4,64,896]{2,1,0:T(8,128)(2,1)S(1)}, bf16[4,64,896]{2,1,0:T(8,128)(2,1)S(1)}, u32[]{:S(2)}, u32[]{:S(2)}) collective-permute-start(bf16[4,64,896]{2,1,0:T(8,128)(2,1)S(1)} %get-tuple-element.31), channel_id=1, source_target_pairs={{0,32},{32,64},{64,96},{96,0},{1,33},{33,65},{65,97},{97,1},{2,34}... | collective-permute-start | bytes 1376264 | tf_op jit(solution)/shard_map/ppermute | solution.py:171
  155.9 1.9 collective-permute-start.11
  157.8 2.9 %collective-permute-start.12 = (bf16[4,64,896]{2,1,0:T(8,128)(2,1)S(1)}, bf16[4,64,896]{2,1,0:T(8,128)(2,1)S(1)}, u32[]{:S(2)}, u32[]{:S(2)}) collective-permute-start(bf16[4,64,896]{2,1,0:T(8,128)(2,1)S(1)} %get-tuple-element.33), channel_id=1, source_target_pairs={{0,96},{32,0},{64,32},{96,64},{1,97},{33,1},{65,33},{97,65},{2,98}... | collective-permute-start | bytes 1376264 | tf_op jit(solution)/shard_map/ppermute | solution.py:171
  160.7 5.8 %collective-permute-done.10.refs_1_ = bf16[4,64,896]{2,1,0:T(8,128)(2,1)S(1)} collective-permute-done((bf16[4,64,896]{2,1,0:T(8,128)(2,1)S(1)}, bf16[4,64,896]{2,1,0:T(8,128)(2,1)S(1)}, u32[]{:S(2)}, u32[]{:S(2)}) %collective-permute-start.10) | collective-permute-done | bytes 458784 | tf_op jit(solution)/shard_map/ppermute | solution.py:171
  166.6 3.7 %collective-permute-done.11.refs_2_ = bf16[4,64,896]{2,1,0:T(8,128)(2,1)S(1)} collective-permute-done((bf16[4,64,896]{2,1,0:T(8,128)(2,1)S(1)}, bf16[4,64,896]{2,1,0:T(8,128)(2,1)S(1)}, u32[]{:S(2)}, u32[]{:S(2)}) %collective-permute-start.11) | collective-permute-done | bytes 458784 | tf_op jit(solution)/shard_map/ppermute | solution.py:171
  170.2 11.3 %collective-permute-done.12.refs_3_ = bf16[4,64,896]{2,1,0:T(8,128)(2,1)S(1)} collective-permute-done((bf16[4,64,896]{2,1,0:T(8,128)(2,1)S(1)}, bf16[4,64,896]{2,1,0:T(8,128)(2,1)S(1)}, u32[]{:S(2)}, u32[]{:S(2)}) %collective-permute-start.12) | collective-permute-done | bytes 458784 | tf_op jit(solution)/shard_map/ppermute | solution.py:171
  181.6 0.2 shard_map.101
  181.8 2.2 %collective-permute-start.13 = (bf16[64,896]{1,0:T(8,128)(2,1)S(1)}, bf16[64,896]{1,0:T(8,128)(2,1)S(1)}, u32[]{:S(2)}, u32[]{:S(2)}) collective-permute-start(bf16[64,896]{1,0:T(8,128)(2,1)S(1)} %get-tuple-element.35), channel_id=1, source_target_pairs={{0,128},{128,256},{256,384},{384,0},{1,129},{129,257},{257,385},{3... | collective-permute-start | bytes 344072 | tf_op jit(solution)/shard_map/ppermute | solution.py:171
  184.0 4.4 %collective-permute-start.14 = (bf16[64,896]{1,0:T(8,128)(2,1)S(1)}, bf16[64,896]{1,0:T(8,128)(2,1)S(1)}, u32[]{:S(2)}, u32[]{:S(2)}) collective-permute-start(bf16[64,896]{1,0:T(8,128)(2,1)S(1)} %get-tuple-element.36), channel_id=1, source_target_pairs={{0,256},{128,384},{256,0},{384,128},{1,257},{129,385},{257,1},{385... | collective-permute-start | bytes 344072 | tf_op jit(solution)/shard_map/ppermute | solution.py:171
  188.4 2.1 %collective-permute-start.15 = (bf16[64,896]{1,0:T(8,128)(2,1)S(1)}, bf16[64,896]{1,0:T(8,128)(2,1)S(1)}, u32[]{:S(2)}, u32[]{:S(2)}) collective-permute-start(bf16[64,896]{1,0:T(8,128)(2,1)S(1)} %get-tuple-element.37), channel_id=1, source_target_pairs={{0,384},{128,0},{256,128},{384,256},{1,385},{129,1},{257,129},{385... | collective-permute-start | bytes 344072 | tf_op jit(solution)/shard_map/ppermute | solution.py:171
  190.5 0.0 collective-permute-done.13.refs_1_
  190.5 3.4 %collective-permute-done.14.refs_2_ = bf16[64,896]{1,0:T(8,128)(2,1)S(1)} collective-permute-done((bf16[64,896]{1,0:T(8,128)(2,1)S(1)}, bf16[64,896]{1,0:T(8,128)(2,1)S(1)}, u32[]{:S(2)}, u32[]{:S(2)}) %collective-permute-start.14) | collective-permute-done | bytes 114720 | tf_op jit(solution)/shard_map/ppermute | solution.py:171
  193.9 9.2 %collective-permute-done.15.refs_3_ = bf16[64,896]{1,0:T(8,128)(2,1)S(1)} collective-permute-done((bf16[64,896]{1,0:T(8,128)(2,1)S(1)}, bf16[64,896]{1,0:T(8,128)(2,1)S(1)}, u32[]{:S(2)}, u32[]{:S(2)}) %collective-permute-start.15) | collective-permute-done | bytes 114720 | tf_op jit(solution)/shard_map/ppermute | solution.py:171
  203.1 0.0 copy-done.8
  203.1 0.0 copy-done.9
  203.2 1.4 shard_map.102
  204.5 0.0 collective-permute-done.8.refs_1_
  204.5 1.8 shard_map.98
  (3 shorter events, 0.0 us)
Async XLA Ops:
  23.4 24.4 %collective-permute-start.2 = (bf16[4,64,896]{2,1,0:T(8,128)(2,1)S(1)}, bf16[4,64,896]{2,1,0:T(8,128)(2,1)S(1)}, u32[]{:S(2)}, u32[]{:S(2)}) collective-permute-start(bf16[4,64,896]{2,1,0:T(8,128)(2,1)S(1)} %all_to_all.15.rest_0_), channel_id=1, source_target_pairs={{0,96},{32,0},{64,32},{96,64},{1,97},{33,1},{65,33},{97,65},{2,98}... | collective-permute-start | bytes 1376264 | tf_op jit(solution)/shard_map/ppermute | solution.py:171
  25.9 25.3 %collective-permute-start.1 = (bf16[4,64,896]{2,1,0:T(8,128)(2,1)S(1)}, bf16[4,64,896]{2,1,0:T(8,128)(2,1)S(1)}, u32[]{:S(2)}, u32[]{:S(2)}) collective-permute-start(bf16[4,64,896]{2,1,0:T(8,128)(2,1)S(1)} %all_to_all.15.rest_0_), channel_id=1, source_target_pairs={{0,64},{32,96},{64,0},{96,32},{1,65},{33,97},{65,1},{97,33},{2,66}... | collective-permute-start | bytes 1376264 | tf_op jit(solution)/shard_map/ppermute | solution.py:171
  28.5 24.6 %collective-permute-start = (bf16[4,64,896]{2,1,0:T(8,128)(2,1)S(1)}, bf16[4,64,896]{2,1,0:T(8,128)(2,1)S(1)}, u32[]{:S(2)}, u32[]{:S(2)}) collective-permute-start(bf16[4,64,896]{2,1,0:T(8,128)(2,1)S(1)} %all_to_all.15.rest_0_), channel_id=1, source_target_pairs={{0,32},{32,64},{64,96},{96,0},{1,33},{33,65},{65,97},{97,1},{2,34}... | collective-permute-start | bytes 1376264 | tf_op jit(solution)/shard_map/ppermute | solution.py:171
  32.4 26.0 %collective-permute-start.3 = (bf16[4,64,896]{2,1,0:T(8,128)(2,1)S(1)}, bf16[4,64,896]{2,1,0:T(8,128)(2,1)}, u32[]{:S(2)}, u32[]{:S(2)}) collective-permute-start(bf16[4,64,896]{2,1,0:T(8,128)(2,1)S(1)} %all_to_all.15.rest_0_), channel_id=1, source_target_pairs={{0,16},{16,0},{1,17},{17,1},{2,18},{18,2},{3,19},{19,3},{4,20},{20... | collective-permute-start | bytes 1376264 | tf_op jit(solution)/shard_map/ppermute | solution.py:167
  47.8 10.5 %collective-permute-start.6 = (bf16[4,64,896]{2,1,0:T(8,128)(2,1)S(1)}, bf16[4,64,896]{2,1,0:T(8,128)(2,1)}, u32[]{:S(2)}, u32[]{:S(2)}) collective-permute-start(bf16[4,64,896]{2,1,0:T(8,128)(2,1)S(1)} %collective-permute-done.2.rest_3_), channel_id=1, source_target_pairs={{0,16},{16,0},{1,17},{17,1},{2,18},{18,2},{3,19},{19,3},{4,20},{20... | collective-permute-start | bytes 1376264 | tf_op jit(solution)/shard_map/ppermute | solution.py:167
  51.2 7.1 %copy-start.3 = (bf16[4,64,896]{2,1,0:T(8,128)(2,1)}, bf16[4,64,896]{2,1,0:T(8,128)(2,1)S(1)}, u32[]{:S(2)}) copy-start(bf16[4,64,896]{2,1,0:T(8,128)(2,1)S(1)} %collective-permute-done.1.rest_2_) | copy-start | bytes 1376260
  51.2 7.1 %collective-permute-start.5 = (bf16[4,64,896]{2,1,0:T(8,128)(2,1)S(1)}, bf16[4,64,896]{2,1,0:T(8,128)(2,1)}, u32[]{:S(2)}, u32[]{:S(2)}) collective-permute-start(bf16[4,64,896]{2,1,0:T(8,128)(2,1)S(1)} %collective-permute-done.1.rest_2_), channel_id=1, source_target_pairs={{0,16},{16,0},{1,17},{17,1},{2,18},{18,2},{3,19},{19,3},{4,20},{20... | collective-permute-start | bytes 1376264 | tf_op jit(solution)/shard_map/ppermute | solution.py:167
  53.2 5.2 %copy-start.5 = (bf16[4,64,896]{2,1,0:T(8,128)(2,1)}, bf16[4,64,896]{2,1,0:T(8,128)(2,1)S(1)}, u32[]{:S(2)}) copy-start(bf16[4,64,896]{2,1,0:T(8,128)(2,1)S(1)} %collective-permute-done.rest_1_) | copy-start | bytes 1376260
  53.2 5.2 %collective-permute-start.4 = (bf16[4,64,896]{2,1,0:T(8,128)(2,1)S(1)}, bf16[4,64,896]{2,1,0:T(8,128)(2,1)}, u32[]{:S(2)}, u32[]{:S(2)}) collective-permute-start(bf16[4,64,896]{2,1,0:T(8,128)(2,1)S(1)} %collective-permute-done.rest_1_), channel_id=1, source_target_pairs={{0,16},{16,0},{1,17},{17,1},{2,18},{18,2},{3,19},{19,3},{4,20},{20... | collective-permute-start | bytes 1376264 | tf_op jit(solution)/shard_map/ppermute | solution.py:167
  55.6 1.4 copy-start.2
  57.0 1.0 copy-start.7
  58.4 1.0 copy-start.4
  59.4 1.0 copy-start.6
  67.6 21.0 %collective-permute-start.7 = (bf16[192,2048]{1,0:T(8,128)(2,1)S(1)}, bf16[192,2048]{1,0:T(8,128)(2,1)S(1)}, u32[]{:S(2)}, u32[]{:S(2)}) collective-permute-start(bf16[192,2048]{1,0:T(8,128)(2,1)S(1)} %get-tuple-element.26), channel_id=1, source_target_pairs={{0,1},{1,0},{2,3},{3,2},{4,5},{5,4},{6,7},{7,6},{8,9},{9,8},{10,11... | collective-permute-start | bytes 2359304 | tf_op jit(solution)/shard_map/ppermute | solution.py:167
  89.6 33.6 %all-to-all-start.1 = ((bf16[8,24,2048]{2,1,0:T(8,128)(2,1)}), bf16[8,24,2048]{2,1,0:T(8,128)(2,1)S(1)}, u32[]{:S(2)}, u32[]{:S(2)}) async-start(bf16[8,24,2048]{2,1,0:T(8,128)(2,1)} %bitcast.6), calls=%async_computation.1 | async-start | bytes 1572864 | tf_op jit(solution)/shard_map/all_to_all | solution.py:260
  103.7 1.2 copy-start
  105.0 46.6 %collective-permute-start.9 = (bf16[4,4,64,896]{3,2,1,0:T(8,128)(2,1)}, bf16[4,4,64,896]{3,2,1,0:T(8,128)(2,1)}, u32[]{:S(2)}, u32[]{:S(2)}) collective-permute-start(bf16[4,4,64,896]{3,2,1,0:T(8,128)(2,1)} %get-tuple-element.29), channel_id=1, source_target_pairs={{0,16},{16,0},{1,17},{17,1},{2,18},{18,2},{3,19},{19,3},{4,20},{20... | collective-permute-start | bytes 5505032 | tf_op jit(solution)/shard_map/ppermute | solution.py:167
  123.2 28.3 %copy-start.1 = (bf16[4,4,64,896]{3,2,1,0:T(8,128)(2,1)S(1)}, bf16[4,4,64,896]{3,2,1,0:T(8,128)(2,1)}, u32[]{:S(2)}) copy-start(bf16[4,4,64,896]{3,2,1,0:T(8,128)(2,1)} %copy-done) | copy-start | bytes 5505028
  149.3 55.2 %collective-permute-start.8 = (bf16[192,2048]{1,0:T(8,128)(2,1)S(1)}, bf16[192,2048]{1,0:T(8,128)(2,1)S(1)}, u32[]{:S(2)}, u32[]{:S(2)}) collective-permute-start(bf16[192,2048]{1,0:T(8,128)(2,1)S(1)} %bitcast.8), channel_id=1, source_target_pairs={{0,1},{1,0},{2,3},{3,2},{4,5},{5,4},{6,7},{7,6},{8,9},{9,8},{10,11... | collective-permute-start | bytes 2359304 | tf_op jit(solution)/shard_map/ppermute | solution.py:167
  153.5 49.7 %copy-start.8 = (s32[1,7]{1,0:T(1,128)S(1)}, s32[1,7]{1,0:T(1,128)}, u32[]{:S(2)}) copy-start(s32[1,7]{1,0:T(1,128)} %gm.1) | copy-start | bytes 88
  153.5 49.6 %copy-start.9 = (s32[1,7]{1,0:T(1,128)S(1)}, s32[1,7]{1,0:T(1,128)}, u32[]{:S(2)}) copy-start(s32[1,7]{1,0:T(1,128)} %um.1) | copy-start | bytes 88
  153.5 13.1 %collective-permute-start.10 = (bf16[4,64,896]{2,1,0:T(8,128)(2,1)S(1)}, bf16[4,64,896]{2,1,0:T(8,128)(2,1)S(1)}, u32[]{:S(2)}, u32[]{:S(2)}) collective-permute-start(bf16[4,64,896]{2,1,0:T(8,128)(2,1)S(1)} %get-tuple-element.31), channel_id=1, source_target_pairs={{0,32},{32,64},{64,96},{96,0},{1,33},{33,65},{65,97},{97,1},{2,34}... | collective-permute-start | bytes 1376264 | tf_op jit(solution)/shard_map/ppermute | solution.py:171
  155.9 14.3 %collective-permute-start.11 = (bf16[4,64,896]{2,1,0:T(8,128)(2,1)S(1)}, bf16[4,64,896]{2,1,0:T(8,128)(2,1)S(1)}, u32[]{:S(2)}, u32[]{:S(2)}) collective-permute-start(bf16[4,64,896]{2,1,0:T(8,128)(2,1)S(1)} %get-tuple-element.32), channel_id=1, source_target_pairs={{0,64},{32,96},{64,0},{96,32},{1,65},{33,97},{65,1},{97,33},{2,66}... | collective-permute-start | bytes 1376264 | tf_op jit(solution)/shard_map/ppermute | solution.py:171
  157.8 23.7 %collective-permute-start.12 = (bf16[4,64,896]{2,1,0:T(8,128)(2,1)S(1)}, bf16[4,64,896]{2,1,0:T(8,128)(2,1)S(1)}, u32[]{:S(2)}, u32[]{:S(2)}) collective-permute-start(bf16[4,64,896]{2,1,0:T(8,128)(2,1)S(1)} %get-tuple-element.33), channel_id=1, source_target_pairs={{0,96},{32,0},{64,32},{96,64},{1,97},{33,1},{65,33},{97,65},{2,98}... | collective-permute-start | bytes 1376264 | tf_op jit(solution)/shard_map/ppermute | solution.py:171
  181.8 8.7 %collective-permute-start.13 = (bf16[64,896]{1,0:T(8,128)(2,1)S(1)}, bf16[64,896]{1,0:T(8,128)(2,1)S(1)}, u32[]{:S(2)}, u32[]{:S(2)}) collective-permute-start(bf16[64,896]{1,0:T(8,128)(2,1)S(1)} %get-tuple-element.35), channel_id=1, source_target_pairs={{0,128},{128,256},{256,384},{384,0},{1,129},{129,257},{257,385},{3... | collective-permute-start | bytes 344072 | tf_op jit(solution)/shard_map/ppermute | solution.py:171
  184.0 9.9 %collective-permute-start.14 = (bf16[64,896]{1,0:T(8,128)(2,1)S(1)}, bf16[64,896]{1,0:T(8,128)(2,1)S(1)}, u32[]{:S(2)}, u32[]{:S(2)}) collective-permute-start(bf16[64,896]{1,0:T(8,128)(2,1)S(1)} %get-tuple-element.36), channel_id=1, source_target_pairs={{0,256},{128,384},{256,0},{384,128},{1,257},{129,385},{257,1},{385... | collective-permute-start | bytes 344072 | tf_op jit(solution)/shard_map/ppermute | solution.py:171
  188.4 14.7 %collective-permute-start.15 = (bf16[64,896]{1,0:T(8,128)(2,1)S(1)}, bf16[64,896]{1,0:T(8,128)(2,1)S(1)}, u32[]{:S(2)}, u32[]{:S(2)}) collective-permute-start(bf16[64,896]{1,0:T(8,128)(2,1)S(1)} %get-tuple-element.37), channel_id=1, source_target_pairs={{0,384},{128,0},{256,128},{384,256},{1,385},{129,1},{257,129},{385... | collective-permute-start | bytes 344072 | tf_op jit(solution)/shard_map/ppermute | solution.py:171

commit v4 on v3

--- a/solution.py
+++ b/solution.py
@@ -12,7 +12,7 @@
 BF16 = jnp.bfloat16
 F32 = jnp.float32
 YH, X, CORE, Z, YL = 4, 4, 2, 8, 2
-PIECES = 1
+FIRST = 1536
 VM = pl.BlockSpec(memory_space=pltpu.VMEM)
 HB = pl.BlockSpec(memory_space=pltpu.HBM)
 SM = pl.BlockSpec(memory_space=pltpu.SMEM)
@@ -52,16 +52,17 @@
 
 def forward_kernel(place, tokens, grad_ref, *rest):
     mine, other = rest[:X], rest[X : 2 * X]
-    hidden_t, d_both, *rest = rest[2 * X :]
-    sends, keeps, w = rest[:PIECES], rest[PIECES:-1], rest[-1]
+    hidden_t, d_both, send, keep, side, w = rest[2 * X :]
     core, half, own_x = place[0], place[1], place[2]
     width = grad_ref.shape[1]
     for yh in range(YH):
         for back in range(X):
             x = lax.rem(own_x + (X - back), X)
-            w[yh * X + x, core] = mine[back][yh]
-            w[yh * X + x, 1 - core] = other[back][yh]
-    weights = w[...].reshape(YH * X * CORE * BLOCK, 2 * width)
+            row = (yh * X + x) * CORE * BLOCK
+            for rows, index in ((mine[back], core), (other[back], 1 - core)):
+                start = pl.multiple_of(row + index * BLOCK, BLOCK)
+                w[pl.ds(start, BLOCK), :] = rows[yh]
+    weights = w[...]
     preact = jnp.dot(tokens[...], weights, preferred_element_type=F32)
     gate = preact[:, :width]
     up = preact[:, width:]
@@ -72,16 +73,17 @@
     d_gate = grad * up * sigmoid * (1.0 + gate * (1.0 - sigmoid))
     d_up = grad * activation
     d_both[...] = jnp.concatenate([d_gate, d_up], axis=1).astype(BF16)
-    rows, columns = sends[0].shape
-    for index, outs in ((1 - half, sends), (half, keeps)):
-        part = d_both[pl.ds(pl.multiple_of(index * rows, rows), rows), :]
-        for piece, out in enumerate(outs):
-            out[...] = lax.dot_general(
-                part,
-                weights[piece * columns : (piece + 1) * columns],
-                (((1,), (1,)), ((), ())),
-                preferred_element_type=F32,
-            ).astype(BF16)
+    rows = send.shape[0]
+    for out, index in ((send, 1 - half), (keep, half)):
+        start = pl.multiple_of(index * rows, rows)
+        out[...] = to_tokens(d_both[pl.ds(start, rows), :], weights[:FIRST])
+    side[...] = to_tokens(d_both[...], weights[FIRST:])
+
+
+def to_tokens(grad, weights):
+    return lax.dot_general(
+        grad, weights, (((1,), (1,)), ((), ())), preferred_element_type=F32
+    ).astype(BF16)
 
 
 def weight_kernel(place, tokens, d_both, keep, send):
@@ -139,20 +141,28 @@
     return total.astype(BF16)
 
 
+def sum_kernel(parts, out):
+    out[...] = total_of(parts)
+
+
 def sum_copies_kernel(parts, out):
     total = total_of(parts)
     for copy in range(out.shape[0]):
         out[copy] = total
 
 
-def join_kernel(place, *refs):
-    mine, other, out = refs[:PIECES], refs[PIECES:-1], refs[-1]
+def add_copies_kernel(first, second, out):
+    total = (first[...].astype(F32) + second[...].astype(F32)).astype(BF16)
+    for copy in range(out.shape[0]):
+        out[copy] = total
+
+
+def join_kernel(place, mine, other, side, out):
     half = place[1]
-    rows, columns = mine[0].shape
-    for piece in range(PIECES):
-        span = slice(piece * columns, (piece + 1) * columns)
-        out[pl.ds(pl.multiple_of(half * rows, rows), rows), span] = mine[piece][...]
-        out[pl.ds(pl.multiple_of((1 - half) * rows, rows), rows), span] = other[piece][...]
+    rows = mine.shape[0]
+    out[pl.ds(pl.multiple_of(half * rows, rows), rows), :FIRST] = mine[...]
+    out[pl.ds(pl.multiple_of((1 - half) * rows, rows), rows), :FIRST] = other[...]
+    out[:, FIRST:] = side[...]
 
 
 def shape(dims, dtype=BF16):
@@ -189,7 +199,7 @@
     count, features = tokens.shape
     half = count // YL
     chunk = half // Z
-    columns = features // PIECES
+    rest = features - FIRST
     place = jnp.stack([lax.axis_index(name) for name in ("core", "yl", "x", "yh")])
     copies = pl.pallas_call(
         mask_kernel,
@@ -213,22 +223,25 @@
     tokens, grad = call(
         prepare_kernel, [shape(tokens.shape), shape((count, width), F32)], tokens, out_grad.T
     )
-    hidden_t, d_both, *partials = call(
+    hidden_t, d_both, send, keep, side = call(
         forward_kernel,
-        [shape((width, count), F32), shape((count, 2 * width))]
-        + [shape((half, columns))] * (2 * PIECES),
+        [
+            shape((width, count), F32),
+            shape((count, 2 * width)),
+            shape((half, FIRST)),
+            shape((half, FIRST)),
+            shape((count, rest)),
+        ],
         place,
         tokens,
         grad,
         *mine,
         *other,
         scalars=1,
-        scratch=[pltpu.VMEM((YH * X, CORE, BLOCK, 2 * width), BF16)],
-    )
-    sends, keeps = partials[:PIECES], partials[PIECES:]
-    received = []
-    for piece in range(PIECES):
-        received.append(swap(sends[piece], "yl"))
+        scratch=[pltpu.VMEM((features, 2 * width), BF16)],
+    )
+    received = swap(send, "yl")
+    side = lax.all_to_all(side.reshape(Z, 2 * chunk, rest), "z", 0, 0, tiled=True)
     w_keep, w_send = call(
         weight_kernel,
         [shape((X, YH, BLOCK, 2 * width))] * 2,
@@ -238,9 +251,7 @@
         scalars=1,
     )
     w_received = swap(w_send, "core")
-    w_parts = call(
-        pair_kernel, [shape((YH, BLOCK, 2 * width))] * X, w_keep, w_received
-    )
+    w_parts = call(pair_kernel, [shape((YH, BLOCK, 2 * width))] * X, w_keep, w_received)
     for steps in range(1, X):
         w_parts[steps] = shift(w_parts[steps], "x", X, steps)
     w_parts = call(rows_kernel, [shape((BLOCK, 2 * width))] * YH, *w_parts)
@@ -254,16 +265,17 @@
         *w_parts,
         scalars=2,
     )
-    own, others = [], []
-    for piece in range(PIECES):
-        x_sum = call(add_kernel, shape((half, columns)), keeps[piece], received[piece])
-        x_parts = lax.all_to_all(x_sum.reshape(Z, chunk, columns), "z", 0, 0, tiled=True)
-        x_copies = call(sum_copies_kernel, shape((Z, chunk, columns)), x_parts)
-        x_half = lax.all_to_all(x_copies, "z", 0, 0, tiled=True).reshape(half, columns)
-        own.append(x_half)
-        others.append(swap(x_half, "yl"))
+    main = call(add_kernel, shape((half, FIRST)), keep, received)
+    main = lax.all_to_all(main.reshape(Z, chunk, FIRST), "z", 0, 0, tiled=True)
+    side = call(sum_kernel, shape((2 * chunk, rest)), side)
+    side_other = swap(side, "yl")
+    side = call(add_copies_kernel, shape((Z, 2 * chunk, rest)), side, side_other)
+    main = call(sum_copies_kernel, shape((Z, chunk, FIRST)), main)
+    main = lax.all_to_all(main, "z", 0, 0, tiled=True).reshape(half, FIRST)
+    main_other = swap(main, "yl")
+    side = lax.all_to_all(side, "z", 0, 0, tiled=True).reshape(count, rest)
     grad_tokens = call(
-        join_kernel, shape((count, features)), place, *own, *others, scalars=1
+        join_kernel, shape((count, features)), place, main, main_other, side, scalars=1
     )
     return (hidden_t.T, grad_tokens, grad_gate, grad_up)
 

time: 207 us -> 217 us (1.048)
  blocking collectives: 47 us -> 21 us
  waiting for transfers between devices: 79.8 us -> 102 us
  starting transfers between devices: 53.1 us -> 65.7 us
    all_to_all x1 -> x0, blocking collectives: 26 us -> none  [compute(): lax.all_to_all(x_copies, 'z', 0, 0, tiled=True).reshape(half, columns)]
    all_to_all x1 -> x4, waiting for transfers between devices: 15.2 us -> 38.5 us  [the longest x1 14.2 us: compute(): lax.all_to_all(side.reshape(Z, 2 * chunk, rest), 'z', 0, 0, tiled=True)]
    all_to_all x1 -> x4, starting transfers between devices: 10.1 us -> 20.5 us  [the longest x1 10.1 us: compute(): main = lax.all_to_all(main.reshape(Z, chunk, FIRST), 'z', 0, 0, tiled=True)]
    ppermute x7 -> x8, starting transfers between devices: 18.2 us -> 20.4 us  [swap(): return lax.ppermute(array, axis, [(0, 1), (1, 0)])]
    pallas_call x9 -> x11, Pallas kernels: 18 us -> 19.6 us  [call(): pl.pallas_call(kernel, in_specs=[SM] * scalars + [VM] * (len(operands) -...]
    ppermute x7 -> x8, waiting for transfers between devices: 19.1 us -> 17.8 us  [swap(): return lax.ppermute(array, axis, [(0, 1), (1, 0)])]
    unnamed x20 -> x16, local copies, waits for them, and re-layouts: 5.66 us -> 4.64 us
  transfers between devices with their start and end apart: 17 -> 21, of which waited for: 8 -> 11; matrix products, arithmetic and copies ran while one was open for 0% -> 0% of each run, Pallas kernels for 4% -> 4%
where the time goes in v4:
time: 217 us; the launch traced here: 216 us
  waiting for transfers between devices  102 us (47%)
  starting transfers between devices  65.7 us (30%)
  Pallas kernels  21.4 us (10%)
  blocking collectives  21 us (10%)
  local copies, waits for them, and re-layouts  4.64 us (2%)
    ppermute x9, waiting for transfers between devices, shift(): lax.ppermute(array, axis, [(i, (i + steps) % size) for i in range(size)])  45.6 us
    ppermute x9, starting transfers between devices, shift(): lax.ppermute(array, axis, [(i, (i + steps) % size) for i in range(size)])  24.8 us
    all_to_all x1, blocking collectives, compute(): rows = lax.all_to_all(copies, 'yh', 0, 0, tiled=True)  21 us
    ppermute x8, starting transfers between devices, swap(): return lax.ppermute(array, axis, [(0, 1), (1, 0)])  20.4 us
    pallas_call x11, Pallas kernels, call(): pl.pallas_call(kernel, in_specs=[SM] * scalars + [VM] * (len(operands) -...  19.6 us
    ppermute x8, waiting for transfers between devices, swap(): return lax.ppermute(array, axis, [(0, 1), (1, 0)])  17.8 us
    all_to_all x1, waiting for transfers between devices, compute(): lax.all_to_all(side.reshape(Z, 2 * chunk, rest), 'z', 0, 0, tiled=True)  14.2 us
    all_to_all x1, waiting for transfers between devices, compute(): main = lax.all_to_all(main, 'z', 0, 0, tiled=True).reshape(half, FIRST)  13.3 us
  transfers between devices with their start and end apart: 21, of which 11 were waited for; matrix products, arithmetic and copies ran while one was open for 0% of the time, Pallas kernels for 4%

profile of v4, /device:TPU:23, one launch (start us, length us, event | category | flops | bytes accessed | tf_op | source)
XLA Modules:
  0.0 215.7 jit_solution(4796262607119583105)
XLA Ops:
  0.6 1.8 shard_map.94
  2.4 21.0 %all_to_all.25.rest_0_ = bf16[4,64,896]{2,1,0:T(8,128)(2,1)S(1)} all-to-all(bf16[4,64,896]{2,1,0:T(8,128)(2,1)} %shard_map.94), channel_id=1, replica_groups=mesh['yh'=4,'x'=4,'core'=2,'z'=8,'yl'=2] {'yh'}, dimensions={0} | all-to-all | bytes 917504 | tf_op jit(solution)/shard_map/all_to_all | solution.py:217
  23.4 2.4 %collective-permute-start.2 = (bf16[4,64,896]{2,1,0:T(8,128)(2,1)S(1)}, bf16[4,64,896]{2,1,0:T(8,128)(2,1)S(1)}, u32[]{:S(2)}, u32[]{:S(2)}) collective-permute-start(bf16[4,64,896]{2,1,0:T(8,128)(2,1)S(1)} %all_to_all.25.rest_0_), channel_id=1, source_target_pairs={{0,96},{32,0},{64,32},{96,64},{1,97},{33,1},{65,33},{97,65},{2,98}... | collective-permute-start | bytes 1376264 | tf_op jit(solution)/shard_map/ppermute | solution.py:181
  25.9 2.6 %collective-permute-start.1 = (bf16[4,64,896]{2,1,0:T(8,128)(2,1)S(1)}, bf16[4,64,896]{2,1,0:T(8,128)(2,1)S(1)}, u32[]{:S(2)}, u32[]{:S(2)}) collective-permute-start(bf16[4,64,896]{2,1,0:T(8,128)(2,1)S(1)} %all_to_all.25.rest_0_), channel_id=1, source_target_pairs={{0,64},{32,96},{64,0},{96,32},{1,65},{33,97},{65,1},{97,33},{2,66}... | collective-permute-start | bytes 1376264 | tf_op jit(solution)/shard_map/ppermute | solution.py:181
  28.5 3.8 %collective-permute-start = (bf16[4,64,896]{2,1,0:T(8,128)(2,1)S(1)}, bf16[4,64,896]{2,1,0:T(8,128)(2,1)}, u32[]{:S(2)}, u32[]{:S(2)}) collective-permute-start(bf16[4,64,896]{2,1,0:T(8,128)(2,1)S(1)} %all_to_all.25.rest_0_), channel_id=1, source_target_pairs={{0,32},{32,64},{64,96},{96,0},{1,33},{33,65},{65,97},{97,1},{2,34}... | collective-permute-start | bytes 1376264 | tf_op jit(solution)/shard_map/ppermute | solution.py:181
  32.4 3.4 %collective-permute-start.3 = (bf16[4,64,896]{2,1,0:T(8,128)(2,1)S(1)}, bf16[4,64,896]{2,1,0:T(8,128)(2,1)}, u32[]{:S(2)}, u32[]{:S(2)}) collective-permute-start(bf16[4,64,896]{2,1,0:T(8,128)(2,1)S(1)} %all_to_all.25.rest_0_), channel_id=1, source_target_pairs={{0,16},{16,0},{1,17},{17,1},{2,18},{18,2},{3,19},{19,3},{4,20},{20... | collective-permute-start | bytes 1376264 | tf_op jit(solution)/shard_map/ppermute | solution.py:177
  35.8 12.1 %collective-permute-done.2.rest_3_ = bf16[4,64,896]{2,1,0:T(8,128)(2,1)S(1)} collective-permute-done((bf16[4,64,896]{2,1,0:T(8,128)(2,1)S(1)}, bf16[4,64,896]{2,1,0:T(8,128)(2,1)S(1)}, u32[]{:S(2)}, u32[]{:S(2)}) %collective-permute-start.2) | collective-permute-done | bytes 458784 | tf_op jit(solution)/shard_map/ppermute | solution.py:181
  47.8 3.4 %collective-permute-start.6 = (bf16[4,64,896]{2,1,0:T(8,128)(2,1)S(1)}, bf16[4,64,896]{2,1,0:T(8,128)(2,1)}, u32[]{:S(2)}, u32[]{:S(2)}) collective-permute-start(bf16[4,64,896]{2,1,0:T(8,128)(2,1)S(1)} %collective-permute-done.2.rest_3_), channel_id=1, source_target_pairs={{0,16},{16,0},{1,17},{17,1},{2,18},{18,2},{3,19},{19,3},{4,20},{20... | collective-permute-start | bytes 1376264 | tf_op jit(solution)/shard_map/ppermute | solution.py:177
  51.2 0.0 collective-permute-done.1.rest_2_
  51.2 0.0 copy-start.3
  51.2 1.9 collective-permute-start.5
  53.2 0.0 collective-permute-done.rest_1_
  53.2 2.4 %collective-permute-start.4 = (bf16[4,64,896]{2,1,0:T(8,128)(2,1)}, bf16[4,64,896]{2,1,0:T(8,128)(2,1)}, u32[]{:S(2)}, u32[]{:S(2)}) collective-permute-start(bf16[4,64,896]{2,1,0:T(8,128)(2,1)} %collective-permute-done.rest_1_), channel_id=1, source_target_pairs={{0,16},{16,0},{1,17},{17,1},{2,18},{18,2},{3,19},{19,3},{4,20},{20... | collective-permute-start | bytes 1376264 | tf_op jit(solution)/shard_map/ppermute | solution.py:177
  55.6 0.0 copy-start.2
  55.6 1.4 copy-done.2
  57.0 1.0 copy-done.5
  58.0 0.2 shard_map.93
  58.2 0.1 pad_add_fusion.place
  58.3 0.0 collective-permute-done.3.rest_4_
  58.3 0.0 collective-permute-done.6.rest_7_
  58.3 0.0 collective-permute-done.5.rest_6_
  58.3 0.0 collective-permute-done.4.rest_5_
  58.4 0.0 copy-start.4
  58.4 1.0 copy-done.4
  59.4 7.3 %shard_map.95 = (f32[448,384]{1,0:T(8,128)}, bf16[384,896]{1,0:T(8,128)(2,1)S(1)}, bf16[192,1536]{1,0:T(8,128)(2,1)S(1)}, bf16[192,1536]{1,0:T(8,128)(2,1)S(1)}, bf16[384,512]{1,0:T(8,128)(2,1)}) custom-call(s32[4]{0:T(128)S(1)} %pad_add_fusion.place, bf16[384,2048]{1,0:T(8,128)(2,1)S(1)} %get-tuple-element.23.tokens, ...), custom_call_target="tpu_custom_call" | custom-call | tf_op jit(solution)/shard_map/pallas_call | solution.py:186
  66.7 1.9 collective-permute-start.7
  68.6 14.8 %collective-permute-done.7.second = bf16[192,1536]{1,0:T(8,128)(2,1)S(1)} collective-permute-done((bf16[192,1536]{1,0:T(8,128)(2,1)S(1)}, bf16[192,1536]{1,0:T(8,128)(2,1)S(1)}, u32[]{:S(2)}, u32[]{:S(2)}) %collective-permute-start.7) | collective-permute-done | bytes 589856 | tf_op jit(solution)/shard_map/ppermute | solution.py:177
  83.4 0.9 shard_map.96
  84.3 10.1 %all-to-all-start.1 = ((bf16[8,24,1536]{2,1,0:T(8,128)(2,1)}), bf16[8,24,1536]{2,1,0:T(8,128)(2,1)S(1)}, u32[]{:S(2)}, u32[]{:S(2)}) async-start(bf16[8,24,1536]{2,1,0:T(8,128)(2,1)} %bitcast.6), calls=%async_computation.1 | async-start | bytes 1179648 | tf_op jit(solution)/shard_map/all_to_all | solution.py:269
  94.4 4.0 %shard_map.101 = (bf16[4,4,64,896]{3,2,1,0:T(8,128)(2,1)S(1)}, bf16[4,4,64,896]{3,2,1,0:T(8,128)(2,1)}) custom-call(s32[4]{0:T(128)S(1)} %pad_add_fusion.place, bf16[384,2048]{1,0:T(8,128)(2,1)S(1)} %get-tuple-element.23.tokens, bf16[384,896]{1,0:T(8,128)(2,1)S(1)} %get-tuple-element.29.d_both), custom_call_target="tpu_custom_call" | custom-call | tf_op jit(solution)/shard_map/pallas_call | solution.py:186
  98.5 1.2 copy-done
  99.7 3.0 %collective-permute-start.10 = (bf16[4,4,64,896]{3,2,1,0:T(8,128)(2,1)}, bf16[4,4,64,896]{3,2,1,0:T(8,128)(2,1)}, u32[]{:S(2)}, u32[]{:S(2)}) collective-permute-start(bf16[4,4,64,896]{3,2,1,0:T(8,128)(2,1)} %get-tuple-element.31), channel_id=1, source_target_pairs={{0,16},{16,0},{1,17},{17,1},{2,18},{18,2},{3,19},{19,3},{4,20},{20... | collective-permute-start | bytes 5505032 | tf_op jit(solution)/shard_map/ppermute | solution.py:177
  102.7 11.1 %all-to-all-done.1.parts = bf16[8,24,1536]{2,1,0:T(8,128)(2,1)S(1)} async-done(((bf16[8,24,1536]{2,1,0:T(8,128)(2,1)}), bf16[8,24,1536]{2,1,0:T(8,128)(2,1)S(1)}, u32[]{:S(2)}, u32[]{:S(2)}) %all-to-all-start.1) | async-done | bytes 589856 | tf_op jit(solution)/shard_map/all_to_all | solution.py:269
  113.8 3.5 %all-to-all-start.3 = ((bf16[8,48,512]{2,1,0:T(8,128)(2,1)}), bf16[8,48,512]{2,1,0:T(8,128)(2,1)S(1)}, u32[]{:S(2)}, u32[]{:S(2)}) async-start(bf16[8,48,512]{2,1,0:T(8,128)(2,1)} %bitcast.8), calls=%async_computation.3 | async-start | bytes 786432 | tf_op jit(solution)/shard_map/all_to_all | solution.py:244
  117.3 0.9 shard_map.97
  118.2 14.2 %all-to-all-done.3.parts = bf16[8,48,512]{2,1,0:T(8,128)(2,1)S(1)} async-done(((bf16[8,48,512]{2,1,0:T(8,128)(2,1)}), bf16[8,48,512]{2,1,0:T(8,128)(2,1)S(1)}, u32[]{:S(2)}, u32[]{:S(2)}) %all-to-all-start.3) | async-done | bytes 393248 | tf_op jit(solution)/shard_map/all_to_all | solution.py:244
  132.3 3.5 %all-to-all-start.2 = ((bf16[8,24,1536]{2,1,0:T(8,128)(2,1)}), bf16[8,24,1536]{2,1,0:T(8,128)(2,1)S(1)}, u32[]{:S(2)}, u32[]{:S(2)}) async-start(bf16[8,24,1536]{2,1,0:T(8,128)(2,1)} %shard_map.97), calls=%async_computation.2 | async-start | bytes 1179648 | tf_op jit(solution)/shard_map/all_to_all | solution.py:274
  135.9 0.1 shard_map.98.first
  135.9 2.2 %collective-permute-start.9 = (bf16[48,512]{1,0:T(8,128)(2,1)S(1)}, bf16[48,512]{1,0:T(8,128)(2,1)S(1)}, u32[]{:S(2)}, u32[]{:S(2)}) collective-permute-start(bf16[48,512]{1,0:T(8,128)(2,1)S(1)} %shard_map.98.first), channel_id=1, source_target_pairs={{0,1},{1,0},{2,3},{3,2},{4,5},{5,4},{6,7},{7,6},{8,9},{9,8},{10,11... | collective-permute-start | bytes 147464 | tf_op jit(solution)/shard_map/ppermute | solution.py:177
  138.1 2.9 %collective-permute-done.9.second = bf16[48,512]{1,0:T(8,128)(2,1)S(1)} collective-permute-done((bf16[48,512]{1,0:T(8,128)(2,1)S(1)}, bf16[48,512]{1,0:T(8,128)(2,1)S(1)}, u32[]{:S(2)}, u32[]{:S(2)}) %collective-permute-start.9) | collective-permute-done | bytes 49184 | tf_op jit(solution)/shard_map/ppermute | solution.py:177
  141.1 0.8 shard_map.99
  141.9 13.3 %all-to-all-done.2 = bf16[8,24,1536]{2,1,0:T(8,128)(2,1)S(1)} async-done(((bf16[8,24,1536]{2,1,0:T(8,128)(2,1)}), bf16[8,24,1536]{2,1,0:T(8,128)(2,1)S(1)}, u32[]{:S(2)}, u32[]{:S(2)}) %all-to-all-start.2) | async-done | bytes 589856 | tf_op jit(solution)/shard_map/all_to_all | solution.py:274
  155.2 3.5 %all-to-all-start.4 = ((bf16[8,48,512]{2,1,0:T(8,128)(2,1)}), bf16[8,48,512]{2,1,0:T(8,128)(2,1)S(1)}, u32[]{:S(2)}, u32[]{:S(2)}) async-start(bf16[8,48,512]{2,1,0:T(8,128)(2,1)} %shard_map.99), calls=%async_computation.4 | async-start | bytes 786432 | tf_op jit(solution)/shard_map/all_to_all | solution.py:276
  158.6 2.2 %collective-permute-start.8 = (bf16[192,1536]{1,0:T(8,128)(2,1)S(1)}, bf16[192,1536]{1,0:T(8,128)(2,1)S(1)}, u32[]{:S(2)}, u32[]{:S(2)}) collective-permute-start(bf16[192,1536]{1,0:T(8,128)(2,1)S(1)} %bitcast.10), channel_id=1, source_target_pairs={{0,1},{1,0},{2,3},{3,2},{4,5},{5,4},{6,7},{7,6},{8,9},{9,8},{10,11... | collective-permute-start | bytes 1769480 | tf_op jit(solution)/shard_map/ppermute | solution.py:177
  160.8 0.0 collective-permute-done.10.second
  160.9 1.9 shard_map.102
  162.8 0.0 copy-start.6
  162.8 0.0 copy-start.7
  162.8 2.5 %collective-permute-start.11 = (bf16[4,64,896]{2,1,0:T(8,128)(2,1)S(1)}, bf16[4,64,896]{2,1,0:T(8,128)(2,1)S(1)}, u32[]{:S(2)}, u32[]{:S(2)}) collective-permute-start(bf16[4,64,896]{2,1,0:T(8,128)(2,1)S(1)} %get-tuple-element.33), channel_id=1, source_target_pairs={{0,32},{32,64},{64,96},{96,0},{1,33},{33,65},{65,97},{97,1},{2,34}... | collective-permute-start | bytes 1376264 | tf_op jit(solution)/shard_map/ppermute | solution.py:181
  165.3 1.9 collective-permute-start.12
  167.2 2.8 %collective-permute-start.13 = (bf16[4,64,896]{2,1,0:T(8,128)(2,1)S(1)}, bf16[4,64,896]{2,1,0:T(8,128)(2,1)S(1)}, u32[]{:S(2)}, u32[]{:S(2)}) collective-permute-start(bf16[4,64,896]{2,1,0:T(8,128)(2,1)S(1)} %get-tuple-element.35), channel_id=1, source_target_pairs={{0,96},{32,0},{64,32},{96,64},{1,97},{33,1},{65,33},{97,65},{2,98}... | collective-permute-start | bytes 1376264 | tf_op jit(solution)/shard_map/ppermute | solution.py:181
  170.0 6.0 %collective-permute-done.11.refs_1_ = bf16[4,64,896]{2,1,0:T(8,128)(2,1)S(1)} collective-permute-done((bf16[4,64,896]{2,1,0:T(8,128)(2,1)S(1)}, bf16[4,64,896]{2,1,0:T(8,128)(2,1)S(1)}, u32[]{:S(2)}, u32[]{:S(2)}) %collective-permute-start.11) | collective-permute-done | bytes 458784 | tf_op jit(solution)/shard_map/ppermute | solution.py:181
  176.0 3.8 %collective-permute-done.12.refs_2_ = bf16[4,64,896]{2,1,0:T(8,128)(2,1)S(1)} collective-permute-done((bf16[4,64,896]{2,1,0:T(8,128)(2,1)S(1)}, bf16[4,64,896]{2,1,0:T(8,128)(2,1)S(1)}, u32[]{:S(2)}, u32[]{:S(2)}) %collective-permute-start.12) | collective-permute-done | bytes 458784 | tf_op jit(solution)/shard_map/ppermute | solution.py:181
  179.8 11.2 %collective-permute-done.13.refs_3_ = bf16[4,64,896]{2,1,0:T(8,128)(2,1)S(1)} collective-permute-done((bf16[4,64,896]{2,1,0:T(8,128)(2,1)S(1)}, bf16[4,64,896]{2,1,0:T(8,128)(2,1)S(1)}, u32[]{:S(2)}, u32[]{:S(2)}) %collective-permute-start.13) | collective-permute-done | bytes 458784 | tf_op jit(solution)/shard_map/ppermute | solution.py:181
  191.0 0.2 shard_map.103
  191.2 2.2 %collective-permute-start.14 = (bf16[64,896]{1,0:T(8,128)(2,1)S(1)}, bf16[64,896]{1,0:T(8,128)(2,1)S(1)}, u32[]{:S(2)}, u32[]{:S(2)}) collective-permute-start(bf16[64,896]{1,0:T(8,128)(2,1)S(1)} %get-tuple-element.37), channel_id=1, source_target_pairs={{0,128},{128,256},{256,384},{384,0},{1,129},{129,257},{257,385},{3... | collective-permute-start | bytes 344072 | tf_op jit(solution)/shard_map/ppermute | solution.py:181
  193.4 4.4 %collective-permute-start.15 = (bf16[64,896]{1,0:T(8,128)(2,1)S(1)}, bf16[64,896]{1,0:T(8,128)(2,1)S(1)}, u32[]{:S(2)}, u32[]{:S(2)}) collective-permute-start(bf16[64,896]{1,0:T(8,128)(2,1)S(1)} %get-tuple-element.38), channel_id=1, source_target_pairs={{0,256},{128,384},{256,0},{384,128},{1,257},{129,385},{257,1},{385... | collective-permute-start | bytes 344072 | tf_op jit(solution)/shard_map/ppermute | solution.py:181
  197.8 2.1 collective-permute-start.16
  199.9 0.0 collective-permute-done.14.refs_1_
  199.9 3.4 %collective-permute-done.15.refs_2_ = bf16[64,896]{1,0:T(8,128)(2,1)S(1)} collective-permute-done((bf16[64,896]{1,0:T(8,128)(2,1)S(1)}, bf16[64,896]{1,0:T(8,128)(2,1)S(1)}, u32[]{:S(2)}, u32[]{:S(2)}) %collective-permute-start.15) | collective-permute-done | bytes 114720 | tf_op jit(solution)/shard_map/ppermute | solution.py:181
  203.4 9.2 %collective-permute-done.16.refs_3_ = bf16[64,896]{1,0:T(8,128)(2,1)S(1)} collective-permute-done((bf16[64,896]{1,0:T(8,128)(2,1)S(1)}, bf16[64,896]{1,0:T(8,128)(2,1)S(1)}, u32[]{:S(2)}, u32[]{:S(2)}) %collective-permute-start.16) | collective-permute-done | bytes 114720 | tf_op jit(solution)/shard_map/ppermute | solution.py:181
  212.6 1.4 shard_map.104
  213.9 0.0 collective-permute-done.8.other
  214.0 1.8 shard_map.100
  (8 shorter events, 0.0 us)
Async XLA Ops:
  23.4 24.4 %collective-permute-start.2 = (bf16[4,64,896]{2,1,0:T(8,128)(2,1)S(1)}, bf16[4,64,896]{2,1,0:T(8,128)(2,1)S(1)}, u32[]{:S(2)}, u32[]{:S(2)}) collective-permute-start(bf16[4,64,896]{2,1,0:T(8,128)(2,1)S(1)} %all_to_all.25.rest_0_), channel_id=1, source_target_pairs={{0,96},{32,0},{64,32},{96,64},{1,97},{33,1},{65,33},{97,65},{2,98}... | collective-permute-start | bytes 1376264 | tf_op jit(solution)/shard_map/ppermute | solution.py:181
  25.9 25.3 %collective-permute-start.1 = (bf16[4,64,896]{2,1,0:T(8,128)(2,1)S(1)}, bf16[4,64,896]{2,1,0:T(8,128)(2,1)S(1)}, u32[]{:S(2)}, u32[]{:S(2)}) collective-permute-start(bf16[4,64,896]{2,1,0:T(8,128)(2,1)S(1)} %all_to_all.25.rest_0_), channel_id=1, source_target_pairs={{0,64},{32,96},{64,0},{96,32},{1,65},{33,97},{65,1},{97,33},{2,66}... | collective-permute-start | bytes 1376264 | tf_op jit(solution)/shard_map/ppermute | solution.py:181
  28.5 24.6 %collective-permute-start = (bf16[4,64,896]{2,1,0:T(8,128)(2,1)S(1)}, bf16[4,64,896]{2,1,0:T(8,128)(2,1)}, u32[]{:S(2)}, u32[]{:S(2)}) collective-permute-start(bf16[4,64,896]{2,1,0:T(8,128)(2,1)S(1)} %all_to_all.25.rest_0_), channel_id=1, source_target_pairs={{0,32},{32,64},{64,96},{96,0},{1,33},{33,65},{65,97},{97,1},{2,34}... | collective-permute-start | bytes 1376264 | tf_op jit(solution)/shard_map/ppermute | solution.py:181
  32.4 25.9 %collective-permute-start.3 = (bf16[4,64,896]{2,1,0:T(8,128)(2,1)S(1)}, bf16[4,64,896]{2,1,0:T(8,128)(2,1)}, u32[]{:S(2)}, u32[]{:S(2)}) collective-permute-start(bf16[4,64,896]{2,1,0:T(8,128)(2,1)S(1)} %all_to_all.25.rest_0_), channel_id=1, source_target_pairs={{0,16},{16,0},{1,17},{17,1},{2,18},{18,2},{3,19},{19,3},{4,20},{20... | collective-permute-start | bytes 1376264 | tf_op jit(solution)/shard_map/ppermute | solution.py:177
  47.8 10.5 %collective-permute-start.6 = (bf16[4,64,896]{2,1,0:T(8,128)(2,1)S(1)}, bf16[4,64,896]{2,1,0:T(8,128)(2,1)}, u32[]{:S(2)}, u32[]{:S(2)}) collective-permute-start(bf16[4,64,896]{2,1,0:T(8,128)(2,1)S(1)} %collective-permute-done.2.rest_3_), channel_id=1, source_target_pairs={{0,16},{16,0},{1,17},{17,1},{2,18},{18,2},{3,19},{19,3},{4,20},{20... | collective-permute-start | bytes 1376264 | tf_op jit(solution)/shard_map/ppermute | solution.py:177
  51.2 7.1 %copy-start.3 = (bf16[4,64,896]{2,1,0:T(8,128)(2,1)}, bf16[4,64,896]{2,1,0:T(8,128)(2,1)S(1)}, u32[]{:S(2)}) copy-start(bf16[4,64,896]{2,1,0:T(8,128)(2,1)S(1)} %collective-permute-done.1.rest_2_) | copy-start | bytes 1376260
  51.2 7.1 %collective-permute-start.5 = (bf16[4,64,896]{2,1,0:T(8,128)(2,1)S(1)}, bf16[4,64,896]{2,1,0:T(8,128)(2,1)}, u32[]{:S(2)}, u32[]{:S(2)}) collective-permute-start(bf16[4,64,896]{2,1,0:T(8,128)(2,1)S(1)} %collective-permute-done.1.rest_2_), channel_id=1, source_target_pairs={{0,16},{16,0},{1,17},{17,1},{2,18},{18,2},{3,19},{19,3},{4,20},{20... | collective-permute-start | bytes 1376264 | tf_op jit(solution)/shard_map/ppermute | solution.py:177
  53.2 5.2 %collective-permute-start.4 = (bf16[4,64,896]{2,1,0:T(8,128)(2,1)}, bf16[4,64,896]{2,1,0:T(8,128)(2,1)}, u32[]{:S(2)}, u32[]{:S(2)}) collective-permute-start(bf16[4,64,896]{2,1,0:T(8,128)(2,1)} %collective-permute-done.rest_1_), channel_id=1, source_target_pairs={{0,16},{16,0},{1,17},{17,1},{2,18},{18,2},{3,19},{19,3},{4,20},{20... | collective-permute-start | bytes 1376264 | tf_op jit(solution)/shard_map/ppermute | solution.py:177
  55.6 1.4 copy-start.2
  57.0 1.0 copy-start.5
  58.4 1.0 copy-start.4
  66.7 16.7 %collective-permute-start.7 = (bf16[192,1536]{1,0:T(8,128)(2,1)S(1)}, bf16[192,1536]{1,0:T(8,128)(2,1)S(1)}, u32[]{:S(2)}, u32[]{:S(2)}) collective-permute-start(bf16[192,1536]{1,0:T(8,128)(2,1)S(1)} %get-tuple-element.27), channel_id=1, source_target_pairs={{0,1},{1,0},{2,3},{3,2},{4,5},{5,4},{6,7},{7,6},{8,9},{9,8},{10,11... | collective-permute-start | bytes 1769480 | tf_op jit(solution)/shard_map/ppermute | solution.py:177
  84.3 29.4 %all-to-all-start.1 = ((bf16[8,24,1536]{2,1,0:T(8,128)(2,1)}), bf16[8,24,1536]{2,1,0:T(8,128)(2,1)S(1)}, u32[]{:S(2)}, u32[]{:S(2)}) async-start(bf16[8,24,1536]{2,1,0:T(8,128)(2,1)} %bitcast.6), calls=%async_computation.1 | async-start | bytes 1179648 | tf_op jit(solution)/shard_map/all_to_all | solution.py:269
  98.5 1.2 copy-start
  99.7 61.1 %collective-permute-start.10 = (bf16[4,4,64,896]{3,2,1,0:T(8,128)(2,1)}, bf16[4,4,64,896]{3,2,1,0:T(8,128)(2,1)}, u32[]{:S(2)}, u32[]{:S(2)}) collective-permute-start(bf16[4,4,64,896]{3,2,1,0:T(8,128)(2,1)} %get-tuple-element.31), channel_id=1, source_target_pairs={{0,16},{16,0},{1,17},{17,1},{2,18},{18,2},{3,19},{19,3},{4,20},{20... | collective-permute-start | bytes 5505032 | tf_op jit(solution)/shard_map/ppermute | solution.py:177
  113.8 18.5 %all-to-all-start.3 = ((bf16[8,48,512]{2,1,0:T(8,128)(2,1)}), bf16[8,48,512]{2,1,0:T(8,128)(2,1)S(1)}, u32[]{:S(2)}, u32[]{:S(2)}) async-start(bf16[8,48,512]{2,1,0:T(8,128)(2,1)} %bitcast.8), calls=%async_computation.3 | async-start | bytes 786432 | tf_op jit(solution)/shard_map/all_to_all | solution.py:244
  118.1 42.7 %copy-start.1 = (bf16[4,4,64,896]{3,2,1,0:T(8,128)(2,1)S(1)}, bf16[4,4,64,896]{3,2,1,0:T(8,128)(2,1)}, u32[]{:S(2)}) copy-start(bf16[4,4,64,896]{3,2,1,0:T(8,128)(2,1)} %copy-done) | copy-start | bytes 5505028
  132.3 22.9 %all-to-all-start.2 = ((bf16[8,24,1536]{2,1,0:T(8,128)(2,1)}), bf16[8,24,1536]{2,1,0:T(8,128)(2,1)S(1)}, u32[]{:S(2)}, u32[]{:S(2)}) async-start(bf16[8,24,1536]{2,1,0:T(8,128)(2,1)} %shard_map.97), calls=%async_computation.2 | async-start | bytes 1179648 | tf_op jit(solution)/shard_map/all_to_all | solution.py:274
  135.9 5.1 %collective-permute-start.9 = (bf16[48,512]{1,0:T(8,128)(2,1)S(1)}, bf16[48,512]{1,0:T(8,128)(2,1)S(1)}, u32[]{:S(2)}, u32[]{:S(2)}) collective-permute-start(bf16[48,512]{1,0:T(8,128)(2,1)S(1)} %shard_map.98.first), channel_id=1, source_target_pairs={{0,1},{1,0},{2,3},{3,2},{4,5},{5,4},{6,7},{7,6},{8,9},{9,8},{10,11... | collective-permute-start | bytes 147464 | tf_op jit(solution)/shard_map/ppermute | solution.py:177
  155.2 58.8 %all-to-all-start.4 = ((bf16[8,48,512]{2,1,0:T(8,128)(2,1)}), bf16[8,48,512]{2,1,0:T(8,128)(2,1)S(1)}, u32[]{:S(2)}, u32[]{:S(2)}) async-start(bf16[8,48,512]{2,1,0:T(8,128)(2,1)} %shard_map.99), calls=%async_computation.4 | async-start | bytes 786432 | tf_op jit(solution)/shard_map/all_to_all | solution.py:276
  158.6 55.3 %collective-permute-start.8 = (bf16[192,1536]{1,0:T(8,128)(2,1)S(1)}, bf16[192,1536]{1,0:T(8,128)(2,1)S(1)}, u32[]{:S(2)}, u32[]{:S(2)}) collective-permute-start(bf16[192,1536]{1,0:T(8,128)(2,1)S(1)} %bitcast.10), channel_id=1, source_target_pairs={{0,1},{1,0},{2,3},{3,2},{4,5},{5,4},{6,7},{7,6},{8,9},{9,8},{10,11... | collective-permute-start | bytes 1769480 | tf_op jit(solution)/shard_map/ppermute | solution.py:177
  162.8 49.8 %copy-start.6 = (s32[1,7]{1,0:T(1,128)S(1)}, s32[1,7]{1,0:T(1,128)}, u32[]{:S(2)}) copy-start(s32[1,7]{1,0:T(1,128)} %gm.1) | copy-start | bytes 88
  162.8 49.8 %copy-start.7 = (s32[1,7]{1,0:T(1,128)S(1)}, s32[1,7]{1,0:T(1,128)}, u32[]{:S(2)}) copy-start(s32[1,7]{1,0:T(1,128)} %um.1) | copy-start | bytes 88
  162.8 13.2 %collective-permute-start.11 = (bf16[4,64,896]{2,1,0:T(8,128)(2,1)S(1)}, bf16[4,64,896]{2,1,0:T(8,128)(2,1)S(1)}, u32[]{:S(2)}, u32[]{:S(2)}) collective-permute-start(bf16[4,64,896]{2,1,0:T(8,128)(2,1)S(1)} %get-tuple-element.33), channel_id=1, source_target_pairs={{0,32},{32,64},{64,96},{96,0},{1,33},{33,65},{65,97},{97,1},{2,34}... | collective-permute-start | bytes 1376264 | tf_op jit(solution)/shard_map/ppermute | solution.py:181
  165.3 14.5 %collective-permute-start.12 = (bf16[4,64,896]{2,1,0:T(8,128)(2,1)S(1)}, bf16[4,64,896]{2,1,0:T(8,128)(2,1)S(1)}, u32[]{:S(2)}, u32[]{:S(2)}) collective-permute-start(bf16[4,64,896]{2,1,0:T(8,128)(2,1)S(1)} %get-tuple-element.34), channel_id=1, source_target_pairs={{0,64},{32,96},{64,0},{96,32},{1,65},{33,97},{65,1},{97,33},{2,66}... | collective-permute-start | bytes 1376264 | tf_op jit(solution)/shard_map/ppermute | solution.py:181
  167.2 23.7 %collective-permute-start.13 = (bf16[4,64,896]{2,1,0:T(8,128)(2,1)S(1)}, bf16[4,64,896]{2,1,0:T(8,128)(2,1)S(1)}, u32[]{:S(2)}, u32[]{:S(2)}) collective-permute-start(bf16[4,64,896]{2,1,0:T(8,128)(2,1)S(1)} %get-tuple-element.35), channel_id=1, source_target_pairs={{0,96},{32,0},{64,32},{96,64},{1,97},{33,1},{65,33},{97,65},{2,98}... | collective-permute-start | bytes 1376264 | tf_op jit(solution)/shard_map/ppermute | solution.py:181
  191.2 8.7 %collective-permute-start.14 = (bf16[64,896]{1,0:T(8,128)(2,1)S(1)}, bf16[64,896]{1,0:T(8,128)(2,1)S(1)}, u32[]{:S(2)}, u32[]{:S(2)}) collective-permute-start(bf16[64,896]{1,0:T(8,128)(2,1)S(1)} %get-tuple-element.37), channel_id=1, source_target_pairs={{0,128},{128,256},{256,384},{384,0},{1,129},{129,257},{257,385},{3... | collective-permute-start | bytes 344072 | tf_op jit(solution)/shard_map/ppermute | solution.py:181
  193.4 9.9 %collective-permute-start.15 = (bf16[64,896]{1,0:T(8,128)(2,1)S(1)}, bf16[64,896]{1,0:T(8,128)(2,1)S(1)}, u32[]{:S(2)}, u32[]{:S(2)}) collective-permute-start(bf16[64,896]{1,0:T(8,128)(2,1)S(1)} %get-tuple-element.38), channel_id=1, source_target_pairs={{0,256},{128,384},{256,0},{384,128},{1,257},{129,385},{257,1},{385... | collective-permute-start | bytes 344072 | tf_op jit(solution)/shard_map/ppermute | solution.py:181
  197.8 14.7 %collective-permute-start.16 = (bf16[64,896]{1,0:T(8,128)(2,1)S(1)}, bf16[64,896]{1,0:T(8,128)(2,1)S(1)}, u32[]{:S(2)}, u32[]{:S(2)}) collective-permute-start(bf16[64,896]{1,0:T(8,128)(2,1)S(1)} %get-tuple-element.39), channel_id=1, source_target_pairs={{0,384},{128,0},{256,128},{384,256},{1,385},{129,1},{257,129},{385... | collective-permute-start | bytes 344072 | tf_op jit(solution)/shard_map/ppermute | solution.py:181

commit v5 on v4

--- a/solution.py
+++ b/solution.py
@@ -52,7 +52,7 @@
 
 def forward_kernel(place, tokens, grad_ref, *rest):
     mine, other = rest[:X], rest[X : 2 * X]
-    hidden_t, d_both, send, keep, side, w = rest[2 * X :]
+    hidden_t, d_both, send, w = rest[2 * X :]
     core, half, own_x = place[0], place[1], place[2]
     width = grad_ref.shape[1]
     for yh in range(YH):
@@ -74,10 +74,8 @@
     d_up = grad * activation
     d_both[...] = jnp.concatenate([d_gate, d_up], axis=1).astype(BF16)
     rows = send.shape[0]
-    for out, index in ((send, 1 - half), (keep, half)):
-        start = pl.multiple_of(index * rows, rows)
-        out[...] = to_tokens(d_both[pl.ds(start, rows), :], weights[:FIRST])
-    side[...] = to_tokens(d_both[...], weights[FIRST:])
+    start = pl.multiple_of((1 - half) * rows, rows)
+    send[...] = to_tokens(d_both[pl.ds(start, rows), :], weights[:FIRST])
 
 
 def to_tokens(grad, weights):
@@ -86,8 +84,12 @@
     ).astype(BF16)
 
 
-def weight_kernel(place, tokens, d_both, keep, send):
-    core, own_x, own_yh = place[0], place[2], place[3]
+def weight_kernel(place, tokens, d_both, weights, keep, send, main, side):
+    part = main.shape[0]
+    start = pl.multiple_of(place[1] * part, part)
+    side[...] = to_tokens(d_both[...], weights[FIRST:, :])
+    main[...] = to_tokens(d_both[pl.ds(start, part), :], weights[:FIRST, :])
+    core, own_x = place[0], place[2]
     rows = CORE * BLOCK * 2
     for step in range(YH * X // 2):
         both = lax.dot_general(
@@ -98,7 +100,7 @@
         ).astype(BF16)
         for pair in range(2):
             yh, x = divmod(step * 2 + pair, X)
-            ahead = lax.rem(x + X - own_x, X), lax.rem(yh + YH - own_yh, YH)
+            ahead = lax.rem(x + X - own_x, X), yh
             low = both[pair * 128 : pair * 128 + 64]
             high = both[pair * 128 + 64 : pair * 128 + 128]
             first = core == 0
@@ -106,28 +108,26 @@
             send[ahead] = jnp.where(first, high, low)
 
 
-def final_kernel(gm, um, *refs):
-    parts, (grad_gate, grad_up) = refs[:-2], refs[-2:]
+def final_kernel(gm, um, parts, grad_gate, grad_up):
     width = grad_gate.shape[1]
+    total = parts[0].astype(F32)
+    for source in range(1, YH):
+        total = total + parts[source].astype(F32)
+    grad_gate[...] = total[:, :width] * keep_row(gm, width)
+    grad_up[...] = total[:, width:] * keep_row(um, width)
+
+
+def pair_kernel(first, second, *outs):
+    for index, out in enumerate(outs):
+        out[...] = (first[index].astype(F32) + second[index].astype(F32)).astype(BF16)
+
+
+def x_sum_kernel(*refs):
+    parts, out = refs[:-1], refs[-1]
     total = parts[0][...].astype(F32)
     for part in parts[1:]:
         total = total + part[...].astype(F32)
-    grad_gate[...] = total[:, :width] * keep_row(gm, width)
-    grad_up[...] = total[:, width:] * keep_row(um, width)
-
-
-def pair_kernel(first, second, *outs):
-    for index, out in enumerate(outs):
-        out[...] = (first[index].astype(F32) + second[index].astype(F32)).astype(BF16)
-
-
-def rows_kernel(*refs):
-    parts, outs = refs[:X], refs[X:]
-    for index, out in enumerate(outs):
-        total = parts[0][index].astype(F32)
-        for part in parts[1:]:
-            total = total + part[index].astype(F32)
-        out[...] = total.astype(BF16)
+    out[...] = total.astype(BF16)
 
 
 def add_kernel(first, second, out):
@@ -141,28 +141,32 @@
     return total.astype(BF16)
 
 
-def sum_kernel(parts, out):
-    out[...] = total_of(parts)
-
-
-def sum_copies_kernel(parts, out):
+def side_kernel(place, parts, keep, send):
+    half = place[1]
+    rows = keep.shape[0]
     total = total_of(parts)
+    low, high = total[:rows], total[rows:]
+    keep[...] = jnp.where(half == 0, low, high)
+    send[...] = jnp.where(half == 0, high, low)
+
+
+def main_kernel(parts, side, side_other, out):
+    total = total_of(parts)
+    rest = (side[...].astype(F32) + side_other[...].astype(F32)).astype(BF16)
     for copy in range(out.shape[0]):
-        out[copy] = total
-
-
-def add_copies_kernel(first, second, out):
-    total = (first[...].astype(F32) + second[...].astype(F32)).astype(BF16)
-    for copy in range(out.shape[0]):
-        out[copy] = total
-
-
-def join_kernel(place, mine, other, side, out):
+        out[copy, :, :FIRST] = total
+        out[copy, :, FIRST:] = rest
+
+
+def join_kernel(place, mine, other, out):
     half = place[1]
-    rows = mine.shape[0]
-    out[pl.ds(pl.multiple_of(half * rows, rows), rows), :FIRST] = mine[...]
-    out[pl.ds(pl.multiple_of((1 - half) * rows, rows), rows), :FIRST] = other[...]
-    out[:, FIRST:] = side[...]
+    chunk = mine.shape[1]
+    for part, index in ((mine, half), (other, 1 - half)):
+        for z in range(Z):
+            start = pl.multiple_of((index * Z + z) * chunk, chunk)
+            out[pl.ds(start, chunk), :FIRST] = part[z, :, :FIRST]
+            start = pl.multiple_of((z * YL + index) * chunk, chunk)
+            out[pl.ds(start, chunk), FIRST:] = part[z, :, FIRST:]
 
 
 def shape(dims, dtype=BF16):
@@ -200,7 +204,7 @@
     half = count // YL
     chunk = half // Z
     rest = features - FIRST
-    place = jnp.stack([lax.axis_index(name) for name in ("core", "yl", "x", "yh")])
+    place = jnp.stack([lax.axis_index(name) for name in ("core", "yl", "x")])
     copies = pl.pallas_call(
         mask_kernel,
         in_specs=[HB] * 4,
@@ -223,14 +227,13 @@
     tokens, grad = call(
         prepare_kernel, [shape(tokens.shape), shape((count, width), F32)], tokens, out_grad.T
     )
-    hidden_t, d_both, send, keep, side = call(
+    hidden_t, d_both, send, weights = call(
         forward_kernel,
         [
             shape((width, count), F32),
             shape((count, 2 * width)),
             shape((half, FIRST)),
-            shape((half, FIRST)),
-            shape((count, rest)),
+            shape((features, 2 * width)),
         ],
         place,
         tokens,
@@ -238,44 +241,43 @@
         *mine,
         *other,
         scalars=1,
-        scratch=[pltpu.VMEM((features, 2 * width), BF16)],
     )
     received = swap(send, "yl")
-    side = lax.all_to_all(side.reshape(Z, 2 * chunk, rest), "z", 0, 0, tiled=True)
-    w_keep, w_send = call(
+    w_keep, w_send, keep, side = call(
         weight_kernel,
-        [shape((X, YH, BLOCK, 2 * width))] * 2,
+        [shape((X, YH, BLOCK, 2 * width))] * 2 + [shape((half, FIRST)), shape((count, rest))],
         place,
         tokens,
         d_both,
+        weights,
         scalars=1,
     )
+    side = lax.all_to_all(side.reshape(Z, 2 * chunk, rest), "z", 0, 0, tiled=True)
     w_received = swap(w_send, "core")
     w_parts = call(pair_kernel, [shape((YH, BLOCK, 2 * width))] * X, w_keep, w_received)
     for steps in range(1, X):
         w_parts[steps] = shift(w_parts[steps], "x", X, steps)
-    w_parts = call(rows_kernel, [shape((BLOCK, 2 * width))] * YH, *w_parts)
-    for steps in range(1, YH):
-        w_parts[steps] = shift(w_parts[steps], "yh", YH, steps)
+    w_sum = call(x_sum_kernel, shape((YH, BLOCK, 2 * width)), *w_parts)
+    w_parts = lax.all_to_all(w_sum, "yh", 0, 0, tiled=True)
     grad_gate, grad_up = call(
         final_kernel,
         [shape((BLOCK, width), F32)] * 2,
         gate_mask,
         up_mask,
-        *w_parts,
+        w_parts,
         scalars=2,
     )
     main = call(add_kernel, shape((half, FIRST)), keep, received)
     main = lax.all_to_all(main.reshape(Z, chunk, FIRST), "z", 0, 0, tiled=True)
-    side = call(sum_kernel, shape((2 * chunk, rest)), side)
-    side_other = swap(side, "yl")
-    side = call(add_copies_kernel, shape((Z, 2 * chunk, rest)), side, side_other)
-    main = call(sum_copies_kernel, shape((Z, chunk, FIRST)), main)
-    main = lax.all_to_all(main, "z", 0, 0, tiled=True).reshape(half, FIRST)
+    side, side_send = call(
+        side_kernel, [shape((chunk, rest))] * 2, place, side, scalars=1
+    )
+    side_other = swap(side_send, "yl")
+    main = call(main_kernel, shape((Z, chunk, features)), main, side, side_other)
+    main = lax.all_to_all(main, "z", 0, 0, tiled=True)
     main_other = swap(main, "yl")
-    side = lax.all_to_all(side, "z", 0, 0, tiled=True).reshape(count, rest)
     grad_tokens = call(
-        join_kernel, shape((count, features)), place, main, main_other, side, scalars=1
+        join_kernel, shape((count, features)), place, main, main_other, scalars=1
     )
     return (hidden_t.T, grad_tokens, grad_gate, grad_up)
 

time: 217 us -> 186 us (0.86)
  the two profiles are of different devices: /device:TPU:23 before, /device:TPU:48 now
where the time goes in v5:
time: 186 us; the launch traced here: 185 us
  starting transfers between devices  57.9 us (31%)
  waiting for transfers between devices  55.3 us (30%)
  blocking collectives  46.3 us (25%)
  Pallas kernels  20.5 us (11%)
  local copies, waits for them, and re-layouts  4.43 us (2%)
    all_to_all x1, blocking collectives, compute(): w_parts = lax.all_to_all(w_sum, 'yh', 0, 0, tiled=True)  27.6 us
    ppermute x6, starting transfers between devices, shift(): lax.ppermute(array, axis, [(i, (i + steps) % size) for i in range(size)])  19.9 us
    ppermute x8, waiting for transfers between devices, swap(): return lax.ppermute(array, axis, [(0, 1), (1, 0)])  18.9 us
    all_to_all x1, blocking collectives, compute(): rows = lax.all_to_all(copies, 'yh', 0, 0, tiled=True)  18.7 us
    pallas_call x10, Pallas kernels, call(): pl.pallas_call(kernel, in_specs=[SM] * scalars + [VM] * (len(operands) -...  18.7 us
    ppermute x8, starting transfers between devices, swap(): return lax.ppermute(array, axis, [(0, 1), (1, 0)])  17.2 us
    ppermute x6, waiting for transfers between devices, shift(): lax.ppermute(array, axis, [(i, (i + steps) % size) for i in range(size)])  17 us
    all_to_all x1, starting transfers between devices, compute(): lax.all_to_all(side.reshape(Z, 2 * chunk, rest), 'z', 0, 0, tiled=True)  10.3 us
  transfers between devices with their start and end apart: 17, of which 8 were waited for; matrix products, arithmetic and copies ran while one was open for 0% of the time, Pallas kernels for 4%

profile of v5, /device:TPU:48, one launch (start us, length us, event | category | flops | bytes accessed | tf_op | source)
XLA Modules:
  0.0 185.3 jit_solution(12172900336572667144)
XLA Ops:
  0.6 1.8 shard_map.94
  2.4 18.7 %all_to_all.25.rest_0_ = bf16[4,64,896]{2,1,0:T(8,128)(2,1)S(1)} all-to-all(bf16[4,64,896]{2,1,0:T(8,128)(2,1)} %shard_map.94), channel_id=1, replica_groups=mesh['yh'=4,'x'=4,'core'=2,'z'=8,'yl'=2] {'yh'}, dimensions={0} | all-to-all | bytes 917504 | tf_op jit(solution)/shard_map/all_to_all | solution.py:221
  21.2 4.7 %collective-permute-start.2 = (bf16[4,64,896]{2,1,0:T(8,128)(2,1)S(1)}, bf16[4,64,896]{2,1,0:T(8,128)(2,1)S(1)}, u32[]{:S(2)}, u32[]{:S(2)}) collective-permute-start(bf16[4,64,896]{2,1,0:T(8,128)(2,1)S(1)} %all_to_all.25.rest_0_), channel_id=1, source_target_pairs={{0,96},{32,0},{64,32},{96,64},{1,97},{33,1},{65,33},{97,65},{2,98}... | collective-permute-start | bytes 1376264 | tf_op jit(solution)/shard_map/ppermute | solution.py:185
  25.8 2.7 %collective-permute-start.1 = (bf16[4,64,896]{2,1,0:T(8,128)(2,1)S(1)}, bf16[4,64,896]{2,1,0:T(8,128)(2,1)S(1)}, u32[]{:S(2)}, u32[]{:S(2)}) collective-permute-start(bf16[4,64,896]{2,1,0:T(8,128)(2,1)S(1)} %all_to_all.25.rest_0_), channel_id=1, source_target_pairs={{0,64},{32,96},{64,0},{96,32},{1,65},{33,97},{65,1},{97,33},{2,66}... | collective-permute-start | bytes 1376264 | tf_op jit(solution)/shard_map/ppermute | solution.py:185
  28.5 2.8 %collective-permute-start = (bf16[4,64,896]{2,1,0:T(8,128)(2,1)S(1)}, bf16[4,64,896]{2,1,0:T(8,128)(2,1)S(1)}, u32[]{:S(2)}, u32[]{:S(2)}) collective-permute-start(bf16[4,64,896]{2,1,0:T(8,128)(2,1)S(1)} %all_to_all.25.rest_0_), channel_id=1, source_target_pairs={{0,32},{32,64},{64,96},{96,0},{1,33},{33,65},{65,97},{97,1},{2,34}... | collective-permute-start | bytes 1376264 | tf_op jit(solution)/shard_map/ppermute | solution.py:185
  31.3 1.9 %collective-permute-start.3 = (bf16[4,64,896]{2,1,0:T(8,128)(2,1)S(1)}, bf16[4,64,896]{2,1,0:T(8,128)(2,1)S(1)}, u32[]{:S(2)}, u32[]{:S(2)}) collective-permute-start(bf16[4,64,896]{2,1,0:T(8,128)(2,1)S(1)} %all_to_all.25.rest_0_), channel_id=1, source_target_pairs={{0,16},{16,0},{1,17},{17,1},{2,18},{18,2},{3,19},{19,3},{4,20},{20... | collective-permute-start | bytes 1376264 | tf_op jit(solution)/shard_map/ppermute | solution.py:181
  33.3 11.3 %collective-permute-done.2.rest_3_ = bf16[4,64,896]{2,1,0:T(8,128)(2,1)S(1)} collective-permute-done((bf16[4,64,896]{2,1,0:T(8,128)(2,1)S(1)}, bf16[4,64,896]{2,1,0:T(8,128)(2,1)S(1)}, u32[]{:S(2)}, u32[]{:S(2)}) %collective-permute-start.2) | collective-permute-done | bytes 458784 | tf_op jit(solution)/shard_map/ppermute | solution.py:185
  44.5 1.9 %collective-permute-start.6 = (bf16[4,64,896]{2,1,0:T(8,128)(2,1)S(1)}, bf16[4,64,896]{2,1,0:T(8,128)(2,1)S(1)}, u32[]{:S(2)}, u32[]{:S(2)}) collective-permute-start(bf16[4,64,896]{2,1,0:T(8,128)(2,1)S(1)} %collective-permute-done.2.rest_3_), channel_id=1, source_target_pairs={{0,16},{16,0},{1,17},{17,1},{2,18},{18,2},{3,19},{19,3},{4,20},{20... | collective-permute-start | bytes 1376264 | tf_op jit(solution)/shard_map/ppermute | solution.py:181
  46.5 0.0 collective-permute-done.1.rest_2_
  46.5 2.4 %collective-permute-start.5 = (bf16[4,64,896]{2,1,0:T(8,128)(2,1)S(1)}, bf16[4,64,896]{2,1,0:T(8,128)(2,1)S(1)}, u32[]{:S(2)}, u32[]{:S(2)}) collective-permute-start(bf16[4,64,896]{2,1,0:T(8,128)(2,1)S(1)} %collective-permute-done.1.rest_2_), channel_id=1, source_target_pairs={{0,16},{16,0},{1,17},{17,1},{2,18},{18,2},{3,19},{19,3},{4,20},{20... | collective-permute-start | bytes 1376264 | tf_op jit(solution)/shard_map/ppermute | solution.py:181
  48.9 1.3 collective-permute-done.rest_1_
  50.2 1.9 %collective-permute-start.4 = (bf16[4,64,896]{2,1,0:T(8,128)(2,1)S(1)}, bf16[4,64,896]{2,1,0:T(8,128)(2,1)}, u32[]{:S(2)}, u32[]{:S(2)}) collective-permute-start(bf16[4,64,896]{2,1,0:T(8,128)(2,1)S(1)} %collective-permute-done.rest_1_), channel_id=1, source_target_pairs={{0,16},{16,0},{1,17},{17,1},{2,18},{18,2},{3,19},{19,3},{4,20},{20... | collective-permute-start | bytes 1376264 | tf_op jit(solution)/shard_map/ppermute | solution.py:181
  52.1 0.0 copy-start
  52.1 1.4 copy-done
  53.5 0.0 copy-start.1
  53.5 1.0 copy-done.1
  54.5 0.2 shard_map.93
  54.7 0.1 pad_add_fusion.place
  54.8 0.0 collective-permute-done.3.rest_4_
  54.8 0.0 collective-permute-done.6.rest_7_
  54.8 0.0 collective-permute-done.5.rest_6_
  54.8 0.0 collective-permute-done.4.rest_5_
  54.8 5.2 %shard_map.95 = (f32[448,384]{1,0:T(8,128)}, bf16[384,896]{1,0:T(8,128)(2,1)S(1)}, bf16[192,1536]{1,0:T(8,128)(2,1)S(1)}, bf16[2048,896]{1,0:T(8,128)(2,1)S(1)}) custom-call(s32[3]{0:T(128)S(1)} %pad_add_fusion.place, bf16[384,2048]{1,0:T(8,128)(2,1)S(1)} %get-tuple-element.22.tokens, f32[384,448]{1,0:T(8,128)S(1)} %get-tuple-element.23.grad_ref, ...), custom_call_target="tpu_custom_call" | custom-call | tf_op jit(solution)/shard_map/pallas_call | solution.py:190
  60.0 0.0 copy-start.5
  60.0 0.8 copy-done.5
  60.8 0.0 copy-start.6
  60.8 4.6 %shard_map.96 = (bf16[4,4,64,896]{3,2,1,0:T(8,128)(2,1)S(1)}, bf16[4,4,64,896]{3,2,1,0:T(8,128)(2,1)S(1)}, bf16[192,1536]{1,0:T(8,128)(2,1)S(1)}, bf16[384,512]{1,0:T(8,128)(2,1)}) custom-call(s32[3]{0:T(128)S(1)} %pad_add_fusion.place, bf16[384,2048]{1,0:T(8,128)(2,1)S(1)} %get-tuple-element.22.tokens, bf16[384,896]{1,0:T(8,128)(2,1)S(1)} %get-tuple-element.25.d_both, ...), custom_call_target="tpu_custom_call" | custom-call | tf_op jit(solution)/shard_map/pallas_call | solution.py:190
  65.5 0.0 copy-start.4
  65.5 1.2 copy-done.4
  66.7 10.3 %all-to-all-start.2 = ((bf16[8,48,512]{2,1,0:T(8,128)(2,1)}), bf16[8,48,512]{2,1,0:T(8,128)(2,1)S(1)}, u32[]{:S(2)}, u32[]{:S(2)}) async-start(bf16[8,48,512]{2,1,0:T(8,128)(2,1)} %bitcast.6), calls=%async_computation.2 | async-start | bytes 786432 | tf_op jit(solution)/shard_map/all_to_all | solution.py:255
  77.0 0.0 copy-done.6
  77.0 1.9 %collective-permute-start.7 = (bf16[192,1536]{1,0:T(8,128)(2,1)S(1)}, bf16[192,1536]{1,0:T(8,128)(2,1)S(1)}, u32[]{:S(2)}, u32[]{:S(2)}) collective-permute-start(bf16[192,1536]{1,0:T(8,128)(2,1)S(1)} %copy-done.6), channel_id=1, source_target_pairs={{0,1},{1,0},{2,3},{3,2},{4,5},{5,4},{6,7},{7,6},{8,9},{9,8},{10,11... | collective-permute-start | bytes 1769480 | tf_op jit(solution)/shard_map/ppermute | solution.py:181
  78.9 15.4 %collective-permute-done.7.second = bf16[192,1536]{1,0:T(8,128)(2,1)S(1)} collective-permute-done((bf16[192,1536]{1,0:T(8,128)(2,1)S(1)}, bf16[192,1536]{1,0:T(8,128)(2,1)S(1)}, u32[]{:S(2)}, u32[]{:S(2)}) %collective-permute-start.7) | collective-permute-done | bytes 589856 | tf_op jit(solution)/shard_map/ppermute | solution.py:181
  94.3 0.9 shard_map.97
  95.3 0.0 all-to-all-done.2.parts
  95.3 6.9 %all-to-all-start.1 = ((bf16[8,24,1536]{2,1,0:T(8,128)(2,1)}), bf16[8,24,1536]{2,1,0:T(8,128)(2,1)S(1)}, u32[]{:S(2)}, u32[]{:S(2)}) async-start(bf16[8,24,1536]{2,1,0:T(8,128)(2,1)} %bitcast.5), calls=%async_computation.1 | async-start | bytes 1179648 | tf_op jit(solution)/shard_map/all_to_all | solution.py:271
  102.2 1.9 %collective-permute-start.10 = (bf16[4,4,64,896]{3,2,1,0:T(8,128)(2,1)}, bf16[4,4,64,896]{3,2,1,0:T(8,128)(2,1)}, u32[]{:S(2)}, u32[]{:S(2)}) collective-permute-start(bf16[4,4,64,896]{3,2,1,0:T(8,128)(2,1)} %copy-done.4), channel_id=1, source_target_pairs={{0,16},{16,0},{1,17},{17,1},{2,18},{18,2},{3,19},{19,3},{4,20},{20... | collective-permute-start | bytes 5505032 | tf_op jit(solution)/shard_map/ppermute | solution.py:181
  104.1 0.6 shard_map.98
  104.7 2.2 %collective-permute-start.8 = (bf16[24,512]{1,0:T(8,128)(2,1)S(1)}, bf16[24,512]{1,0:T(8,128)(2,1)S(1)}, u32[]{:S(2)}, u32[]{:S(2)}) collective-permute-start(bf16[24,512]{1,0:T(8,128)(2,1)S(1)} %get-tuple-element.31), channel_id=1, source_target_pairs={{0,1},{1,0},{2,3},{3,2},{4,5},{5,4},{6,7},{7,6},{8,9},{9,8},{10,11... | collective-permute-start | bytes 73736 | tf_op jit(solution)/shard_map/ppermute | solution.py:181
  106.9 3.5 %collective-permute-done.8.side_other = bf16[24,512]{1,0:T(8,128)(2,1)S(1)} collective-permute-done((bf16[24,512]{1,0:T(8,128)(2,1)S(1)}, bf16[24,512]{1,0:T(8,128)(2,1)S(1)}, u32[]{:S(2)}, u32[]{:S(2)}) %collective-permute-start.8) | collective-permute-done | bytes 24608 | tf_op jit(solution)/shard_map/ppermute | solution.py:181
  110.5 9.9 %all-to-all-done.1.parts = bf16[8,24,1536]{2,1,0:T(8,128)(2,1)S(1)} async-done(((bf16[8,24,1536]{2,1,0:T(8,128)(2,1)}), bf16[8,24,1536]{2,1,0:T(8,128)(2,1)S(1)}, u32[]{:S(2)}, u32[]{:S(2)}) %all-to-all-start.1) | async-done | bytes 589856 | tf_op jit(solution)/shard_map/all_to_all | solution.py:271
  120.4 1.0 shard_map.99
  121.3 3.5 %all-to-all-start.3 = ((bf16[8,24,2048]{2,1,0:T(8,128)(2,1)}), bf16[8,24,2048]{2,1,0:T(8,128)(2,1)S(1)}, u32[]{:S(2)}, u32[]{:S(2)}) async-start(bf16[8,24,2048]{2,1,0:T(8,128)(2,1)} %shard_map.99), calls=%async_computation.3 | async-start | bytes 1572864 | tf_op jit(solution)/shard_map/all_to_all | solution.py:277
  124.9 0.0 collective-permute-done.10.second
  124.9 2.7 %shard_map.101 = (bf16[4,64,896]{2,1,0:T(8,128)(2,1)S(1)}, bf16[4,64,896]{2,1,0:T(8,128)(2,1)}, bf16[4,64,896]{2,1,0:T(8,128)(2,1)}, bf16[4,64,896]{2,1,0:T(8,128)(2,1)}) custom-call(bf16[4,4,64,896]{3,2,1,0:T(8,128)(2,1)S(1)} %get-tuple-element.32.first, bf16[4,4,64,896]{3,2,1,0:T(8,128)(2,1)} %collective-permute-done.10.second), custom_call_target="tpu_custom_call" | custom-call | tf_op jit(solution)/shard_map/pallas_call | solution.py:190
  127.6 0.0 copy-start.2
  127.6 0.0 copy-start.3
  127.6 2.0 %collective-permute-start.11 = (bf16[4,64,896]{2,1,0:T(8,128)(2,1)}, bf16[4,64,896]{2,1,0:T(8,128)(2,1)S(1)}, u32[]{:S(2)}, u32[]{:S(2)}) collective-permute-start(bf16[4,64,896]{2,1,0:T(8,128)(2,1)} %get-tuple-element.35), channel_id=1, source_target_pairs={{0,32},{32,64},{64,96},{96,0},{1,33},{33,65},{65,97},{97,1},{2,34}... | collective-permute-start | bytes 1376264 | tf_op jit(solution)/shard_map/ppermute | solution.py:185
  129.7 5.8 %collective-permute-start.12 = (bf16[4,64,896]{2,1,0:T(8,128)(2,1)}, bf16[4,64,896]{2,1,0:T(8,128)(2,1)S(1)}, u32[]{:S(2)}, u32[]{:S(2)}) collective-permute-start(bf16[4,64,896]{2,1,0:T(8,128)(2,1)} %get-tuple-element.36), channel_id=1, source_target_pairs={{0,64},{32,96},{64,0},{96,32},{1,65},{33,97},{65,1},{97,33},{2,66}... | collective-permute-start | bytes 1376264 | tf_op jit(solution)/shard_map/ppermute | solution.py:185
  135.5 1.9 %collective-permute-start.13 = (bf16[4,64,896]{2,1,0:T(8,128)(2,1)}, bf16[4,64,896]{2,1,0:T(8,128)(2,1)S(1)}, u32[]{:S(2)}, u32[]{:S(2)}) collective-permute-start(bf16[4,64,896]{2,1,0:T(8,128)(2,1)} %get-tuple-element.37), channel_id=1, source_target_pairs={{0,96},{32,0},{64,32},{96,64},{1,97},{33,1},{65,33},{97,65},{2,98}... | collective-permute-start | bytes 1376264 | tf_op jit(solution)/shard_map/ppermute | solution.py:185
  137.4 9.4 %all-to-all-done.3.mine = bf16[8,24,2048]{2,1,0:T(8,128)(2,1)S(1)} async-done(((bf16[8,24,2048]{2,1,0:T(8,128)(2,1)}), bf16[8,24,2048]{2,1,0:T(8,128)(2,1)S(1)}, u32[]{:S(2)}, u32[]{:S(2)}) %all-to-all-start.3) | async-done | bytes 786464 | tf_op jit(solution)/shard_map/all_to_all | solution.py:277
  146.8 3.0 %collective-permute-start.9 = (bf16[8,24,2048]{2,1,0:T(8,128)(2,1)S(1)}, bf16[8,24,2048]{2,1,0:T(8,128)(2,1)S(1)}, u32[]{:S(2)}, u32[]{:S(2)}) collective-permute-start(bf16[8,24,2048]{2,1,0:T(8,128)(2,1)S(1)} %all-to-all-done.3.mine), channel_id=1, source_target_pairs={{0,1},{1,0},{2,3},{3,2},{4,5},{5,4},{6,7},{7,6},{8,9},{9,8},{10,11... | collective-permute-start | bytes 2359304 | tf_op jit(solution)/shard_map/ppermute | solution.py:181
  149.8 0.0 collective-permute-done.11.refs_1_
  149.8 2.6 %collective-permute-done.12.refs_2_ = bf16[4,64,896]{2,1,0:T(8,128)(2,1)S(1)} collective-permute-done((bf16[4,64,896]{2,1,0:T(8,128)(2,1)}, bf16[4,64,896]{2,1,0:T(8,128)(2,1)S(1)}, u32[]{:S(2)}, u32[]{:S(2)}) %collective-permute-start.12) | collective-permute-done | bytes 458784 | tf_op jit(solution)/shard_map/ppermute | solution.py:185
  152.4 1.9 %collective-permute-done.13.refs_3_ = bf16[4,64,896]{2,1,0:T(8,128)(2,1)S(1)} collective-permute-done((bf16[4,64,896]{2,1,0:T(8,128)(2,1)}, bf16[4,64,896]{2,1,0:T(8,128)(2,1)S(1)}, u32[]{:S(2)}, u32[]{:S(2)}) %collective-permute-start.13) | collective-permute-done | bytes 458784 | tf_op jit(solution)/shard_map/ppermute | solution.py:185
  154.3 0.2 shard_map.102
  154.5 27.6 %all_to_all.26.parts = bf16[4,64,896]{2,1,0:T(8,128)(2,1)S(1)} all-to-all(bf16[4,64,896]{2,1,0:T(8,128)(2,1)S(1)} %shard_map.102), channel_id=1, replica_groups=mesh['yh'=4,'x'=4,'core'=2,'z'=8,'yl'=2] {'yh'}, dimensions={0} | all-to-all | bytes 917504 | tf_op jit(solution)/shard_map/all_to_all | solution.py:261
  182.1 0.0 copy-done.2
  182.1 0.0 copy-done.3
  182.1 1.4 shard_map.103
  183.5 0.0 collective-permute-done.9.other
  183.5 1.8 shard_map.100
Async XLA Ops:
  21.2 23.4 %collective-permute-start.2 = (bf16[4,64,896]{2,1,0:T(8,128)(2,1)S(1)}, bf16[4,64,896]{2,1,0:T(8,128)(2,1)S(1)}, u32[]{:S(2)}, u32[]{:S(2)}) collective-permute-start(bf16[4,64,896]{2,1,0:T(8,128)(2,1)S(1)} %all_to_all.25.rest_0_), channel_id=1, source_target_pairs={{0,96},{32,0},{64,32},{96,64},{1,97},{33,1},{65,33},{97,65},{2,98}... | collective-permute-start | bytes 1376264 | tf_op jit(solution)/shard_map/ppermute | solution.py:185
  25.8 20.6 %collective-permute-start.1 = (bf16[4,64,896]{2,1,0:T(8,128)(2,1)S(1)}, bf16[4,64,896]{2,1,0:T(8,128)(2,1)S(1)}, u32[]{:S(2)}, u32[]{:S(2)}) collective-permute-start(bf16[4,64,896]{2,1,0:T(8,128)(2,1)S(1)} %all_to_all.25.rest_0_), channel_id=1, source_target_pairs={{0,64},{32,96},{64,0},{96,32},{1,65},{33,97},{65,1},{97,33},{2,66}... | collective-permute-start | bytes 1376264 | tf_op jit(solution)/shard_map/ppermute | solution.py:185
  28.5 21.6 %collective-permute-start = (bf16[4,64,896]{2,1,0:T(8,128)(2,1)S(1)}, bf16[4,64,896]{2,1,0:T(8,128)(2,1)S(1)}, u32[]{:S(2)}, u32[]{:S(2)}) collective-permute-start(bf16[4,64,896]{2,1,0:T(8,128)(2,1)S(1)} %all_to_all.25.rest_0_), channel_id=1, source_target_pairs={{0,32},{32,64},{64,96},{96,0},{1,33},{33,65},{65,97},{97,1},{2,34}... | collective-permute-start | bytes 1376264 | tf_op jit(solution)/shard_map/ppermute | solution.py:185
  31.3 23.5 %collective-permute-start.3 = (bf16[4,64,896]{2,1,0:T(8,128)(2,1)S(1)}, bf16[4,64,896]{2,1,0:T(8,128)(2,1)S(1)}, u32[]{:S(2)}, u32[]{:S(2)}) collective-permute-start(bf16[4,64,896]{2,1,0:T(8,128)(2,1)S(1)} %all_to_all.25.rest_0_), channel_id=1, source_target_pairs={{0,16},{16,0},{1,17},{17,1},{2,18},{18,2},{3,19},{19,3},{4,20},{20... | collective-permute-start | bytes 1376264 | tf_op jit(solution)/shard_map/ppermute | solution.py:181
  44.5 10.3 %collective-permute-start.6 = (bf16[4,64,896]{2,1,0:T(8,128)(2,1)S(1)}, bf16[4,64,896]{2,1,0:T(8,128)(2,1)S(1)}, u32[]{:S(2)}, u32[]{:S(2)}) collective-permute-start(bf16[4,64,896]{2,1,0:T(8,128)(2,1)S(1)} %collective-permute-done.2.rest_3_), channel_id=1, source_target_pairs={{0,16},{16,0},{1,17},{17,1},{2,18},{18,2},{3,19},{19,3},{4,20},{20... | collective-permute-start | bytes 1376264 | tf_op jit(solution)/shard_map/ppermute | solution.py:181
  46.5 8.4 %collective-permute-start.5 = (bf16[4,64,896]{2,1,0:T(8,128)(2,1)S(1)}, bf16[4,64,896]{2,1,0:T(8,128)(2,1)S(1)}, u32[]{:S(2)}, u32[]{:S(2)}) collective-permute-start(bf16[4,64,896]{2,1,0:T(8,128)(2,1)S(1)} %collective-permute-done.1.rest_2_), channel_id=1, source_target_pairs={{0,16},{16,0},{1,17},{17,1},{2,18},{18,2},{3,19},{19,3},{4,20},{20... | collective-permute-start | bytes 1376264 | tf_op jit(solution)/shard_map/ppermute | solution.py:181
  50.2 4.7 %collective-permute-start.4 = (bf16[4,64,896]{2,1,0:T(8,128)(2,1)S(1)}, bf16[4,64,896]{2,1,0:T(8,128)(2,1)}, u32[]{:S(2)}, u32[]{:S(2)}) collective-permute-start(bf16[4,64,896]{2,1,0:T(8,128)(2,1)S(1)} %collective-permute-done.rest_1_), channel_id=1, source_target_pairs={{0,16},{16,0},{1,17},{17,1},{2,18},{18,2},{3,19},{19,3},{4,20},{20... | collective-permute-start | bytes 1376264 | tf_op jit(solution)/shard_map/ppermute | solution.py:181
  52.1 1.4 copy-start
  53.5 1.0 copy-start.1
  60.0 0.8 copy-start.5
  60.8 16.2 %copy-start.6 = (bf16[192,1536]{1,0:T(8,128)(2,1)S(1)}, bf16[192,1536]{1,0:T(8,128)(2,1)}, u32[]{:S(2)}) copy-start(bf16[192,1536]{1,0:T(8,128)(2,1)} %copy-done.5) | copy-start | bytes 1769476
  65.5 1.2 copy-start.4
  66.7 28.6 %all-to-all-start.2 = ((bf16[8,48,512]{2,1,0:T(8,128)(2,1)}), bf16[8,48,512]{2,1,0:T(8,128)(2,1)S(1)}, u32[]{:S(2)}, u32[]{:S(2)}) async-start(bf16[8,48,512]{2,1,0:T(8,128)(2,1)} %bitcast.6), calls=%async_computation.2 | async-start | bytes 786432 | tf_op jit(solution)/shard_map/all_to_all | solution.py:255
  77.0 17.3 %collective-permute-start.7 = (bf16[192,1536]{1,0:T(8,128)(2,1)S(1)}, bf16[192,1536]{1,0:T(8,128)(2,1)S(1)}, u32[]{:S(2)}, u32[]{:S(2)}) collective-permute-start(bf16[192,1536]{1,0:T(8,128)(2,1)S(1)} %copy-done.6), channel_id=1, source_target_pairs={{0,1},{1,0},{2,3},{3,2},{4,5},{5,4},{6,7},{7,6},{8,9},{9,8},{10,11... | collective-permute-start | bytes 1769480 | tf_op jit(solution)/shard_map/ppermute | solution.py:181
  95.3 25.1 %all-to-all-start.1 = ((bf16[8,24,1536]{2,1,0:T(8,128)(2,1)}), bf16[8,24,1536]{2,1,0:T(8,128)(2,1)S(1)}, u32[]{:S(2)}, u32[]{:S(2)}) async-start(bf16[8,24,1536]{2,1,0:T(8,128)(2,1)} %bitcast.5), calls=%async_computation.1 | async-start | bytes 1179648 | tf_op jit(solution)/shard_map/all_to_all | solution.py:271
  102.2 22.7 %collective-permute-start.10 = (bf16[4,4,64,896]{3,2,1,0:T(8,128)(2,1)}, bf16[4,4,64,896]{3,2,1,0:T(8,128)(2,1)}, u32[]{:S(2)}, u32[]{:S(2)}) collective-permute-start(bf16[4,4,64,896]{3,2,1,0:T(8,128)(2,1)} %copy-done.4), channel_id=1, source_target_pairs={{0,16},{16,0},{1,17},{17,1},{2,18},{18,2},{3,19},{19,3},{4,20},{20... | collective-permute-start | bytes 5505032 | tf_op jit(solution)/shard_map/ppermute | solution.py:181
  104.7 5.7 %collective-permute-start.8 = (bf16[24,512]{1,0:T(8,128)(2,1)S(1)}, bf16[24,512]{1,0:T(8,128)(2,1)S(1)}, u32[]{:S(2)}, u32[]{:S(2)}) collective-permute-start(bf16[24,512]{1,0:T(8,128)(2,1)S(1)} %get-tuple-element.31), channel_id=1, source_target_pairs={{0,1},{1,0},{2,3},{3,2},{4,5},{5,4},{6,7},{7,6},{8,9},{9,8},{10,11... | collective-permute-start | bytes 73736 | tf_op jit(solution)/shard_map/ppermute | solution.py:181
  121.3 25.5 %all-to-all-start.3 = ((bf16[8,24,2048]{2,1,0:T(8,128)(2,1)}), bf16[8,24,2048]{2,1,0:T(8,128)(2,1)S(1)}, u32[]{:S(2)}, u32[]{:S(2)}) async-start(bf16[8,24,2048]{2,1,0:T(8,128)(2,1)} %shard_map.99), calls=%async_computation.3 | async-start | bytes 1572864 | tf_op jit(solution)/shard_map/all_to_all | solution.py:277
  127.6 54.5 %copy-start.2 = (s32[1,7]{1,0:T(1,128)S(1)}, s32[1,7]{1,0:T(1,128)}, u32[]{:S(2)}) copy-start(s32[1,7]{1,0:T(1,128)} %gm.1) | copy-start | bytes 88
  127.6 54.5 %copy-start.3 = (s32[1,7]{1,0:T(1,128)S(1)}, s32[1,7]{1,0:T(1,128)}, u32[]{:S(2)}) copy-start(s32[1,7]{1,0:T(1,128)} %um.1) | copy-start | bytes 88
  127.6 22.2 %collective-permute-start.11 = (bf16[4,64,896]{2,1,0:T(8,128)(2,1)}, bf16[4,64,896]{2,1,0:T(8,128)(2,1)S(1)}, u32[]{:S(2)}, u32[]{:S(2)}) collective-permute-start(bf16[4,64,896]{2,1,0:T(8,128)(2,1)} %get-tuple-element.35), channel_id=1, source_target_pairs={{0,32},{32,64},{64,96},{96,0},{1,33},{33,65},{65,97},{97,1},{2,34}... | collective-permute-start | bytes 1376264 | tf_op jit(solution)/shard_map/ppermute | solution.py:185
  129.7 22.8 %collective-permute-start.12 = (bf16[4,64,896]{2,1,0:T(8,128)(2,1)}, bf16[4,64,896]{2,1,0:T(8,128)(2,1)S(1)}, u32[]{:S(2)}, u32[]{:S(2)}) collective-permute-start(bf16[4,64,896]{2,1,0:T(8,128)(2,1)} %get-tuple-element.36), channel_id=1, source_target_pairs={{0,64},{32,96},{64,0},{96,32},{1,65},{33,97},{65,1},{97,33},{2,66}... | collective-permute-start | bytes 1376264 | tf_op jit(solution)/shard_map/ppermute | solution.py:185
  135.5 18.8 %collective-permute-start.13 = (bf16[4,64,896]{2,1,0:T(8,128)(2,1)}, bf16[4,64,896]{2,1,0:T(8,128)(2,1)S(1)}, u32[]{:S(2)}, u32[]{:S(2)}) collective-permute-start(bf16[4,64,896]{2,1,0:T(8,128)(2,1)} %get-tuple-element.37), channel_id=1, source_target_pairs={{0,96},{32,0},{64,32},{96,64},{1,97},{33,1},{65,33},{97,65},{2,98}... | collective-permute-start | bytes 1376264 | tf_op jit(solution)/shard_map/ppermute | solution.py:185
  146.8 36.7 %collective-permute-start.9 = (bf16[8,24,2048]{2,1,0:T(8,128)(2,1)S(1)}, bf16[8,24,2048]{2,1,0:T(8,128)(2,1)S(1)}, u32[]{:S(2)}, u32[]{:S(2)}) collective-permute-start(bf16[8,24,2048]{2,1,0:T(8,128)(2,1)S(1)} %all-to-all-done.3.mine), channel_id=1, source_target_pairs={{0,1},{1,0},{2,3},{3,2},{4,5},{5,4},{6,7},{7,6},{8,9},{9,8},{10,11... | collective-permute-start | bytes 2359304 | tf_op jit(solution)/shard_map/ppermute | solution.py:181

commit v6 on v4

--- a/solution.py
+++ b/solution.py
@@ -15,6 +15,7 @@
 FIRST = 1536
 VM = pl.BlockSpec(memory_space=pltpu.VMEM)
 HB = pl.BlockSpec(memory_space=pltpu.HBM)
+ANY = pl.BlockSpec(memory_space=pl.ANY)
 SM = pl.BlockSpec(memory_space=pltpu.SMEM)
 
 
@@ -51,33 +52,61 @@
 
 
 def forward_kernel(place, tokens, grad_ref, *rest):
-    mine, other = rest[:X], rest[X : 2 * X]
-    hidden_t, d_both, send, keep, side, w = rest[2 * X :]
+    pieces = (rest[:X], rest[X : 2 * X])
+    hidden_out, send_out, keep_out, side_out, d_both, *scratch = rest[2 * X :]
+    w, preact_ref, hidden_t, send, keep, side, sems, out_sems = scratch
+    outs = []
+
+    def put(source, target):
+        outs.append(pltpu.make_async_copy(source, target, out_sems.at[len(outs)]))
+        outs[-1].start()
+
     core, half, own_x = place[0], place[1], place[2]
     width = grad_ref.shape[1]
+    group = X * CORE * BLOCK
+    moves = []
     for yh in range(YH):
         for back in range(X):
             x = lax.rem(own_x + (X - back), X)
-            row = (yh * X + x) * CORE * BLOCK
-            for rows, index in ((mine[back], core), (other[back], 1 - core)):
-                start = pl.multiple_of(row + index * BLOCK, BLOCK)
-                w[pl.ds(start, BLOCK), :] = rows[yh]
+            row = yh * group + x * CORE * BLOCK
+            for index, place_of in enumerate((core, 1 - core)):
+                start = pl.multiple_of(row + place_of * BLOCK, BLOCK)
+                moves.append(
+                    pltpu.make_async_copy(
+                        pieces[index][back].at[yh],
+                        w.at[pl.ds(start, BLOCK), :],
+                        sems.at[len(moves)],
+                    )
+                )
+    for move in moves:
+        move.start()
+    for yh in range(YH):
+        for move in moves[yh * CORE * X : (yh + 1) * CORE * X]:
+            move.wait()
+        span = slice(yh * group, (yh + 1) * group)
+        part = jnp.dot(tokens[:, span], w[span, :], preferred_element_type=F32)
+        preact_ref[...] = part if yh == 0 else preact_ref[...] + part
+    preact = preact_ref[...]
     weights = w[...]
-    preact = jnp.dot(tokens[...], weights, preferred_element_type=F32)
     gate = preact[:, :width]
     up = preact[:, width:]
     sigmoid = jax.nn.sigmoid(gate)
     activation = gate * sigmoid
     hidden_t[...] = (activation * up).T
+    put(hidden_t, hidden_out)
     grad = grad_ref[...]
     d_gate = grad * up * sigmoid * (1.0 + gate * (1.0 - sigmoid))
     d_up = grad * activation
     d_both[...] = jnp.concatenate([d_gate, d_up], axis=1).astype(BF16)
     rows = send.shape[0]
-    for out, index in ((send, 1 - half), (keep, half)):
+    side[...] = to_tokens(d_both[...], weights[FIRST:])
+    put(side, side_out)
+    for part, target, index in ((keep, keep_out, half), (send, send_out, 1 - half)):
         start = pl.multiple_of(index * rows, rows)
-        out[...] = to_tokens(d_both[pl.ds(start, rows), :], weights[:FIRST])
-    side[...] = to_tokens(d_both[...], weights[FIRST:])
+        part[...] = to_tokens(d_both[pl.ds(start, rows), :], weights[:FIRST])
+        put(part, target)
+    for move in outs:
+        move.wait()
 
 
 def to_tokens(grad, weights):
@@ -181,14 +210,13 @@
     return lax.ppermute(array, axis, [(i, (i + steps) % size) for i in range(size)])
 
 
-def call(kernel, out_shape, *operands, scalars=0, scratch=()):
+def call(kernel, out_shape, *operands, scalars=0):
     many = isinstance(out_shape, list)
     results = pl.pallas_call(
         kernel,
         in_specs=[SM] * scalars + [VM] * (len(operands) - scalars),
         out_specs=[VM] * len(out_shape) if many else VM,
         out_shape=out_shape,
-        scratch_shapes=list(scratch),
         compiler_params=params(),
     )(*operands)
     return list(results) if many else results
@@ -223,23 +251,22 @@
     tokens, grad = call(
         prepare_kernel, [shape(tokens.shape), shape((count, width), F32)], tokens, out_grad.T
     )
-    hidden_t, d_both, send, keep, side = call(
+    dims = [(width, count), (half, FIRST), (half, FIRST), (count, rest)]
+    types = [F32, BF16, BF16, BF16]
+    hidden_t, send, keep, side, d_both = pl.pallas_call(
         forward_kernel,
-        [
-            shape((width, count), F32),
-            shape((count, 2 * width)),
-            shape((half, FIRST)),
-            shape((half, FIRST)),
-            shape((count, rest)),
+        in_specs=[SM, VM, VM] + [ANY] * (2 * X),
+        out_specs=[HB] * 4 + [VM],
+        out_shape=[shape(*pair) for pair in zip(dims, types)] + [shape((count, 2 * width))],
+        scratch_shapes=[
+            pltpu.VMEM((features, 2 * width), BF16),
+            pltpu.VMEM((count, 2 * width), F32),
+            *(pltpu.VMEM(*pair) for pair in zip(dims, types)),
+            pltpu.SemaphoreType.DMA((YH * X * CORE,)),
+            pltpu.SemaphoreType.DMA((4,)),
         ],
-        place,
-        tokens,
-        grad,
-        *mine,
-        *other,
-        scalars=1,
-        scratch=[pltpu.VMEM((features, 2 * width), BF16)],
-    )
+        compiler_params=params(),
+    )(place, tokens, grad, *mine, *other)
     received = swap(send, "yl")
     side = lax.all_to_all(side.reshape(Z, 2 * chunk, rest), "z", 0, 0, tiled=True)
     w_keep, w_send = call(

time: 217 us -> 217 us (level)
    pallas_call x0 -> x1, Pallas kernels: none -> 7.68 us  [compute(): pl.pallas_call(forward_kernel, in_specs=[SM, VM, VM] + [ANY] * (2 * X), o...]
    pallas_call x11 -> x10, Pallas kernels: 19.6 us -> 12.3 us  [call(): pl.pallas_call(kernel, in_specs=[SM] * scalars + [VM] * (len(operands) -...]
where the time goes in v6:
time: 217 us; the launch traced here: 216 us
  waiting for transfers between devices  102 us (47%)
  starting transfers between devices  65.7 us (30%)
  Pallas kernels  21.8 us (10%)
  blocking collectives  21 us (10%)
  local copies, waits for them, and re-layouts  4.64 us (2%)
    ppermute x9, waiting for transfers between devices, shift(): lax.ppermute(array, axis, [(i, (i + steps) % size) for i in range(size)])  45.7 us
    ppermute x9, starting transfers between devices, shift(): lax.ppermute(array, axis, [(i, (i + steps) % size) for i in range(size)])  24.8 us
    all_to_all x1, blocking collectives, compute(): rows = lax.all_to_all(copies, 'yh', 0, 0, tiled=True)  21 us
    ppermute x8, starting transfers between devices, swap(): return lax.ppermute(array, axis, [(0, 1), (1, 0)])  20.4 us
    ppermute x8, waiting for transfers between devices, swap(): return lax.ppermute(array, axis, [(0, 1), (1, 0)])  17.8 us
    all_to_all x1, waiting for transfers between devices, compute(): lax.all_to_all(side.reshape(Z, 2 * chunk, rest), 'z', 0, 0, tiled=True)  14.2 us
    all_to_all x1, waiting for transfers between devices, compute(): main = lax.all_to_all(main, 'z', 0, 0, tiled=True).reshape(half, FIRST)  13.3 us
    pallas_call x10, Pallas kernels, call(): pl.pallas_call(kernel, in_specs=[SM] * scalars + [VM] * (len(operands) -...  12.3 us
  transfers between devices with their start and end apart: 21, of which 11 were waited for; matrix products, arithmetic and copies ran while one was open for 0% of the time, Pallas kernels for 4%

profile of v6, /device:TPU:23, one launch (start us, length us, event | category | flops | bytes accessed | tf_op | source)
XLA Modules:
  0.0 216.2 jit_solution(12676831275397772698)
XLA Ops:
  0.6 1.8 shard_map.94
  2.4 21.0 %all_to_all.25.rest_0_ = bf16[4,64,896]{2,1,0:T(8,128)(2,1)S(1)} all-to-all(bf16[4,64,896]{2,1,0:T(8,128)(2,1)} %shard_map.94), channel_id=1, replica_groups=mesh['yh'=4,'x'=4,'core'=2,'z'=8,'yl'=2] {'yh'}, dimensions={0} | all-to-all | bytes 917504 | tf_op jit(solution)/shard_map/all_to_all | solution.py:245
  23.4 2.4 %collective-permute-start.2 = (bf16[4,64,896]{2,1,0:T(8,128)(2,1)S(1)}, bf16[4,64,896]{2,1,0:T(8,128)(2,1)S(1)}, u32[]{:S(2)}, u32[]{:S(2)}) collective-permute-start(bf16[4,64,896]{2,1,0:T(8,128)(2,1)S(1)} %all_to_all.25.rest_0_), channel_id=1, source_target_pairs={{0,96},{32,0},{64,32},{96,64},{1,97},{33,1},{65,33},{97,65},{2,98}... | collective-permute-start | bytes 1376264 | tf_op jit(solution)/shard_map/ppermute | solution.py:210
  25.9 2.6 %collective-permute-start.1 = (bf16[4,64,896]{2,1,0:T(8,128)(2,1)S(1)}, bf16[4,64,896]{2,1,0:T(8,128)(2,1)S(1)}, u32[]{:S(2)}, u32[]{:S(2)}) collective-permute-start(bf16[4,64,896]{2,1,0:T(8,128)(2,1)S(1)} %all_to_all.25.rest_0_), channel_id=1, source_target_pairs={{0,64},{32,96},{64,0},{96,32},{1,65},{33,97},{65,1},{97,33},{2,66}... | collective-permute-start | bytes 1376264 | tf_op jit(solution)/shard_map/ppermute | solution.py:210
  28.5 3.8 %collective-permute-start = (bf16[4,64,896]{2,1,0:T(8,128)(2,1)S(1)}, bf16[4,64,896]{2,1,0:T(8,128)(2,1)}, u32[]{:S(2)}, u32[]{:S(2)}) collective-permute-start(bf16[4,64,896]{2,1,0:T(8,128)(2,1)S(1)} %all_to_all.25.rest_0_), channel_id=1, source_target_pairs={{0,32},{32,64},{64,96},{96,0},{1,33},{33,65},{65,97},{97,1},{2,34}... | collective-permute-start | bytes 1376264 | tf_op jit(solution)/shard_map/ppermute | solution.py:210
  32.4 3.4 %collective-permute-start.3 = (bf16[4,64,896]{2,1,0:T(8,128)(2,1)S(1)}, bf16[4,64,896]{2,1,0:T(8,128)(2,1)}, u32[]{:S(2)}, u32[]{:S(2)}) collective-permute-start(bf16[4,64,896]{2,1,0:T(8,128)(2,1)S(1)} %all_to_all.25.rest_0_), channel_id=1, source_target_pairs={{0,16},{16,0},{1,17},{17,1},{2,18},{18,2},{3,19},{19,3},{4,20},{20... | collective-permute-start | bytes 1376264 | tf_op jit(solution)/shard_map/ppermute | solution.py:206
  35.8 12.1 %collective-permute-done.2.rest_3_ = bf16[4,64,896]{2,1,0:T(8,128)(2,1)S(1)} collective-permute-done((bf16[4,64,896]{2,1,0:T(8,128)(2,1)S(1)}, bf16[4,64,896]{2,1,0:T(8,128)(2,1)S(1)}, u32[]{:S(2)}, u32[]{:S(2)}) %collective-permute-start.2) | collective-permute-done | bytes 458784 | tf_op jit(solution)/shard_map/ppermute | solution.py:210
  47.8 3.4 %collective-permute-start.6 = (bf16[4,64,896]{2,1,0:T(8,128)(2,1)S(1)}, bf16[4,64,896]{2,1,0:T(8,128)(2,1)}, u32[]{:S(2)}, u32[]{:S(2)}) collective-permute-start(bf16[4,64,896]{2,1,0:T(8,128)(2,1)S(1)} %collective-permute-done.2.rest_3_), channel_id=1, source_target_pairs={{0,16},{16,0},{1,17},{17,1},{2,18},{18,2},{3,19},{19,3},{4,20},{20... | collective-permute-start | bytes 1376264 | tf_op jit(solution)/shard_map/ppermute | solution.py:206
  51.2 0.0 collective-permute-done.1.rest_2_
  51.2 0.0 copy-start.3
  51.2 1.9 collective-permute-start.5
  53.2 0.0 collective-permute-done.rest_1_
  53.2 2.4 %collective-permute-start.4 = (bf16[4,64,896]{2,1,0:T(8,128)(2,1)}, bf16[4,64,896]{2,1,0:T(8,128)(2,1)}, u32[]{:S(2)}, u32[]{:S(2)}) collective-permute-start(bf16[4,64,896]{2,1,0:T(8,128)(2,1)} %collective-permute-done.rest_1_), channel_id=1, source_target_pairs={{0,16},{16,0},{1,17},{17,1},{2,18},{18,2},{3,19},{19,3},{4,20},{20... | collective-permute-start | bytes 1376264 | tf_op jit(solution)/shard_map/ppermute | solution.py:206
  55.6 0.0 copy-start.2
  55.6 1.4 copy-done.2
  57.0 1.0 copy-done.5
  58.0 0.2 shard_map.93
  58.2 0.1 pad_add_fusion.place
  58.3 0.0 collective-permute-done.3.rest_4_
  58.3 0.0 collective-permute-done.6.rest_7_
  58.3 0.0 collective-permute-done.5.rest_6_
  58.3 0.0 collective-permute-done.4.rest_5_
  58.4 0.0 copy-start.4
  58.4 1.0 copy-done.4
  59.4 7.7 %shard_map.95 = (f32[448,384]{1,0:T(8,128)}, bf16[192,1536]{1,0:T(8,128)(2,1)S(1)}, bf16[192,1536]{1,0:T(8,128)(2,1)S(1)}, bf16[384,512]{1,0:T(8,128)(2,1)}, bf16[384,896]{1,0:T(8,128)(2,1)S(1)}) custom-call(s32[4]{0:T(128)S(1)} %pad_add_fusion.place, bf16[384,2048]{1,0:T(8,128)(2,1)S(1)} %get-tuple-element.23.tokens, ...), custom_call_target="tpu_custom_call" | custom-call | tf_op jit(solution)/shard_map/pallas_call | solution.py:256
  67.1 1.9 collective-permute-start.7
  69.0 14.8 %collective-permute-done.7.second = bf16[192,1536]{1,0:T(8,128)(2,1)S(1)} collective-permute-done((bf16[192,1536]{1,0:T(8,128)(2,1)S(1)}, bf16[192,1536]{1,0:T(8,128)(2,1)S(1)}, u32[]{:S(2)}, u32[]{:S(2)}) %collective-permute-start.7) | collective-permute-done | bytes 589856 | tf_op jit(solution)/shard_map/ppermute | solution.py:206
  83.8 0.9 shard_map.96
  84.8 10.0 %all-to-all-start.1 = ((bf16[8,24,1536]{2,1,0:T(8,128)(2,1)}), bf16[8,24,1536]{2,1,0:T(8,128)(2,1)S(1)}, u32[]{:S(2)}, u32[]{:S(2)}) async-start(bf16[8,24,1536]{2,1,0:T(8,128)(2,1)} %bitcast.6), calls=%async_computation.1 | async-start | bytes 1179648 | tf_op jit(solution)/shard_map/all_to_all | solution.py:296
  94.8 4.0 %shard_map.101 = (bf16[4,4,64,896]{3,2,1,0:T(8,128)(2,1)S(1)}, bf16[4,4,64,896]{3,2,1,0:T(8,128)(2,1)}) custom-call(s32[4]{0:T(128)S(1)} %pad_add_fusion.place, bf16[384,2048]{1,0:T(8,128)(2,1)S(1)} %get-tuple-element.23.tokens, bf16[384,896]{1,0:T(8,128)(2,1)S(1)} %get-tuple-element.29.d_both), custom_call_target="tpu_custom_call" | custom-call | tf_op jit(solution)/shard_map/pallas_call | solution.py:215
  98.9 1.2 copy-done
  100.1 3.0 %collective-permute-start.10 = (bf16[4,4,64,896]{3,2,1,0:T(8,128)(2,1)}, bf16[4,4,64,896]{3,2,1,0:T(8,128)(2,1)}, u32[]{:S(2)}, u32[]{:S(2)}) collective-permute-start(bf16[4,4,64,896]{3,2,1,0:T(8,128)(2,1)} %get-tuple-element.31), channel_id=1, source_target_pairs={{0,16},{16,0},{1,17},{17,1},{2,18},{18,2},{3,19},{19,3},{4,20},{20... | collective-permute-start | bytes 5505032 | tf_op jit(solution)/shard_map/ppermute | solution.py:206
  103.1 11.0 %all-to-all-done.1.parts = bf16[8,24,1536]{2,1,0:T(8,128)(2,1)S(1)} async-done(((bf16[8,24,1536]{2,1,0:T(8,128)(2,1)}), bf16[8,24,1536]{2,1,0:T(8,128)(2,1)S(1)}, u32[]{:S(2)}, u32[]{:S(2)}) %all-to-all-start.1) | async-done | bytes 589856 | tf_op jit(solution)/shard_map/all_to_all | solution.py:296
  114.2 3.5 %all-to-all-start.3 = ((bf16[8,48,512]{2,1,0:T(8,128)(2,1)}), bf16[8,48,512]{2,1,0:T(8,128)(2,1)S(1)}, u32[]{:S(2)}, u32[]{:S(2)}) async-start(bf16[8,48,512]{2,1,0:T(8,128)(2,1)} %bitcast.8), calls=%async_computation.3 | async-start | bytes 786432 | tf_op jit(solution)/shard_map/all_to_all | solution.py:271
  117.7 0.9 shard_map.97
  118.6 14.2 %all-to-all-done.3.parts = bf16[8,48,512]{2,1,0:T(8,128)(2,1)S(1)} async-done(((bf16[8,48,512]{2,1,0:T(8,128)(2,1)}), bf16[8,48,512]{2,1,0:T(8,128)(2,1)S(1)}, u32[]{:S(2)}, u32[]{:S(2)}) %all-to-all-start.3) | async-done | bytes 393248 | tf_op jit(solution)/shard_map/all_to_all | solution.py:271
  132.7 3.5 %all-to-all-start.2 = ((bf16[8,24,1536]{2,1,0:T(8,128)(2,1)}), bf16[8,24,1536]{2,1,0:T(8,128)(2,1)S(1)}, u32[]{:S(2)}, u32[]{:S(2)}) async-start(bf16[8,24,1536]{2,1,0:T(8,128)(2,1)} %shard_map.97), calls=%async_computation.2 | async-start | bytes 1179648 | tf_op jit(solution)/shard_map/all_to_all | solution.py:301
  136.3 0.1 shard_map.98.first
  136.3 2.2 %collective-permute-start.9 = (bf16[48,512]{1,0:T(8,128)(2,1)S(1)}, bf16[48,512]{1,0:T(8,128)(2,1)S(1)}, u32[]{:S(2)}, u32[]{:S(2)}) collective-permute-start(bf16[48,512]{1,0:T(8,128)(2,1)S(1)} %shard_map.98.first), channel_id=1, source_target_pairs={{0,1},{1,0},{2,3},{3,2},{4,5},{5,4},{6,7},{7,6},{8,9},{9,8},{10,11... | collective-permute-start | bytes 147464 | tf_op jit(solution)/shard_map/ppermute | solution.py:206
  138.5 2.9 %collective-permute-done.9.second = bf16[48,512]{1,0:T(8,128)(2,1)S(1)} collective-permute-done((bf16[48,512]{1,0:T(8,128)(2,1)S(1)}, bf16[48,512]{1,0:T(8,128)(2,1)S(1)}, u32[]{:S(2)}, u32[]{:S(2)}) %collective-permute-start.9) | collective-permute-done | bytes 49184 | tf_op jit(solution)/shard_map/ppermute | solution.py:206
  141.5 0.8 shard_map.99
  142.3 13.3 %all-to-all-done.2 = bf16[8,24,1536]{2,1,0:T(8,128)(2,1)S(1)} async-done(((bf16[8,24,1536]{2,1,0:T(8,128)(2,1)}), bf16[8,24,1536]{2,1,0:T(8,128)(2,1)S(1)}, u32[]{:S(2)}, u32[]{:S(2)}) %all-to-all-start.2) | async-done | bytes 589856 | tf_op jit(solution)/shard_map/all_to_all | solution.py:301
  155.6 3.5 %all-to-all-start.4 = ((bf16[8,48,512]{2,1,0:T(8,128)(2,1)}), bf16[8,48,512]{2,1,0:T(8,128)(2,1)S(1)}, u32[]{:S(2)}, u32[]{:S(2)}) async-start(bf16[8,48,512]{2,1,0:T(8,128)(2,1)} %shard_map.99), calls=%async_computation.4 | async-start | bytes 786432 | tf_op jit(solution)/shard_map/all_to_all | solution.py:303
  159.0 2.2 %collective-permute-start.8 = (bf16[192,1536]{1,0:T(8,128)(2,1)S(1)}, bf16[192,1536]{1,0:T(8,128)(2,1)S(1)}, u32[]{:S(2)}, u32[]{:S(2)}) collective-permute-start(bf16[192,1536]{1,0:T(8,128)(2,1)S(1)} %bitcast.10), channel_id=1, source_target_pairs={{0,1},{1,0},{2,3},{3,2},{4,5},{5,4},{6,7},{7,6},{8,9},{9,8},{10,11... | collective-permute-start | bytes 1769480 | tf_op jit(solution)/shard_map/ppermute | solution.py:206
  161.3 1.9 shard_map.102
  163.2 0.0 copy-start.6
  163.2 0.0 copy-start.7
  163.2 2.5 %collective-permute-start.11 = (bf16[4,64,896]{2,1,0:T(8,128)(2,1)S(1)}, bf16[4,64,896]{2,1,0:T(8,128)(2,1)S(1)}, u32[]{:S(2)}, u32[]{:S(2)}) collective-permute-start(bf16[4,64,896]{2,1,0:T(8,128)(2,1)S(1)} %get-tuple-element.33), channel_id=1, source_target_pairs={{0,32},{32,64},{64,96},{96,0},{1,33},{33,65},{65,97},{97,1},{2,34}... | collective-permute-start | bytes 1376264 | tf_op jit(solution)/shard_map/ppermute | solution.py:210
  165.7 1.9 collective-permute-start.12
  167.7 2.8 %collective-permute-start.13 = (bf16[4,64,896]{2,1,0:T(8,128)(2,1)S(1)}, bf16[4,64,896]{2,1,0:T(8,128)(2,1)S(1)}, u32[]{:S(2)}, u32[]{:S(2)}) collective-permute-start(bf16[4,64,896]{2,1,0:T(8,128)(2,1)S(1)} %get-tuple-element.35), channel_id=1, source_target_pairs={{0,96},{32,0},{64,32},{96,64},{1,97},{33,1},{65,33},{97,65},{2,98}... | collective-permute-start | bytes 1376264 | tf_op jit(solution)/shard_map/ppermute | solution.py:210
  170.4 6.0 %collective-permute-done.11.refs_1_ = bf16[4,64,896]{2,1,0:T(8,128)(2,1)S(1)} collective-permute-done((bf16[4,64,896]{2,1,0:T(8,128)(2,1)S(1)}, bf16[4,64,896]{2,1,0:T(8,128)(2,1)S(1)}, u32[]{:S(2)}, u32[]{:S(2)}) %collective-permute-start.11) | collective-permute-done | bytes 458784 | tf_op jit(solution)/shard_map/ppermute | solution.py:210
  176.4 3.8 %collective-permute-done.12.refs_2_ = bf16[4,64,896]{2,1,0:T(8,128)(2,1)S(1)} collective-permute-done((bf16[4,64,896]{2,1,0:T(8,128)(2,1)S(1)}, bf16[4,64,896]{2,1,0:T(8,128)(2,1)S(1)}, u32[]{:S(2)}, u32[]{:S(2)}) %collective-permute-start.12) | collective-permute-done | bytes 458784 | tf_op jit(solution)/shard_map/ppermute | solution.py:210
  180.2 11.2 %collective-permute-done.13.refs_3_ = bf16[4,64,896]{2,1,0:T(8,128)(2,1)S(1)} collective-permute-done((bf16[4,64,896]{2,1,0:T(8,128)(2,1)S(1)}, bf16[4,64,896]{2,1,0:T(8,128)(2,1)S(1)}, u32[]{:S(2)}, u32[]{:S(2)}) %collective-permute-start.13) | collective-permute-done | bytes 458784 | tf_op jit(solution)/shard_map/ppermute | solution.py:210
  191.4 0.2 shard_map.103
  191.6 2.2 %collective-permute-start.14 = (bf16[64,896]{1,0:T(8,128)(2,1)S(1)}, bf16[64,896]{1,0:T(8,128)(2,1)S(1)}, u32[]{:S(2)}, u32[]{:S(2)}) collective-permute-start(bf16[64,896]{1,0:T(8,128)(2,1)S(1)} %get-tuple-element.37), channel_id=1, source_target_pairs={{0,128},{128,256},{256,384},{384,0},{1,129},{129,257},{257,385},{3... | collective-permute-start | bytes 344072 | tf_op jit(solution)/shard_map/ppermute | solution.py:210
  193.8 4.4 %collective-permute-start.15 = (bf16[64,896]{1,0:T(8,128)(2,1)S(1)}, bf16[64,896]{1,0:T(8,128)(2,1)S(1)}, u32[]{:S(2)}, u32[]{:S(2)}) collective-permute-start(bf16[64,896]{1,0:T(8,128)(2,1)S(1)} %get-tuple-element.38), channel_id=1, source_target_pairs={{0,256},{128,384},{256,0},{384,128},{1,257},{129,385},{257,1},{385... | collective-permute-start | bytes 344072 | tf_op jit(solution)/shard_map/ppermute | solution.py:210
  198.2 2.1 collective-permute-start.16
  200.3 0.0 collective-permute-done.14.refs_1_
  200.4 3.4 %collective-permute-done.15.refs_2_ = bf16[64,896]{1,0:T(8,128)(2,1)S(1)} collective-permute-done((bf16[64,896]{1,0:T(8,128)(2,1)S(1)}, bf16[64,896]{1,0:T(8,128)(2,1)S(1)}, u32[]{:S(2)}, u32[]{:S(2)}) %collective-permute-start.15) | collective-permute-done | bytes 114720 | tf_op jit(solution)/shard_map/ppermute | solution.py:210
  203.7 9.3 %collective-permute-done.16.refs_3_ = bf16[64,896]{1,0:T(8,128)(2,1)S(1)} collective-permute-done((bf16[64,896]{1,0:T(8,128)(2,1)S(1)}, bf16[64,896]{1,0:T(8,128)(2,1)S(1)}, u32[]{:S(2)}, u32[]{:S(2)}) %collective-permute-start.16) | collective-permute-done | bytes 114720 | tf_op jit(solution)/shard_map/ppermute | solution.py:210
  213.0 1.4 shard_map.104
  214.4 0.0 all-to-all-done.4
  214.4 0.0 collective-permute-done.8.other
  214.4 1.8 shard_map.100
  (8 shorter events, 0.0 us)
Async XLA Ops:
  23.4 24.4 %collective-permute-start.2 = (bf16[4,64,896]{2,1,0:T(8,128)(2,1)S(1)}, bf16[4,64,896]{2,1,0:T(8,128)(2,1)S(1)}, u32[]{:S(2)}, u32[]{:S(2)}) collective-permute-start(bf16[4,64,896]{2,1,0:T(8,128)(2,1)S(1)} %all_to_all.25.rest_0_), channel_id=1, source_target_pairs={{0,96},{32,0},{64,32},{96,64},{1,97},{33,1},{65,33},{97,65},{2,98}... | collective-permute-start | bytes 1376264 | tf_op jit(solution)/shard_map/ppermute | solution.py:210
  25.9 25.3 %collective-permute-start.1 = (bf16[4,64,896]{2,1,0:T(8,128)(2,1)S(1)}, bf16[4,64,896]{2,1,0:T(8,128)(2,1)S(1)}, u32[]{:S(2)}, u32[]{:S(2)}) collective-permute-start(bf16[4,64,896]{2,1,0:T(8,128)(2,1)S(1)} %all_to_all.25.rest_0_), channel_id=1, source_target_pairs={{0,64},{32,96},{64,0},{96,32},{1,65},{33,97},{65,1},{97,33},{2,66}... | collective-permute-start | bytes 1376264 | tf_op jit(solution)/shard_map/ppermute | solution.py:210
  28.5 24.6 %collective-permute-start = (bf16[4,64,896]{2,1,0:T(8,128)(2,1)S(1)}, bf16[4,64,896]{2,1,0:T(8,128)(2,1)}, u32[]{:S(2)}, u32[]{:S(2)}) collective-permute-start(bf16[4,64,896]{2,1,0:T(8,128)(2,1)S(1)} %all_to_all.25.rest_0_), channel_id=1, source_target_pairs={{0,32},{32,64},{64,96},{96,0},{1,33},{33,65},{65,97},{97,1},{2,34}... | collective-permute-start | bytes 1376264 | tf_op jit(solution)/shard_map/ppermute | solution.py:210
  32.4 25.9 %collective-permute-start.3 = (bf16[4,64,896]{2,1,0:T(8,128)(2,1)S(1)}, bf16[4,64,896]{2,1,0:T(8,128)(2,1)}, u32[]{:S(2)}, u32[]{:S(2)}) collective-permute-start(bf16[4,64,896]{2,1,0:T(8,128)(2,1)S(1)} %all_to_all.25.rest_0_), channel_id=1, source_target_pairs={{0,16},{16,0},{1,17},{17,1},{2,18},{18,2},{3,19},{19,3},{4,20},{20... | collective-permute-start | bytes 1376264 | tf_op jit(solution)/shard_map/ppermute | solution.py:206
  47.8 10.5 %collective-permute-start.6 = (bf16[4,64,896]{2,1,0:T(8,128)(2,1)S(1)}, bf16[4,64,896]{2,1,0:T(8,128)(2,1)}, u32[]{:S(2)}, u32[]{:S(2)}) collective-permute-start(bf16[4,64,896]{2,1,0:T(8,128)(2,1)S(1)} %collective-permute-done.2.rest_3_), channel_id=1, source_target_pairs={{0,16},{16,0},{1,17},{17,1},{2,18},{18,2},{3,19},{19,3},{4,20},{20... | collective-permute-start | bytes 1376264 | tf_op jit(solution)/shard_map/ppermute | solution.py:206
  51.2 7.1 %copy-start.3 = (bf16[4,64,896]{2,1,0:T(8,128)(2,1)}, bf16[4,64,896]{2,1,0:T(8,128)(2,1)S(1)}, u32[]{:S(2)}) copy-start(bf16[4,64,896]{2,1,0:T(8,128)(2,1)S(1)} %collective-permute-done.1.rest_2_) | copy-start | bytes 1376260
  51.2 7.1 %collective-permute-start.5 = (bf16[4,64,896]{2,1,0:T(8,128)(2,1)S(1)}, bf16[4,64,896]{2,1,0:T(8,128)(2,1)}, u32[]{:S(2)}, u32[]{:S(2)}) collective-permute-start(bf16[4,64,896]{2,1,0:T(8,128)(2,1)S(1)} %collective-permute-done.1.rest_2_), channel_id=1, source_target_pairs={{0,16},{16,0},{1,17},{17,1},{2,18},{18,2},{3,19},{19,3},{4,20},{20... | collective-permute-start | bytes 1376264 | tf_op jit(solution)/shard_map/ppermute | solution.py:206
  53.2 5.2 %collective-permute-start.4 = (bf16[4,64,896]{2,1,0:T(8,128)(2,1)}, bf16[4,64,896]{2,1,0:T(8,128)(2,1)}, u32[]{:S(2)}, u32[]{:S(2)}) collective-permute-start(bf16[4,64,896]{2,1,0:T(8,128)(2,1)} %collective-permute-done.rest_1_), channel_id=1, source_target_pairs={{0,16},{16,0},{1,17},{17,1},{2,18},{18,2},{3,19},{19,3},{4,20},{20... | collective-permute-start | bytes 1376264 | tf_op jit(solution)/shard_map/ppermute | solution.py:206
  55.6 1.4 copy-start.2
  57.0 1.0 copy-start.5
  58.4 1.0 copy-start.4
  67.1 16.8 %collective-permute-start.7 = (bf16[192,1536]{1,0:T(8,128)(2,1)S(1)}, bf16[192,1536]{1,0:T(8,128)(2,1)S(1)}, u32[]{:S(2)}, u32[]{:S(2)}) collective-permute-start(bf16[192,1536]{1,0:T(8,128)(2,1)S(1)} %get-tuple-element.27), channel_id=1, source_target_pairs={{0,1},{1,0},{2,3},{3,2},{4,5},{5,4},{6,7},{7,6},{8,9},{9,8},{10,11... | collective-permute-start | bytes 1769480 | tf_op jit(solution)/shard_map/ppermute | solution.py:206
  84.8 29.4 %all-to-all-start.1 = ((bf16[8,24,1536]{2,1,0:T(8,128)(2,1)}), bf16[8,24,1536]{2,1,0:T(8,128)(2,1)S(1)}, u32[]{:S(2)}, u32[]{:S(2)}) async-start(bf16[8,24,1536]{2,1,0:T(8,128)(2,1)} %bitcast.6), calls=%async_computation.1 | async-start | bytes 1179648 | tf_op jit(solution)/shard_map/all_to_all | solution.py:296
  98.9 1.2 copy-start
  100.1 61.1 %collective-permute-start.10 = (bf16[4,4,64,896]{3,2,1,0:T(8,128)(2,1)}, bf16[4,4,64,896]{3,2,1,0:T(8,128)(2,1)}, u32[]{:S(2)}, u32[]{:S(2)}) collective-permute-start(bf16[4,4,64,896]{3,2,1,0:T(8,128)(2,1)} %get-tuple-element.31), channel_id=1, source_target_pairs={{0,16},{16,0},{1,17},{17,1},{2,18},{18,2},{3,19},{19,3},{4,20},{20... | collective-permute-start | bytes 5505032 | tf_op jit(solution)/shard_map/ppermute | solution.py:206
  114.2 18.5 %all-to-all-start.3 = ((bf16[8,48,512]{2,1,0:T(8,128)(2,1)}), bf16[8,48,512]{2,1,0:T(8,128)(2,1)S(1)}, u32[]{:S(2)}, u32[]{:S(2)}) async-start(bf16[8,48,512]{2,1,0:T(8,128)(2,1)} %bitcast.8), calls=%async_computation.3 | async-start | bytes 786432 | tf_op jit(solution)/shard_map/all_to_all | solution.py:271
  118.6 42.7 %copy-start.1 = (bf16[4,4,64,896]{3,2,1,0:T(8,128)(2,1)S(1)}, bf16[4,4,64,896]{3,2,1,0:T(8,128)(2,1)}, u32[]{:S(2)}) copy-start(bf16[4,4,64,896]{3,2,1,0:T(8,128)(2,1)} %copy-done) | copy-start | bytes 5505028
  132.7 22.9 %all-to-all-start.2 = ((bf16[8,24,1536]{2,1,0:T(8,128)(2,1)}), bf16[8,24,1536]{2,1,0:T(8,128)(2,1)S(1)}, u32[]{:S(2)}, u32[]{:S(2)}) async-start(bf16[8,24,1536]{2,1,0:T(8,128)(2,1)} %shard_map.97), calls=%async_computation.2 | async-start | bytes 1179648 | tf_op jit(solution)/shard_map/all_to_all | solution.py:301
  136.3 5.1 %collective-permute-start.9 = (bf16[48,512]{1,0:T(8,128)(2,1)S(1)}, bf16[48,512]{1,0:T(8,128)(2,1)S(1)}, u32[]{:S(2)}, u32[]{:S(2)}) collective-permute-start(bf16[48,512]{1,0:T(8,128)(2,1)S(1)} %shard_map.98.first), channel_id=1, source_target_pairs={{0,1},{1,0},{2,3},{3,2},{4,5},{5,4},{6,7},{7,6},{8,9},{9,8},{10,11... | collective-permute-start | bytes 147464 | tf_op jit(solution)/shard_map/ppermute | solution.py:206
  155.6 58.8 %all-to-all-start.4 = ((bf16[8,48,512]{2,1,0:T(8,128)(2,1)}), bf16[8,48,512]{2,1,0:T(8,128)(2,1)S(1)}, u32[]{:S(2)}, u32[]{:S(2)}) async-start(bf16[8,48,512]{2,1,0:T(8,128)(2,1)} %shard_map.99), calls=%async_computation.4 | async-start | bytes 786432 | tf_op jit(solution)/shard_map/all_to_all | solution.py:303
  159.0 55.3 %collective-permute-start.8 = (bf16[192,1536]{1,0:T(8,128)(2,1)S(1)}, bf16[192,1536]{1,0:T(8,128)(2,1)S(1)}, u32[]{:S(2)}, u32[]{:S(2)}) collective-permute-start(bf16[192,1536]{1,0:T(8,128)(2,1)S(1)} %bitcast.10), channel_id=1, source_target_pairs={{0,1},{1,0},{2,3},{3,2},{4,5},{5,4},{6,7},{7,6},{8,9},{9,8},{10,11... | collective-permute-start | bytes 1769480 | tf_op jit(solution)/shard_map/ppermute | solution.py:206
  163.2 49.8 %copy-start.6 = (s32[1,7]{1,0:T(1,128)S(1)}, s32[1,7]{1,0:T(1,128)}, u32[]{:S(2)}) copy-start(s32[1,7]{1,0:T(1,128)} %gm.1) | copy-start | bytes 88
  163.2 49.8 %copy-start.7 = (s32[1,7]{1,0:T(1,128)S(1)}, s32[1,7]{1,0:T(1,128)}, u32[]{:S(2)}) copy-start(s32[1,7]{1,0:T(1,128)} %um.1) | copy-start | bytes 88
  163.2 13.2 %collective-permute-start.11 = (bf16[4,64,896]{2,1,0:T(8,128)(2,1)S(1)}, bf16[4,64,896]{2,1,0:T(8,128)(2,1)S(1)}, u32[]{:S(2)}, u32[]{:S(2)}) collective-permute-start(bf16[4,64,896]{2,1,0:T(8,128)(2,1)S(1)} %get-tuple-element.33), channel_id=1, source_target_pairs={{0,32},{32,64},{64,96},{96,0},{1,33},{33,65},{65,97},{97,1},{2,34}... | collective-permute-start | bytes 1376264 | tf_op jit(solution)/shard_map/ppermute | solution.py:210
  165.7 14.5 %collective-permute-start.12 = (bf16[4,64,896]{2,1,0:T(8,128)(2,1)S(1)}, bf16[4,64,896]{2,1,0:T(8,128)(2,1)S(1)}, u32[]{:S(2)}, u32[]{:S(2)}) collective-permute-start(bf16[4,64,896]{2,1,0:T(8,128)(2,1)S(1)} %get-tuple-element.34), channel_id=1, source_target_pairs={{0,64},{32,96},{64,0},{96,32},{1,65},{33,97},{65,1},{97,33},{2,66}... | collective-permute-start | bytes 1376264 | tf_op jit(solution)/shard_map/ppermute | solution.py:210
  167.7 23.7 %collective-permute-start.13 = (bf16[4,64,896]{2,1,0:T(8,128)(2,1)S(1)}, bf16[4,64,896]{2,1,0:T(8,128)(2,1)S(1)}, u32[]{:S(2)}, u32[]{:S(2)}) collective-permute-start(bf16[4,64,896]{2,1,0:T(8,128)(2,1)S(1)} %get-tuple-element.35), channel_id=1, source_target_pairs={{0,96},{32,0},{64,32},{96,64},{1,97},{33,1},{65,33},{97,65},{2,98}... | collective-permute-start | bytes 1376264 | tf_op jit(solution)/shard_map/ppermute | solution.py:210
  191.6 8.7 %collective-permute-start.14 = (bf16[64,896]{1,0:T(8,128)(2,1)S(1)}, bf16[64,896]{1,0:T(8,128)(2,1)S(1)}, u32[]{:S(2)}, u32[]{:S(2)}) collective-permute-start(bf16[64,896]{1,0:T(8,128)(2,1)S(1)} %get-tuple-element.37), channel_id=1, source_target_pairs={{0,128},{128,256},{256,384},{384,0},{1,129},{129,257},{257,385},{3... | collective-permute-start | bytes 344072 | tf_op jit(solution)/shard_map/ppermute | solution.py:210
  193.8 9.9 %collective-permute-start.15 = (bf16[64,896]{1,0:T(8,128)(2,1)S(1)}, bf16[64,896]{1,0:T(8,128)(2,1)S(1)}, u32[]{:S(2)}, u32[]{:S(2)}) collective-permute-start(bf16[64,896]{1,0:T(8,128)(2,1)S(1)} %get-tuple-element.38), channel_id=1, source_target_pairs={{0,256},{128,384},{256,0},{384,128},{1,257},{129,385},{257,1},{385... | collective-permute-start | bytes 344072 | tf_op jit(solution)/shard_map/ppermute | solution.py:210
  198.2 14.8 %collective-permute-start.16 = (bf16[64,896]{1,0:T(8,128)(2,1)S(1)}, bf16[64,896]{1,0:T(8,128)(2,1)S(1)}, u32[]{:S(2)}, u32[]{:S(2)}) collective-permute-start(bf16[64,896]{1,0:T(8,128)(2,1)S(1)} %get-tuple-element.39), channel_id=1, source_target_pairs={{0,384},{128,0},{256,128},{384,256},{1,385},{129,1},{257,129},{385... | collective-permute-start | bytes 344072 | tf_op jit(solution)/shard_map/ppermute | solution.py:210

commit v7 on v4

--- a/solution.py
+++ b/solution.py
@@ -47,21 +47,19 @@
 
 def prepare_kernel(tokens, ogt, tokens_out, grad_out):
     tokens_out[...] = tokens[...]
-    grad_out[...] = ogt[...].astype(F32).T
+    grad_out[...] = ogt[...].astype(F32).T.astype(BF16)
 
 
 def forward_kernel(place, tokens, grad_ref, *rest):
-    mine, other = rest[:X], rest[X : 2 * X]
-    hidden_t, d_both, send, keep, side, w = rest[2 * X :]
-    core, half, own_x = place[0], place[1], place[2]
+    mine, other, hidden_t, d_both, send, keep, side, w = rest
+    core, half = place[0], place[1]
     width = grad_ref.shape[1]
     for yh in range(YH):
-        for back in range(X):
-            x = lax.rem(own_x + (X - back), X)
+        for x in range(X):
             row = (yh * X + x) * CORE * BLOCK
-            for rows, index in ((mine[back], core), (other[back], 1 - core)):
+            for rows, index in ((mine, core), (other, 1 - core)):
                 start = pl.multiple_of(row + index * BLOCK, BLOCK)
-                w[pl.ds(start, BLOCK), :] = rows[yh]
+                w[pl.ds(start, BLOCK), :] = rows[x, yh]
     weights = w[...]
     preact = jnp.dot(tokens[...], weights, preferred_element_type=F32)
     gate = preact[:, :width]
@@ -69,7 +67,7 @@
     sigmoid = jax.nn.sigmoid(gate)
     activation = gate * sigmoid
     hidden_t[...] = (activation * up).T
-    grad = grad_ref[...]
+    grad = grad_ref[...].astype(F32)
     d_gate = grad * up * sigmoid * (1.0 + gate * (1.0 - sigmoid))
     d_up = grad * activation
     d_both[...] = jnp.concatenate([d_gate, d_up], axis=1).astype(BF16)
@@ -167,6 +165,10 @@
 
 def shape(dims, dtype=BF16):
     return jax.ShapeDtypeStruct(dims, dtype)
+
+
+def far(dims):
+    return pltpu.HBM(dims, BF16)
 
 
 def params():
@@ -215,28 +217,26 @@
         ],
     )(gate_mask, up_mask, gate_weight, up_weight)
     rows = lax.all_to_all(copies, "yh", 0, 0, tiled=True)
-    mine, other = [rows], []
-    for steps in range(1, X):
-        mine.append(shift(rows, "x", X, steps))
-    for steps in range(X):
-        other.append(swap(mine[steps], "core"))
+    rows = jnp.broadcast_to(rows[None], (X,) + rows.shape)
+    mine = lax.all_to_all(rows, "x", 0, 0, tiled=True)
+    other = swap(mine, "core")
     tokens, grad = call(
-        prepare_kernel, [shape(tokens.shape), shape((count, width), F32)], tokens, out_grad.T
+        prepare_kernel, [shape(tokens.shape), far((count, width))], tokens, out_grad.T
     )
     hidden_t, d_both, send, keep, side = call(
         forward_kernel,
         [
             shape((width, count), F32),
-            shape((count, 2 * width)),
-            shape((half, FIRST)),
-            shape((half, FIRST)),
-            shape((count, rest)),
+            far((count, 2 * width)),
+            far((half, FIRST)),
+            far((half, FIRST)),
+            far((count, rest)),
         ],
         place,
         tokens,
         grad,
-        *mine,
-        *other,
+        mine,
+        other,
         scalars=1,
         scratch=[pltpu.VMEM((features, 2 * width), BF16)],
     )

time: 217 us -> 215 us (level)
  the two profiles are of different devices: /device:TPU:23 before, /device:TPU:1 now
where the time goes in v7:
time: 215 us; the launch traced here: 214 us
  waiting for transfers between devices  72.2 us (34%)
  starting transfers between devices  67.6 us (31%)
  blocking collectives  45.6 us (21%)
  Pallas kernels  22.1 us (10%)
  local copies, waits for them, and re-layouts  5.92 us (3%)
    ppermute x6, waiting for transfers between devices, shift(): lax.ppermute(array, axis, [(i, (i + steps) % size) for i in range(size)])  27.2 us
    ppermute x5, starting transfers between devices, swap(): return lax.ppermute(array, axis, [(0, 1), (1, 0)])  26.4 us
    all_to_all x1, blocking collectives, compute(): mine = lax.all_to_all(rows, 'x', 0, 0, tiled=True)  25.2 us
    ppermute x6, starting transfers between devices, shift(): lax.ppermute(array, axis, [(i, (i + steps) % size) for i in range(size)])  20.7 us
    all_to_all x1, blocking collectives, compute(): rows = lax.all_to_all(copies, 'yh', 0, 0, tiled=True)  20.4 us
    pallas_call x11, Pallas kernels, call(): pl.pallas_call(kernel, in_specs=[SM] * scalars + [VM] * (len(operands) -...  20.3 us
    ppermute x5, waiting for transfers between devices, swap(): return lax.ppermute(array, axis, [(0, 1), (1, 0)])  16.5 us
    all_to_all x1, waiting for transfers between devices, compute(): lax.all_to_all(side.reshape(Z, 2 * chunk, rest), 'z', 0, 0, tiled=True)  11.6 us
  transfers between devices with their start and end apart: 15, of which 11 were waited for; matrix products, arithmetic and copies ran while one was open for 0% of the time, Pallas kernels for 5%

profile of v7, /device:TPU:1, one launch (start us, length us, event | category | flops | bytes accessed | tf_op | source)
XLA Modules:
  0.0 214.4 jit_solution(2536623370431206838)
XLA Ops:
  0.6 1.8 shard_map.94
  2.4 20.4 %all_to_all.30 = bf16[4,64,896]{2,1,0:T(8,128)(2,1)S(1)} all-to-all(bf16[4,64,896]{2,1,0:T(8,128)(2,1)} %shard_map.94), channel_id=1, replica_groups=mesh['yh'=4,'x'=4,'core'=2,'z'=8,'yl'=2] {'yh'}, dimensions={0} | all-to-all | bytes 917504 | tf_op jit(solution)/shard_map/all_to_all | solution.py:219
  22.8 0.2 broadcast_in_dim.2
  23.1 25.2 %all_to_all.31.rest_0_ = bf16[4,4,64,896]{3,2,1,0:T(8,128)(2,1)S(1)} all-to-all(bf16[4,4,64,896]{3,2,1,0:T(8,128)(2,1)S(1)} %broadcast_in_dim.2), channel_id=1, replica_groups=mesh['yh'=4,'x'=4,'core'=2,'z'=8,'yl'=2] {'x'}, dimensions={0} | all-to-all | bytes 3670016 | tf_op jit(solution)/shard_map/all_to_all | solution.py:221
  48.3 5.8 %collective-permute-start = (bf16[4,4,64,896]{3,2,1,0:T(8,128)(2,1)S(1)}, bf16[4,4,64,896]{3,2,1,0:T(8,128)(2,1)}, u32[]{:S(2)}, u32[]{:S(2)}) collective-permute-start(bf16[4,4,64,896]{3,2,1,0:T(8,128)(2,1)S(1)} %all_to_all.31.rest_0_), channel_id=1, source_target_pairs={{0,16},{16,0},{1,17},{17,1},{2,18},{18,2},{3,19},{19,3},{4,20},{20... | collective-permute-start | bytes 5505032 | tf_op jit(solution)/shard_map/ppermute | solution.py:179
  54.1 0.0 copy-start.2
  54.1 1.4 copy-done.2
  55.5 0.0 copy-start.6
  55.5 1.0 copy-done.6
  56.5 1.0 shard_map.93
  57.5 0.1 pad_add_fusion.place
  57.6 0.1 collective-permute-done.rest_1_
  57.6 0.0 copy-start.5
  57.6 1.0 copy-done.5
  58.6 7.2 %shard_map.95 = (f32[448,384]{1,0:T(8,128)}, bf16[384,896]{1,0:T(8,128)(2,1)}, bf16[192,1536]{1,0:T(8,128)(2,1)}, bf16[192,1536]{1,0:T(8,128)(2,1)}, bf16[384,512]{1,0:T(8,128)(2,1)}) custom-call(s32[4]{0:T(128)S(1)} %pad_add_fusion.place, bf16[384,2048]{1,0:T(8,128)(2,1)S(1)} %get-tuple-element.23.tokens, bf16[384,448]{1,0:T(8,128)(2,1)S(1)} %copy-done.5, ...), custom_call_target="tpu_custom_call" | custom-call | tf_op jit(solution)/shard_map/pallas_call | solution.py:188
  65.8 0.0 copy-start.3
  65.8 2.0 collective-permute-start.1
  67.9 14.7 %collective-permute-done.1.second = bf16[192,1536]{1,0:T(8,128)(2,1)S(1)} collective-permute-done((bf16[192,1536]{1,0:T(8,128)(2,1)}, bf16[192,1536]{1,0:T(8,128)(2,1)S(1)}, u32[]{:S(2)}, u32[]{:S(2)}) %collective-permute-start.1) | collective-permute-done | bytes 589856 | tf_op jit(solution)/shard_map/ppermute | solution.py:179
  82.6 0.0 copy-start.4
  82.6 1.1 copy-done.4
  83.6 1.0 shard_map.96
  84.6 10.0 %all-to-all-start.2 = ((bf16[8,24,1536]{2,1,0:T(8,128)(2,1)}), bf16[8,24,1536]{2,1,0:T(8,128)(2,1)S(1)}, u32[]{:S(2)}, u32[]{:S(2)}) async-start(bf16[8,24,1536]{2,1,0:T(8,128)(2,1)} %bitcast.6), calls=%async_computation.2 | async-start | bytes 1179648 | tf_op jit(solution)/shard_map/all_to_all | solution.py:269
  94.6 0.0 copy-done.3
  94.6 4.1 %shard_map.101 = (bf16[4,4,64,896]{3,2,1,0:T(8,128)(2,1)S(1)}, bf16[4,4,64,896]{3,2,1,0:T(8,128)(2,1)}) custom-call(s32[4]{0:T(128)S(1)} %pad_add_fusion.place, bf16[384,2048]{1,0:T(8,128)(2,1)S(1)} %get-tuple-element.23.tokens, bf16[384,896]{1,0:T(8,128)(2,1)S(1)} %copy-done.3), custom_call_target="tpu_custom_call" | custom-call | tf_op jit(solution)/shard_map/pallas_call | solution.py:188
  98.7 0.0 copy-start
  98.7 1.2 copy-done
  100.0 3.4 %collective-permute-start.4 = (bf16[4,4,64,896]{3,2,1,0:T(8,128)(2,1)}, bf16[4,4,64,896]{3,2,1,0:T(8,128)(2,1)}, u32[]{:S(2)}, u32[]{:S(2)}) collective-permute-start(bf16[4,4,64,896]{3,2,1,0:T(8,128)(2,1)} %get-tuple-element.31), channel_id=1, source_target_pairs={{0,16},{16,0},{1,17},{17,1},{2,18},{18,2},{3,19},{19,3},{4,20},{20... | collective-permute-start | bytes 5505032 | tf_op jit(solution)/shard_map/ppermute | solution.py:179
  103.4 9.4 %all-to-all-done.2.parts = bf16[8,24,1536]{2,1,0:T(8,128)(2,1)S(1)} async-done(((bf16[8,24,1536]{2,1,0:T(8,128)(2,1)}), bf16[8,24,1536]{2,1,0:T(8,128)(2,1)S(1)}, u32[]{:S(2)}, u32[]{:S(2)}) %all-to-all-start.2) | async-done | bytes 589856 | tf_op jit(solution)/shard_map/all_to_all | solution.py:269
  112.8 3.5 %all-to-all-start.4 = ((bf16[8,48,512]{2,1,0:T(8,128)(2,1)}), bf16[8,48,512]{2,1,0:T(8,128)(2,1)S(1)}, u32[]{:S(2)}, u32[]{:S(2)}) async-start(bf16[8,48,512]{2,1,0:T(8,128)(2,1)} %bitcast.8), calls=%async_computation.4 | async-start | bytes 786432 | tf_op jit(solution)/shard_map/all_to_all | solution.py:244
  116.3 0.0 copy-start.1
  116.3 0.9 shard_map.97
  117.2 11.6 %all-to-all-done.4.parts = bf16[8,48,512]{2,1,0:T(8,128)(2,1)S(1)} async-done(((bf16[8,48,512]{2,1,0:T(8,128)(2,1)}), bf16[8,48,512]{2,1,0:T(8,128)(2,1)S(1)}, u32[]{:S(2)}, u32[]{:S(2)}) %all-to-all-start.4) | async-done | bytes 393248 | tf_op jit(solution)/shard_map/all_to_all | solution.py:244
  128.7 3.5 %all-to-all-start.3 = ((bf16[8,24,1536]{2,1,0:T(8,128)(2,1)}), bf16[8,24,1536]{2,1,0:T(8,128)(2,1)S(1)}, u32[]{:S(2)}, u32[]{:S(2)}) async-start(bf16[8,24,1536]{2,1,0:T(8,128)(2,1)} %shard_map.97), calls=%async_computation.3 | async-start | bytes 1179648 | tf_op jit(solution)/shard_map/all_to_all | solution.py:274
  132.3 0.1 shard_map.98.first
  132.3 6.0 %collective-permute-start.3 = (bf16[48,512]{1,0:T(8,128)(2,1)S(1)}, bf16[48,512]{1,0:T(8,128)(2,1)S(1)}, u32[]{:S(2)}, u32[]{:S(2)}) collective-permute-start(bf16[48,512]{1,0:T(8,128)(2,1)S(1)} %shard_map.98.first), channel_id=1, source_target_pairs={{0,1},{1,0},{2,3},{3,2},{4,5},{5,4},{6,7},{7,6},{8,9},{9,8},{10,11... | collective-permute-start | bytes 147464 | tf_op jit(solution)/shard_map/ppermute | solution.py:179
  138.3 1.8 collective-permute-done.3.second
  140.1 0.8 shard_map.99
  140.9 7.6 %all-to-all-done.3 = bf16[8,24,1536]{2,1,0:T(8,128)(2,1)S(1)} async-done(((bf16[8,24,1536]{2,1,0:T(8,128)(2,1)}), bf16[8,24,1536]{2,1,0:T(8,128)(2,1)S(1)}, u32[]{:S(2)}, u32[]{:S(2)}) %all-to-all-start.3) | async-done | bytes 589856 | tf_op jit(solution)/shard_map/all_to_all | solution.py:274
  148.4 3.5 %all-to-all-start.5 = ((bf16[8,48,512]{2,1,0:T(8,128)(2,1)}), bf16[8,48,512]{2,1,0:T(8,128)(2,1)S(1)}, u32[]{:S(2)}, u32[]{:S(2)}) async-start(bf16[8,48,512]{2,1,0:T(8,128)(2,1)} %shard_map.99), calls=%async_computation.5 | async-start | bytes 786432 | tf_op jit(solution)/shard_map/all_to_all | solution.py:276
  151.9 9.1 %collective-permute-start.2 = (bf16[192,1536]{1,0:T(8,128)(2,1)S(1)}, bf16[192,1536]{1,0:T(8,128)(2,1)S(1)}, u32[]{:S(2)}, u32[]{:S(2)}) collective-permute-start(bf16[192,1536]{1,0:T(8,128)(2,1)S(1)} %bitcast.10), channel_id=1, source_target_pairs={{0,1},{1,0},{2,3},{3,2},{4,5},{5,4},{6,7},{7,6},{8,9},{9,8},{10,11... | collective-permute-start | bytes 1769480 | tf_op jit(solution)/shard_map/ppermute | solution.py:179
  161.0 0.0 collective-permute-done.4.second
  161.1 0.0 copy-done.1
  161.1 1.9 shard_map.102
  163.0 0.0 copy-start.7
  163.0 0.0 copy-start.8
  163.0 2.2 %collective-permute-start.5 = (bf16[4,64,896]{2,1,0:T(8,128)(2,1)S(1)}, bf16[4,64,896]{2,1,0:T(8,128)(2,1)S(1)}, u32[]{:S(2)}, u32[]{:S(2)}) collective-permute-start(bf16[4,64,896]{2,1,0:T(8,128)(2,1)S(1)} %get-tuple-element.33), channel_id=1, source_target_pairs={{0,32},{32,64},{64,96},{96,0},{1,33},{33,65},{65,97},{97,1},{2,34}... | collective-permute-start | bytes 1376264 | tf_op jit(solution)/shard_map/ppermute | solution.py:183
  165.3 3.7 %collective-permute-start.6 = (bf16[4,64,896]{2,1,0:T(8,128)(2,1)S(1)}, bf16[4,64,896]{2,1,0:T(8,128)(2,1)S(1)}, u32[]{:S(2)}, u32[]{:S(2)}) collective-permute-start(bf16[4,64,896]{2,1,0:T(8,128)(2,1)S(1)} %get-tuple-element.34), channel_id=1, source_target_pairs={{0,64},{32,96},{64,0},{96,32},{1,65},{33,97},{65,1},{97,33},{2,66}... | collective-permute-start | bytes 1376264 | tf_op jit(solution)/shard_map/ppermute | solution.py:183
  169.0 2.5 %collective-permute-start.7 = (bf16[4,64,896]{2,1,0:T(8,128)(2,1)S(1)}, bf16[4,64,896]{2,1,0:T(8,128)(2,1)S(1)}, u32[]{:S(2)}, u32[]{:S(2)}) collective-permute-start(bf16[4,64,896]{2,1,0:T(8,128)(2,1)S(1)} %get-tuple-element.35), channel_id=1, source_target_pairs={{0,96},{32,0},{64,32},{96,64},{1,97},{33,1},{65,33},{97,65},{2,98}... | collective-permute-start | bytes 1376264 | tf_op jit(solution)/shard_map/ppermute | solution.py:183
  171.5 6.5 %collective-permute-done.5.refs_1_ = bf16[4,64,896]{2,1,0:T(8,128)(2,1)S(1)} collective-permute-done((bf16[4,64,896]{2,1,0:T(8,128)(2,1)S(1)}, bf16[4,64,896]{2,1,0:T(8,128)(2,1)S(1)}, u32[]{:S(2)}, u32[]{:S(2)}) %collective-permute-start.5) | collective-permute-done | bytes 458784 | tf_op jit(solution)/shard_map/ppermute | solution.py:183
  178.0 8.8 %collective-permute-done.6.refs_2_ = bf16[4,64,896]{2,1,0:T(8,128)(2,1)S(1)} collective-permute-done((bf16[4,64,896]{2,1,0:T(8,128)(2,1)S(1)}, bf16[4,64,896]{2,1,0:T(8,128)(2,1)S(1)}, u32[]{:S(2)}, u32[]{:S(2)}) %collective-permute-start.6) | collective-permute-done | bytes 458784 | tf_op jit(solution)/shard_map/ppermute | solution.py:183
  186.8 3.1 %collective-permute-done.7.refs_3_ = bf16[4,64,896]{2,1,0:T(8,128)(2,1)S(1)} collective-permute-done((bf16[4,64,896]{2,1,0:T(8,128)(2,1)S(1)}, bf16[4,64,896]{2,1,0:T(8,128)(2,1)S(1)}, u32[]{:S(2)}, u32[]{:S(2)}) %collective-permute-start.7) | collective-permute-done | bytes 458784 | tf_op jit(solution)/shard_map/ppermute | solution.py:183
  189.9 0.2 shard_map.103
  190.1 4.9 %collective-permute-start.8 = (bf16[64,896]{1,0:T(8,128)(2,1)S(1)}, bf16[64,896]{1,0:T(8,128)(2,1)S(1)}, u32[]{:S(2)}, u32[]{:S(2)}) collective-permute-start(bf16[64,896]{1,0:T(8,128)(2,1)S(1)} %get-tuple-element.37), channel_id=1, source_target_pairs={{0,128},{128,256},{256,384},{384,0},{1,129},{129,257},{257,385},{3... | collective-permute-start | bytes 344072 | tf_op jit(solution)/shard_map/ppermute | solution.py:183
  195.0 2.5 %collective-permute-start.9 = (bf16[64,896]{1,0:T(8,128)(2,1)S(1)}, bf16[64,896]{1,0:T(8,128)(2,1)S(1)}, u32[]{:S(2)}, u32[]{:S(2)}) collective-permute-start(bf16[64,896]{1,0:T(8,128)(2,1)S(1)} %get-tuple-element.38), channel_id=1, source_target_pairs={{0,256},{128,384},{256,0},{384,128},{1,257},{129,385},{257,1},{385... | collective-permute-start | bytes 344072 | tf_op jit(solution)/shard_map/ppermute | solution.py:183
  197.4 4.9 %collective-permute-start.10 = (bf16[64,896]{1,0:T(8,128)(2,1)S(1)}, bf16[64,896]{1,0:T(8,128)(2,1)S(1)}, u32[]{:S(2)}, u32[]{:S(2)}) collective-permute-start(bf16[64,896]{1,0:T(8,128)(2,1)S(1)} %get-tuple-element.39), channel_id=1, source_target_pairs={{0,384},{128,0},{256,128},{384,256},{1,385},{129,1},{257,129},{385... | collective-permute-start | bytes 344072 | tf_op jit(solution)/shard_map/ppermute | solution.py:183
  202.4 0.0 collective-permute-done.8.refs_1_
  202.4 2.2 %collective-permute-done.9.refs_2_ = bf16[64,896]{1,0:T(8,128)(2,1)S(1)} collective-permute-done((bf16[64,896]{1,0:T(8,128)(2,1)S(1)}, bf16[64,896]{1,0:T(8,128)(2,1)S(1)}, u32[]{:S(2)}, u32[]{:S(2)}) %collective-permute-start.9) | collective-permute-done | bytes 114720 | tf_op jit(solution)/shard_map/ppermute | solution.py:183
  204.6 6.6 %collective-permute-done.10.refs_3_ = bf16[64,896]{1,0:T(8,128)(2,1)S(1)} collective-permute-done((bf16[64,896]{1,0:T(8,128)(2,1)S(1)}, bf16[64,896]{1,0:T(8,128)(2,1)S(1)}, u32[]{:S(2)}, u32[]{:S(2)}) %collective-permute-start.10) | collective-permute-done | bytes 114720 | tf_op jit(solution)/shard_map/ppermute | solution.py:183
  211.2 0.0 copy-done.7
  211.2 0.0 copy-done.8
  211.2 1.4 shard_map.104
  212.6 0.0 all-to-all-done.5
  212.6 0.0 collective-permute-done.2.other
  212.6 1.8 shard_map.100
Async XLA Ops:
  48.3 9.4 %collective-permute-start = (bf16[4,4,64,896]{3,2,1,0:T(8,128)(2,1)S(1)}, bf16[4,4,64,896]{3,2,1,0:T(8,128)(2,1)}, u32[]{:S(2)}, u32[]{:S(2)}) collective-permute-start(bf16[4,4,64,896]{3,2,1,0:T(8,128)(2,1)S(1)} %all_to_all.31.rest_0_), channel_id=1, source_target_pairs={{0,16},{16,0},{1,17},{17,1},{2,18},{18,2},{3,19},{19,3},{4,20},{20... | collective-permute-start | bytes 5505032 | tf_op jit(solution)/shard_map/ppermute | solution.py:179
  54.1 1.4 copy-start.2
  55.5 1.0 copy-start.6
  57.6 1.0 copy-start.5
  65.8 28.8 %copy-start.3 = (bf16[384,896]{1,0:T(8,128)(2,1)S(1)}, bf16[384,896]{1,0:T(8,128)(2,1)}, u32[]{:S(2)}) copy-start(bf16[384,896]{1,0:T(8,128)(2,1)} %get-tuple-element.29.d_both) | copy-start | bytes 2064388
  65.8 16.7 %collective-permute-start.1 = (bf16[192,1536]{1,0:T(8,128)(2,1)}, bf16[192,1536]{1,0:T(8,128)(2,1)S(1)}, u32[]{:S(2)}, u32[]{:S(2)}) collective-permute-start(bf16[192,1536]{1,0:T(8,128)(2,1)} %get-tuple-element.27), channel_id=1, source_target_pairs={{0,1},{1,0},{2,3},{3,2},{4,5},{5,4},{6,7},{7,6},{8,9},{9,8},{10,11... | collective-permute-start | bytes 1769480 | tf_op jit(solution)/shard_map/ppermute | solution.py:179
  82.6 1.1 copy-start.4
  84.6 28.2 %all-to-all-start.2 = ((bf16[8,24,1536]{2,1,0:T(8,128)(2,1)}), bf16[8,24,1536]{2,1,0:T(8,128)(2,1)S(1)}, u32[]{:S(2)}, u32[]{:S(2)}) async-start(bf16[8,24,1536]{2,1,0:T(8,128)(2,1)} %bitcast.6), calls=%async_computation.2 | async-start | bytes 1179648 | tf_op jit(solution)/shard_map/all_to_all | solution.py:269
  98.7 1.2 copy-start
  100.0 61.1 %collective-permute-start.4 = (bf16[4,4,64,896]{3,2,1,0:T(8,128)(2,1)}, bf16[4,4,64,896]{3,2,1,0:T(8,128)(2,1)}, u32[]{:S(2)}, u32[]{:S(2)}) collective-permute-start(bf16[4,4,64,896]{3,2,1,0:T(8,128)(2,1)} %get-tuple-element.31), channel_id=1, source_target_pairs={{0,16},{16,0},{1,17},{17,1},{2,18},{18,2},{3,19},{19,3},{4,20},{20... | collective-permute-start | bytes 5505032 | tf_op jit(solution)/shard_map/ppermute | solution.py:179
  112.8 15.9 %all-to-all-start.4 = ((bf16[8,48,512]{2,1,0:T(8,128)(2,1)}), bf16[8,48,512]{2,1,0:T(8,128)(2,1)S(1)}, u32[]{:S(2)}, u32[]{:S(2)}) async-start(bf16[8,48,512]{2,1,0:T(8,128)(2,1)} %bitcast.8), calls=%async_computation.4 | async-start | bytes 786432 | tf_op jit(solution)/shard_map/all_to_all | solution.py:244
  116.3 44.8 %copy-start.1 = (bf16[4,4,64,896]{3,2,1,0:T(8,128)(2,1)S(1)}, bf16[4,4,64,896]{3,2,1,0:T(8,128)(2,1)}, u32[]{:S(2)}) copy-start(bf16[4,4,64,896]{3,2,1,0:T(8,128)(2,1)} %copy-done) | copy-start | bytes 5505028
  128.7 19.7 %all-to-all-start.3 = ((bf16[8,24,1536]{2,1,0:T(8,128)(2,1)}), bf16[8,24,1536]{2,1,0:T(8,128)(2,1)S(1)}, u32[]{:S(2)}, u32[]{:S(2)}) async-start(bf16[8,24,1536]{2,1,0:T(8,128)(2,1)} %shard_map.97), calls=%async_computation.3 | async-start | bytes 1179648 | tf_op jit(solution)/shard_map/all_to_all | solution.py:274
  132.3 7.8 %collective-permute-start.3 = (bf16[48,512]{1,0:T(8,128)(2,1)S(1)}, bf16[48,512]{1,0:T(8,128)(2,1)S(1)}, u32[]{:S(2)}, u32[]{:S(2)}) collective-permute-start(bf16[48,512]{1,0:T(8,128)(2,1)S(1)} %shard_map.98.first), channel_id=1, source_target_pairs={{0,1},{1,0},{2,3},{3,2},{4,5},{5,4},{6,7},{7,6},{8,9},{9,8},{10,11... | collective-permute-start | bytes 147464 | tf_op jit(solution)/shard_map/ppermute | solution.py:179
  148.4 64.1 %all-to-all-start.5 = ((bf16[8,48,512]{2,1,0:T(8,128)(2,1)}), bf16[8,48,512]{2,1,0:T(8,128)(2,1)S(1)}, u32[]{:S(2)}, u32[]{:S(2)}) async-start(bf16[8,48,512]{2,1,0:T(8,128)(2,1)} %shard_map.99), calls=%async_computation.5 | async-start | bytes 786432 | tf_op jit(solution)/shard_map/all_to_all | solution.py:276
  151.9 60.7 %collective-permute-start.2 = (bf16[192,1536]{1,0:T(8,128)(2,1)S(1)}, bf16[192,1536]{1,0:T(8,128)(2,1)S(1)}, u32[]{:S(2)}, u32[]{:S(2)}) collective-permute-start(bf16[192,1536]{1,0:T(8,128)(2,1)S(1)} %bitcast.10), channel_id=1, source_target_pairs={{0,1},{1,0},{2,3},{3,2},{4,5},{5,4},{6,7},{7,6},{8,9},{9,8},{10,11... | collective-permute-start | bytes 1769480 | tf_op jit(solution)/shard_map/ppermute | solution.py:179
  163.0 48.2 %copy-start.7 = (s32[1,7]{1,0:T(1,128)S(1)}, s32[1,7]{1,0:T(1,128)}, u32[]{:S(2)}) copy-start(s32[1,7]{1,0:T(1,128)} %gm.1) | copy-start | bytes 88
  163.0 48.2 %copy-start.8 = (s32[1,7]{1,0:T(1,128)S(1)}, s32[1,7]{1,0:T(1,128)}, u32[]{:S(2)}) copy-start(s32[1,7]{1,0:T(1,128)} %um.1) | copy-start | bytes 88
  163.0 15.0 %collective-permute-start.5 = (bf16[4,64,896]{2,1,0:T(8,128)(2,1)S(1)}, bf16[4,64,896]{2,1,0:T(8,128)(2,1)S(1)}, u32[]{:S(2)}, u32[]{:S(2)}) collective-permute-start(bf16[4,64,896]{2,1,0:T(8,128)(2,1)S(1)} %get-tuple-element.33), channel_id=1, source_target_pairs={{0,32},{32,64},{64,96},{96,0},{1,33},{33,65},{65,97},{97,1},{2,34}... | collective-permute-start | bytes 1376264 | tf_op jit(solution)/shard_map/ppermute | solution.py:183
  165.3 21.5 %collective-permute-start.6 = (bf16[4,64,896]{2,1,0:T(8,128)(2,1)S(1)}, bf16[4,64,896]{2,1,0:T(8,128)(2,1)S(1)}, u32[]{:S(2)}, u32[]{:S(2)}) collective-permute-start(bf16[4,64,896]{2,1,0:T(8,128)(2,1)S(1)} %get-tuple-element.34), channel_id=1, source_target_pairs={{0,64},{32,96},{64,0},{96,32},{1,65},{33,97},{65,1},{97,33},{2,66}... | collective-permute-start | bytes 1376264 | tf_op jit(solution)/shard_map/ppermute | solution.py:183
  169.0 20.9 %collective-permute-start.7 = (bf16[4,64,896]{2,1,0:T(8,128)(2,1)S(1)}, bf16[4,64,896]{2,1,0:T(8,128)(2,1)S(1)}, u32[]{:S(2)}, u32[]{:S(2)}) collective-permute-start(bf16[4,64,896]{2,1,0:T(8,128)(2,1)S(1)} %get-tuple-element.35), channel_id=1, source_target_pairs={{0,96},{32,0},{64,32},{96,64},{1,97},{33,1},{65,33},{97,65},{2,98}... | collective-permute-start | bytes 1376264 | tf_op jit(solution)/shard_map/ppermute | solution.py:183
  190.1 12.3 %collective-permute-start.8 = (bf16[64,896]{1,0:T(8,128)(2,1)S(1)}, bf16[64,896]{1,0:T(8,128)(2,1)S(1)}, u32[]{:S(2)}, u32[]{:S(2)}) collective-permute-start(bf16[64,896]{1,0:T(8,128)(2,1)S(1)} %get-tuple-element.37), channel_id=1, source_target_pairs={{0,128},{128,256},{256,384},{384,0},{1,129},{129,257},{257,385},{3... | collective-permute-start | bytes 344072 | tf_op jit(solution)/shard_map/ppermute | solution.py:183
  195.0 9.6 %collective-permute-start.9 = (bf16[64,896]{1,0:T(8,128)(2,1)S(1)}, bf16[64,896]{1,0:T(8,128)(2,1)S(1)}, u32[]{:S(2)}, u32[]{:S(2)}) collective-permute-start(bf16[64,896]{1,0:T(8,128)(2,1)S(1)} %get-tuple-element.38), channel_id=1, source_target_pairs={{0,256},{128,384},{256,0},{384,128},{1,257},{129,385},{257,1},{385... | collective-permute-start | bytes 344072 | tf_op jit(solution)/shard_map/ppermute | solution.py:183
  197.4 13.7 %collective-permute-start.10 = (bf16[64,896]{1,0:T(8,128)(2,1)S(1)}, bf16[64,896]{1,0:T(8,128)(2,1)S(1)}, u32[]{:S(2)}, u32[]{:S(2)}) collective-permute-start(bf16[64,896]{1,0:T(8,128)(2,1)S(1)} %get-tuple-element.39), channel_id=1, source_target_pairs={{0,384},{128,0},{256,128},{384,256},{1,385},{129,1},{257,129},{385... | collective-permute-start | bytes 344072 | tf_op jit(solution)/shard_map/ppermute | solution.py:183

commit v8 on v4

--- a/solution.py
+++ b/solution.py
@@ -12,7 +12,7 @@
 BF16 = jnp.bfloat16
 F32 = jnp.float32
 YH, X, CORE, Z, YL = 4, 4, 2, 8, 2
-FIRST = 1536
+FIRST = 1664
 VM = pl.BlockSpec(memory_space=pltpu.VMEM)
 HB = pl.BlockSpec(memory_space=pltpu.HBM)
 SM = pl.BlockSpec(memory_space=pltpu.SMEM)
@@ -157,16 +157,32 @@
         out[copy] = total
 
 
-def join_kernel(place, mine, other, side, out):
-    half = place[1]
+def join_main_kernel(place, mine, other, out, sems):
     rows = mine.shape[0]
-    out[pl.ds(pl.multiple_of(half * rows, rows), rows), :FIRST] = mine[...]
-    out[pl.ds(pl.multiple_of((1 - half) * rows, rows), rows), :FIRST] = other[...]
-    out[:, FIRST:] = side[...]
+    moves = []
+    for part, index in ((mine, place[1]), (other, 1 - place[1])):
+        start = pl.multiple_of(index * rows, rows)
+        target = out.at[pl.ds(start, rows), pl.ds(0, FIRST)]
+        moves.append(pltpu.make_async_copy(part, target, sems.at[len(moves)]))
+    for move in moves:
+        move.start()
+    for move in moves:
+        move.wait()
+
+
+def join_side_kernel(side, before, out, sem):
+    rest = side.shape[1]
+    move = pltpu.make_async_copy(side, out.at[:, pl.ds(FIRST, rest)], sem)
+    move.start()
+    move.wait()
 
 
 def shape(dims, dtype=BF16):
     return jax.ShapeDtypeStruct(dims, dtype)
+
+
+def far(dims):
+    return pltpu.HBM(dims, BF16)
 
 
 def params():
@@ -227,10 +243,10 @@
         forward_kernel,
         [
             shape((width, count), F32),
-            shape((count, 2 * width)),
-            shape((half, FIRST)),
-            shape((half, FIRST)),
-            shape((count, rest)),
+            far((count, 2 * width)),
+            far((half, FIRST)),
+            far((half, FIRST)),
+            far((count, rest)),
         ],
         place,
         tokens,
@@ -274,9 +290,23 @@
     main = lax.all_to_all(main, "z", 0, 0, tiled=True).reshape(half, FIRST)
     main_other = swap(main, "yl")
     side = lax.all_to_all(side, "z", 0, 0, tiled=True).reshape(count, rest)
-    grad_tokens = call(
-        join_kernel, shape((count, features)), place, main, main_other, side, scalars=1
-    )
+    grad_tokens = pl.pallas_call(
+        join_main_kernel,
+        in_specs=[SM, VM, VM],
+        out_specs=HB,
+        out_shape=far((count, features)),
+        scratch_shapes=[pltpu.SemaphoreType.DMA((2,))],
+        compiler_params=params(),
+    )(place, main, main_other)
+    grad_tokens = pl.pallas_call(
+        join_side_kernel,
+        in_specs=[VM, HB],
+        out_specs=HB,
+        out_shape=far((count, features)),
+        scratch_shapes=[pltpu.SemaphoreType.DMA],
+        input_output_aliases={1: 0},
+        compiler_params=params(),
+    )(side, grad_tokens)
     return (hidden_t.T, grad_tokens, grad_gate, grad_up)
 
 

time: 217 us -> 203 us (0.935)
  waiting for transfers between devices: 102 us -> 63.5 us
  blocking collectives: 21 us -> 43.1 us
    all_to_all x0 -> x1, blocking collectives: none -> 22.1 us  [compute(): main = lax.all_to_all(main, 'z', 0, 0, tiled=True).reshape(half, FIRST)]
    all_to_all x1, waiting for transfers between devices: 14.2 us -> 0.01 us  [compute(): lax.all_to_all(side.reshape(Z, 2 * chunk, rest), 'z', 0, 0, tiled=True)]
    all_to_all x1 -> x0, waiting for transfers between devices: 13.3 us -> none  [compute(): main = lax.all_to_all(main, 'z', 0, 0, tiled=True).reshape(half, FIRST)]
    ppermute x9, waiting for transfers between devices: 45.6 us -> 32.9 us  [shift(): lax.ppermute(array, axis, [(i, (i + steps) % size) for i in range(size)])]
    all_to_all x1 -> x0, starting transfers between devices: 3.54 us -> none  [compute(): main = lax.all_to_all(main, 'z', 0, 0, tiled=True).reshape(half, FIRST)]
    all_to_all x1, starting transfers between devices: 3.45 us -> 6.55 us  [compute(): side = lax.all_to_all(side, 'z', 0, 0, tiled=True).reshape(count, rest)]
    pallas_call x0 -> x2, Pallas kernels: none -> 2.88 us  [the longest x1 2.15 us: compute(): pl.pallas_call(join_main_kernel, in_specs=[SM, VM, VM], out_specs=HB, out...]
    pallas_call x11 -> x10, Pallas kernels: 19.6 us -> 17.7 us  [call(): pl.pallas_call(kernel, in_specs=[SM] * scalars + [VM] * (len(operands) -...]
  transfers between devices with their start and end apart: 21 -> 20, of which waited for: 11 -> 7; matrix products, arithmetic and copies ran while one was open for 0% -> 0% of each run, Pallas kernels for 4% -> 6%
where the time goes in v8:
time: 203 us; the launch traced here: 202 us
  starting transfers between devices  66.2 us (33%)
  waiting for transfers between devices  63.5 us (31%)
  blocking collectives  43.1 us (21%)
  Pallas kernels  22.3 us (11%)
  local copies, waits for them, and re-layouts  5.52 us (3%)
    ppermute x9, waiting for transfers between devices, shift(): lax.ppermute(array, axis, [(i, (i + steps) % size) for i in range(size)])  32.9 us
    ppermute x9, starting transfers between devices, shift(): lax.ppermute(array, axis, [(i, (i + steps) % size) for i in range(size)])  24.9 us
    all_to_all x1, blocking collectives, compute(): main = lax.all_to_all(main, 'z', 0, 0, tiled=True).reshape(half, FIRST)  22.1 us
    ppermute x8, starting transfers between devices, swap(): return lax.ppermute(array, axis, [(0, 1), (1, 0)])  21.3 us
    all_to_all x1, blocking collectives, compute(): rows = lax.all_to_all(copies, 'yh', 0, 0, tiled=True)  21 us
    ppermute x8, waiting for transfers between devices, swap(): return lax.ppermute(array, axis, [(0, 1), (1, 0)])  18.5 us
    pallas_call x10, Pallas kernels, call(): pl.pallas_call(kernel, in_specs=[SM] * scalars + [VM] * (len(operands) -...  17.7 us
    all_to_all x1, waiting for transfers between devices, compute(): main = lax.all_to_all(main.reshape(Z, chunk, FIRST), 'z', 0, 0, tiled=True)  12 us
  transfers between devices with their start and end apart: 20, of which 7 were waited for; matrix products, arithmetic and copies ran while one was open for 0% of the time, Pallas kernels for 6%

profile of v8, /device:TPU:23, one launch (start us, length us, event | category | flops | bytes accessed | tf_op | source)
XLA Modules:
  0.0 201.7 jit_solution(13402659646001658959)
XLA Ops:
  0.6 1.8 shard_map.94
  2.4 21.0 %all_to_all.25.rest_0_ = bf16[4,64,896]{2,1,0:T(8,128)(2,1)S(1)} all-to-all(bf16[4,64,896]{2,1,0:T(8,128)(2,1)} %shard_map.94), channel_id=1, replica_groups=mesh['yh'=4,'x'=4,'core'=2,'z'=8,'yl'=2] {'yh'}, dimensions={0} | all-to-all | bytes 917504 | tf_op jit(solution)/shard_map/all_to_all | solution.py:233
  23.4 2.4 %collective-permute-start.2 = (bf16[4,64,896]{2,1,0:T(8,128)(2,1)S(1)}, bf16[4,64,896]{2,1,0:T(8,128)(2,1)S(1)}, u32[]{:S(2)}, u32[]{:S(2)}) collective-permute-start(bf16[4,64,896]{2,1,0:T(8,128)(2,1)S(1)} %all_to_all.25.rest_0_), channel_id=1, source_target_pairs={{0,96},{32,0},{64,32},{96,64},{1,97},{33,1},{65,33},{97,65},{2,98}... | collective-permute-start | bytes 1376264 | tf_op jit(solution)/shard_map/ppermute | solution.py:197
  25.9 2.6 %collective-permute-start.1 = (bf16[4,64,896]{2,1,0:T(8,128)(2,1)S(1)}, bf16[4,64,896]{2,1,0:T(8,128)(2,1)S(1)}, u32[]{:S(2)}, u32[]{:S(2)}) collective-permute-start(bf16[4,64,896]{2,1,0:T(8,128)(2,1)S(1)} %all_to_all.25.rest_0_), channel_id=1, source_target_pairs={{0,64},{32,96},{64,0},{96,32},{1,65},{33,97},{65,1},{97,33},{2,66}... | collective-permute-start | bytes 1376264 | tf_op jit(solution)/shard_map/ppermute | solution.py:197
  28.5 3.8 %collective-permute-start = (bf16[4,64,896]{2,1,0:T(8,128)(2,1)S(1)}, bf16[4,64,896]{2,1,0:T(8,128)(2,1)S(1)}, u32[]{:S(2)}, u32[]{:S(2)}) collective-permute-start(bf16[4,64,896]{2,1,0:T(8,128)(2,1)S(1)} %all_to_all.25.rest_0_), channel_id=1, source_target_pairs={{0,32},{32,64},{64,96},{96,0},{1,33},{33,65},{65,97},{97,1},{2,34}... | collective-permute-start | bytes 1376264 | tf_op jit(solution)/shard_map/ppermute | solution.py:197
  32.4 3.4 %collective-permute-start.3 = (bf16[4,64,896]{2,1,0:T(8,128)(2,1)S(1)}, bf16[4,64,896]{2,1,0:T(8,128)(2,1)}, u32[]{:S(2)}, u32[]{:S(2)}) collective-permute-start(bf16[4,64,896]{2,1,0:T(8,128)(2,1)S(1)} %all_to_all.25.rest_0_), channel_id=1, source_target_pairs={{0,16},{16,0},{1,17},{17,1},{2,18},{18,2},{3,19},{19,3},{4,20},{20... | collective-permute-start | bytes 1376264 | tf_op jit(solution)/shard_map/ppermute | solution.py:193
  35.8 12.1 %collective-permute-done.2.rest_3_ = bf16[4,64,896]{2,1,0:T(8,128)(2,1)S(1)} collective-permute-done((bf16[4,64,896]{2,1,0:T(8,128)(2,1)S(1)}, bf16[4,64,896]{2,1,0:T(8,128)(2,1)S(1)}, u32[]{:S(2)}, u32[]{:S(2)}) %collective-permute-start.2) | collective-permute-done | bytes 458784 | tf_op jit(solution)/shard_map/ppermute | solution.py:197
  47.8 3.4 %collective-permute-start.6 = (bf16[4,64,896]{2,1,0:T(8,128)(2,1)S(1)}, bf16[4,64,896]{2,1,0:T(8,128)(2,1)}, u32[]{:S(2)}, u32[]{:S(2)}) collective-permute-start(bf16[4,64,896]{2,1,0:T(8,128)(2,1)S(1)} %collective-permute-done.2.rest_3_), channel_id=1, source_target_pairs={{0,16},{16,0},{1,17},{17,1},{2,18},{18,2},{3,19},{19,3},{4,20},{20... | collective-permute-start | bytes 1376264 | tf_op jit(solution)/shard_map/ppermute | solution.py:193
  51.2 0.0 collective-permute-done.1.rest_2_
  51.2 1.9 collective-permute-start.5
  53.2 0.0 collective-permute-done.rest_1_
  53.2 2.4 %collective-permute-start.4 = (bf16[4,64,896]{2,1,0:T(8,128)(2,1)S(1)}, bf16[4,64,896]{2,1,0:T(8,128)(2,1)}, u32[]{:S(2)}, u32[]{:S(2)}) collective-permute-start(bf16[4,64,896]{2,1,0:T(8,128)(2,1)S(1)} %collective-permute-done.rest_1_), channel_id=1, source_target_pairs={{0,16},{16,0},{1,17},{17,1},{2,18},{18,2},{3,19},{19,3},{4,20},{20... | collective-permute-start | bytes 1376264 | tf_op jit(solution)/shard_map/ppermute | solution.py:193
  55.6 0.0 copy-start.2
  55.6 1.4 copy-done.2
  57.0 1.0 copy-done.7
  58.0 0.2 shard_map.93
  58.2 0.1 pad_add_fusion.place
  58.3 0.0 collective-permute-done.3.rest_4_
  58.3 0.0 collective-permute-done.6.rest_7_
  58.3 0.0 collective-permute-done.5.rest_6_
  58.3 0.0 collective-permute-done.4.rest_5_
  58.3 7.2 %shard_map.95 = (f32[448,384]{1,0:T(8,128)}, bf16[384,896]{1,0:T(8,128)(2,1)}, bf16[192,1664]{1,0:T(8,128)(2,1)}, bf16[192,1664]{1,0:T(8,128)(2,1)}, bf16[384,384]{1,0:T(8,128)(2,1)}) custom-call(s32[4]{0:T(128)S(1)} %pad_add_fusion.place, bf16[384,2048]{1,0:T(8,128)(2,1)S(1)} %get-tuple-element.23.tokens, f32[384,448]{1,0:T(8,128)S(1)} %get-tuple-element.24.grad_ref, ...), custom_call_target="tpu_custom_call" | custom-call | tf_op jit(solution)/shard_map/pallas_call | solution.py:202
  65.5 1.9 collective-permute-start.8
  67.5 16.1 %collective-permute-done.8.second = bf16[192,1664]{1,0:T(8,128)(2,1)S(1)} collective-permute-done((bf16[192,1664]{1,0:T(8,128)(2,1)}, bf16[192,1664]{1,0:T(8,128)(2,1)S(1)}, u32[]{:S(2)}, u32[]{:S(2)}) %collective-permute-start.8) | collective-permute-done | bytes 639008 | tf_op jit(solution)/shard_map/ppermute | solution.py:193
  83.6 1.1 copy-done.4
  84.6 1.0 shard_map.98
  85.6 10.0 %all-to-all-start.3 = ((bf16[8,24,1664]{2,1,0:T(8,128)(2,1)}), bf16[8,24,1664]{2,1,0:T(8,128)(2,1)S(1)}, u32[]{:S(2)}, u32[]{:S(2)}) async-start(bf16[8,24,1664]{2,1,0:T(8,128)(2,1)} %bitcast.8), calls=%async_computation.3 | async-start | bytes 1277952 | tf_op jit(solution)/shard_map/all_to_all | solution.py:285
  95.7 4.0 %shard_map.102 = (bf16[4,4,64,896]{3,2,1,0:T(8,128)(2,1)S(1)}, bf16[4,4,64,896]{3,2,1,0:T(8,128)(2,1)}) custom-call(s32[4]{0:T(128)S(1)} %pad_add_fusion.place, bf16[384,2048]{1,0:T(8,128)(2,1)S(1)} %get-tuple-element.23.tokens, bf16[384,896]{1,0:T(8,128)(2,1)S(1)} %copy-done.3), custom_call_target="tpu_custom_call" | custom-call | tf_op jit(solution)/shard_map/pallas_call | solution.py:202
  99.7 1.3 copy-done
  101.0 3.0 %collective-permute-start.10 = (bf16[4,4,64,896]{3,2,1,0:T(8,128)(2,1)}, bf16[4,4,64,896]{3,2,1,0:T(8,128)(2,1)}, u32[]{:S(2)}, u32[]{:S(2)}) collective-permute-start(bf16[4,4,64,896]{3,2,1,0:T(8,128)(2,1)} %get-tuple-element.31), channel_id=1, source_target_pairs={{0,16},{16,0},{1,17},{17,1},{2,18},{18,2},{3,19},{19,3},{4,20},{20... | collective-permute-start | bytes 5505032 | tf_op jit(solution)/shard_map/ppermute | solution.py:193
  104.0 12.0 %all-to-all-done.3.parts = bf16[8,24,1664]{2,1,0:T(8,128)(2,1)S(1)} async-done(((bf16[8,24,1664]{2,1,0:T(8,128)(2,1)}), bf16[8,24,1664]{2,1,0:T(8,128)(2,1)S(1)}, u32[]{:S(2)}, u32[]{:S(2)}) %all-to-all-start.3) | async-done | bytes 639008 | tf_op jit(solution)/shard_map/all_to_all | solution.py:285
  116.1 0.1 shard_map.99
  116.2 0.0 copy-start.1
  116.2 22.1 %all_to_all.26 = bf16[8,24,1664]{2,1,0:T(8,128)(2,1)S(1)} all-to-all(bf16[8,24,1664]{2,1,0:T(8,128)(2,1)S(1)} %shard_map.99), channel_id=1, replica_groups=mesh['yh'=4,'x'=4,'core'=2,'z'=8,'yl'=2] {'z'}, dimensions={0} | all-to-all | bytes 1277952 | tf_op jit(solution)/shard_map/all_to_all | solution.py:290
  138.3 3.4 %all-to-all-start.1 = ((bf16[8,48,384]{2,1,0:T(8,128)(2,1)}), bf16[8,48,384]{2,1,0:T(8,128)(2,1)S(1)}, u32[]{:S(2)}, u32[]{:S(2)}) async-start(bf16[8,48,384]{2,1,0:T(8,128)(2,1)} %bitcast.6), calls=%async_computation.1 | async-start | bytes 589824 | tf_op jit(solution)/shard_map/all_to_all | solution.py:260
  141.7 2.2 %collective-permute-start.9 = (bf16[192,1664]{1,0:T(8,128)(2,1)S(1)}, bf16[192,1664]{1,0:T(8,128)(2,1)}, u32[]{:S(2)}, u32[]{:S(2)}) collective-permute-start(bf16[192,1664]{1,0:T(8,128)(2,1)S(1)} %bitcast.10), channel_id=1, source_target_pairs={{0,1},{1,0},{2,3},{3,2},{4,5},{5,4},{6,7},{7,6},{8,9},{9,8},{10,11... | collective-permute-start | bytes 1916936 | tf_op jit(solution)/shard_map/ppermute | solution.py:193
  143.9 0.0 collective-permute-done.10.second
  143.9 2.7 %shard_map.103 = (bf16[4,64,896]{2,1,0:T(8,128)(2,1)S(1)}, bf16[4,64,896]{2,1,0:T(8,128)(2,1)}, bf16[4,64,896]{2,1,0:T(8,128)(2,1)}, bf16[4,64,896]{2,1,0:T(8,128)(2,1)}) custom-call(bf16[4,4,64,896]{3,2,1,0:T(8,128)(2,1)S(1)} %copy-done.1, bf16[4,4,64,896]{3,2,1,0:T(8,128)(2,1)} %collective-permute-done.10.second), custom_call_target="tpu_custom_call" | custom-call | tf_op jit(solution)/shard_map/pallas_call | solution.py:202
  146.6 0.8 copy-done.5
  147.4 2.5 %collective-permute-start.11 = (bf16[4,64,896]{2,1,0:T(8,128)(2,1)}, bf16[4,64,896]{2,1,0:T(8,128)(2,1)S(1)}, u32[]{:S(2)}, u32[]{:S(2)}) collective-permute-start(bf16[4,64,896]{2,1,0:T(8,128)(2,1)} %get-tuple-element.33), channel_id=1, source_target_pairs={{0,32},{32,64},{64,96},{96,0},{1,33},{33,65},{65,97},{97,1},{2,34}... | collective-permute-start | bytes 1376264 | tf_op jit(solution)/shard_map/ppermute | solution.py:197
  150.0 1.9 collective-permute-start.12
  151.9 2.9 %collective-permute-start.13 = (bf16[4,64,896]{2,1,0:T(8,128)(2,1)}, bf16[4,64,896]{2,1,0:T(8,128)(2,1)S(1)}, u32[]{:S(2)}, u32[]{:S(2)}) collective-permute-start(bf16[4,64,896]{2,1,0:T(8,128)(2,1)} %get-tuple-element.35), channel_id=1, source_target_pairs={{0,96},{32,0},{64,32},{96,64},{1,97},{33,1},{65,33},{97,65},{2,98}... | collective-permute-start | bytes 1376264 | tf_op jit(solution)/shard_map/ppermute | solution.py:197
  154.8 0.0 all-to-all-done.1.parts
  154.8 3.1 %collective-permute-start.7 = (bf16[48,384]{1,0:T(8,128)(2,1)S(1)}, bf16[48,384]{1,0:T(8,128)(2,1)S(1)}, u32[]{:S(2)}, u32[]{:S(2)}) collective-permute-start(bf16[48,384]{1,0:T(8,128)(2,1)S(1)} %shard_map.96.first), channel_id=1, source_target_pairs={{0,1},{1,0},{2,3},{3,2},{4,5},{5,4},{6,7},{7,6},{8,9},{9,8},{10,11... | collective-permute-start | bytes 110600 | tf_op jit(solution)/shard_map/ppermute | solution.py:193
  157.9 2.4 %collective-permute-done.7.second = bf16[48,384]{1,0:T(8,128)(2,1)S(1)} collective-permute-done((bf16[48,384]{1,0:T(8,128)(2,1)S(1)}, bf16[48,384]{1,0:T(8,128)(2,1)S(1)}, u32[]{:S(2)}, u32[]{:S(2)}) %collective-permute-start.7) | collective-permute-done | bytes 36896 | tf_op jit(solution)/shard_map/ppermute | solution.py:193
  160.3 0.7 shard_map.97
  161.1 6.6 %all-to-all-start.2 = ((bf16[8,48,384]{2,1,0:T(8,128)(2,1)}), bf16[8,48,384]{2,1,0:T(8,128)(2,1)S(1)}, u32[]{:S(2)}, u32[]{:S(2)}) async-start(bf16[8,48,384]{2,1,0:T(8,128)(2,1)} %shard_map.97), calls=%async_computation.2 | async-start | bytes 589824 | tf_op jit(solution)/shard_map/all_to_all | solution.py:292
  167.6 0.0 collective-permute-done.11.refs_1_
  167.6 0.0 collective-permute-done.12.refs_2_
  167.6 8.2 %collective-permute-done.13.refs_3_ = bf16[4,64,896]{2,1,0:T(8,128)(2,1)S(1)} collective-permute-done((bf16[4,64,896]{2,1,0:T(8,128)(2,1)}, bf16[4,64,896]{2,1,0:T(8,128)(2,1)S(1)}, u32[]{:S(2)}, u32[]{:S(2)}) %collective-permute-start.13) | collective-permute-done | bytes 458784 | tf_op jit(solution)/shard_map/ppermute | solution.py:197
  175.9 0.0 copy-done.6
  175.9 0.2 shard_map.104
  176.1 2.2 %collective-permute-start.14 = (bf16[64,896]{1,0:T(8,128)(2,1)S(1)}, bf16[64,896]{1,0:T(8,128)(2,1)S(1)}, u32[]{:S(2)}, u32[]{:S(2)}) collective-permute-start(bf16[64,896]{1,0:T(8,128)(2,1)S(1)} %get-tuple-element.37), channel_id=1, source_target_pairs={{0,128},{128,256},{256,384},{384,0},{1,129},{129,257},{257,385},{3... | collective-permute-start | bytes 344072 | tf_op jit(solution)/shard_map/ppermute | solution.py:197
  178.3 4.4 %collective-permute-start.15 = (bf16[64,896]{1,0:T(8,128)(2,1)S(1)}, bf16[64,896]{1,0:T(8,128)(2,1)S(1)}, u32[]{:S(2)}, u32[]{:S(2)}) collective-permute-start(bf16[64,896]{1,0:T(8,128)(2,1)S(1)} %get-tuple-element.38), channel_id=1, source_target_pairs={{0,256},{128,384},{256,0},{384,128},{1,257},{129,385},{257,1},{385... | collective-permute-start | bytes 344072 | tf_op jit(solution)/shard_map/ppermute | solution.py:197
  182.7 2.1 %collective-permute-start.16 = (bf16[64,896]{1,0:T(8,128)(2,1)S(1)}, bf16[64,896]{1,0:T(8,128)(2,1)S(1)}, u32[]{:S(2)}, u32[]{:S(2)}) collective-permute-start(bf16[64,896]{1,0:T(8,128)(2,1)S(1)} %get-tuple-element.39), channel_id=1, source_target_pairs={{0,384},{128,0},{256,128},{384,256},{1,385},{129,1},{257,129},{385... | collective-permute-start | bytes 344072 | tf_op jit(solution)/shard_map/ppermute | solution.py:197
  184.8 0.0 collective-permute-done.14.refs_1_
  184.8 3.4 %collective-permute-done.15.refs_2_ = bf16[64,896]{1,0:T(8,128)(2,1)S(1)} collective-permute-done((bf16[64,896]{1,0:T(8,128)(2,1)S(1)}, bf16[64,896]{1,0:T(8,128)(2,1)S(1)}, u32[]{:S(2)}, u32[]{:S(2)}) %collective-permute-start.15) | collective-permute-done | bytes 114720 | tf_op jit(solution)/shard_map/ppermute | solution.py:197
  188.2 9.2 %collective-permute-done.16.refs_3_ = bf16[64,896]{1,0:T(8,128)(2,1)S(1)} collective-permute-done((bf16[64,896]{1,0:T(8,128)(2,1)S(1)}, bf16[64,896]{1,0:T(8,128)(2,1)S(1)}, u32[]{:S(2)}, u32[]{:S(2)}) %collective-permute-start.16) | collective-permute-done | bytes 114720 | tf_op jit(solution)/shard_map/ppermute | solution.py:197
  197.4 0.0 copy-done.9
  197.4 1.4 shard_map.105
  198.8 0.0 collective-permute-done.9.other
  198.8 2.2 %shard_map.100.before = bf16[384,2048]{1,0:T(8,128)(2,1)} custom-call(s32[4]{0:T(128)S(1)} %pad_add_fusion.place, bf16[192,1664]{1,0:T(8,128)(2,1)S(1)} %bitcast.11, bf16[192,1664]{1,0:T(8,128)(2,1)} %collective-permute-done.9.other), custom_call_target="tpu_custom_call" | custom-call | tf_op jit(solution)/shard_map/pallas_call | solution.py:293
  201.0 0.0 all-to-all-done.2
  201.0 0.7 shard_map.101
  (12 shorter events, 0.1 us)
Async XLA Ops:
  23.4 24.4 %collective-permute-start.2 = (bf16[4,64,896]{2,1,0:T(8,128)(2,1)S(1)}, bf16[4,64,896]{2,1,0:T(8,128)(2,1)S(1)}, u32[]{:S(2)}, u32[]{:S(2)}) collective-permute-start(bf16[4,64,896]{2,1,0:T(8,128)(2,1)S(1)} %all_to_all.25.rest_0_), channel_id=1, source_target_pairs={{0,96},{32,0},{64,32},{96,64},{1,97},{33,1},{65,33},{97,65},{2,98}... | collective-permute-start | bytes 1376264 | tf_op jit(solution)/shard_map/ppermute | solution.py:197
  25.9 25.3 %collective-permute-start.1 = (bf16[4,64,896]{2,1,0:T(8,128)(2,1)S(1)}, bf16[4,64,896]{2,1,0:T(8,128)(2,1)S(1)}, u32[]{:S(2)}, u32[]{:S(2)}) collective-permute-start(bf16[4,64,896]{2,1,0:T(8,128)(2,1)S(1)} %all_to_all.25.rest_0_), channel_id=1, source_target_pairs={{0,64},{32,96},{64,0},{96,32},{1,65},{33,97},{65,1},{97,33},{2,66}... | collective-permute-start | bytes 1376264 | tf_op jit(solution)/shard_map/ppermute | solution.py:197
  28.5 24.6 %collective-permute-start = (bf16[4,64,896]{2,1,0:T(8,128)(2,1)S(1)}, bf16[4,64,896]{2,1,0:T(8,128)(2,1)S(1)}, u32[]{:S(2)}, u32[]{:S(2)}) collective-permute-start(bf16[4,64,896]{2,1,0:T(8,128)(2,1)S(1)} %all_to_all.25.rest_0_), channel_id=1, source_target_pairs={{0,32},{32,64},{64,96},{96,0},{1,33},{33,65},{65,97},{97,1},{2,34}... | collective-permute-start | bytes 1376264 | tf_op jit(solution)/shard_map/ppermute | solution.py:197
  32.4 25.9 %collective-permute-start.3 = (bf16[4,64,896]{2,1,0:T(8,128)(2,1)S(1)}, bf16[4,64,896]{2,1,0:T(8,128)(2,1)}, u32[]{:S(2)}, u32[]{:S(2)}) collective-permute-start(bf16[4,64,896]{2,1,0:T(8,128)(2,1)S(1)} %all_to_all.25.rest_0_), channel_id=1, source_target_pairs={{0,16},{16,0},{1,17},{17,1},{2,18},{18,2},{3,19},{19,3},{4,20},{20... | collective-permute-start | bytes 1376264 | tf_op jit(solution)/shard_map/ppermute | solution.py:193
  47.8 10.5 %collective-permute-start.6 = (bf16[4,64,896]{2,1,0:T(8,128)(2,1)S(1)}, bf16[4,64,896]{2,1,0:T(8,128)(2,1)}, u32[]{:S(2)}, u32[]{:S(2)}) collective-permute-start(bf16[4,64,896]{2,1,0:T(8,128)(2,1)S(1)} %collective-permute-done.2.rest_3_), channel_id=1, source_target_pairs={{0,16},{16,0},{1,17},{17,1},{2,18},{18,2},{3,19},{19,3},{4,20},{20... | collective-permute-start | bytes 1376264 | tf_op jit(solution)/shard_map/ppermute | solution.py:193
  51.2 7.1 %collective-permute-start.5 = (bf16[4,64,896]{2,1,0:T(8,128)(2,1)S(1)}, bf16[4,64,896]{2,1,0:T(8,128)(2,1)}, u32[]{:S(2)}, u32[]{:S(2)}) collective-permute-start(bf16[4,64,896]{2,1,0:T(8,128)(2,1)S(1)} %collective-permute-done.1.rest_2_), channel_id=1, source_target_pairs={{0,16},{16,0},{1,17},{17,1},{2,18},{18,2},{3,19},{19,3},{4,20},{20... | collective-permute-start | bytes 1376264 | tf_op jit(solution)/shard_map/ppermute | solution.py:193
  53.2 5.2 %collective-permute-start.4 = (bf16[4,64,896]{2,1,0:T(8,128)(2,1)S(1)}, bf16[4,64,896]{2,1,0:T(8,128)(2,1)}, u32[]{:S(2)}, u32[]{:S(2)}) collective-permute-start(bf16[4,64,896]{2,1,0:T(8,128)(2,1)S(1)} %collective-permute-done.rest_1_), channel_id=1, source_target_pairs={{0,16},{16,0},{1,17},{17,1},{2,18},{18,2},{3,19},{19,3},{4,20},{20... | collective-permute-start | bytes 1376264 | tf_op jit(solution)/shard_map/ppermute | solution.py:193
  55.6 1.4 copy-start.2
  57.0 1.0 copy-start.7
  65.5 18.0 %collective-permute-start.8 = (bf16[192,1664]{1,0:T(8,128)(2,1)}, bf16[192,1664]{1,0:T(8,128)(2,1)S(1)}, u32[]{:S(2)}, u32[]{:S(2)}) collective-permute-start(bf16[192,1664]{1,0:T(8,128)(2,1)} %get-tuple-element.28), channel_id=1, source_target_pairs={{0,1},{1,0},{2,3},{3,2},{4,5},{5,4},{6,7},{7,6},{8,9},{9,8},{10,11... | collective-permute-start | bytes 1916936 | tf_op jit(solution)/shard_map/ppermute | solution.py:193
  83.6 1.1 copy-start.4
  84.6 11.0 %copy-start.3 = (bf16[384,896]{1,0:T(8,128)(2,1)S(1)}, bf16[384,896]{1,0:T(8,128)(2,1)}, u32[]{:S(2)}) copy-start(bf16[384,896]{1,0:T(8,128)(2,1)} %get-tuple-element.29.d_both) | copy-start | bytes 2064388
  85.6 30.5 %all-to-all-start.3 = ((bf16[8,24,1664]{2,1,0:T(8,128)(2,1)}), bf16[8,24,1664]{2,1,0:T(8,128)(2,1)S(1)}, u32[]{:S(2)}, u32[]{:S(2)}) async-start(bf16[8,24,1664]{2,1,0:T(8,128)(2,1)} %bitcast.8), calls=%async_computation.3 | async-start | bytes 1277952 | tf_op jit(solution)/shard_map/all_to_all | solution.py:285
  99.7 1.3 copy-start
  101.0 42.9 %collective-permute-start.10 = (bf16[4,4,64,896]{3,2,1,0:T(8,128)(2,1)}, bf16[4,4,64,896]{3,2,1,0:T(8,128)(2,1)}, u32[]{:S(2)}, u32[]{:S(2)}) collective-permute-start(bf16[4,4,64,896]{3,2,1,0:T(8,128)(2,1)} %get-tuple-element.31), channel_id=1, source_target_pairs={{0,16},{16,0},{1,17},{17,1},{2,18},{18,2},{3,19},{19,3},{4,20},{20... | collective-permute-start | bytes 5505032 | tf_op jit(solution)/shard_map/ppermute | solution.py:193
  116.2 27.8 %copy-start.1 = (bf16[4,4,64,896]{3,2,1,0:T(8,128)(2,1)S(1)}, bf16[4,4,64,896]{3,2,1,0:T(8,128)(2,1)}, u32[]{:S(2)}) copy-start(bf16[4,4,64,896]{3,2,1,0:T(8,128)(2,1)} %copy-done) | copy-start | bytes 5505028
  138.3 16.5 %all-to-all-start.1 = ((bf16[8,48,384]{2,1,0:T(8,128)(2,1)}), bf16[8,48,384]{2,1,0:T(8,128)(2,1)S(1)}, u32[]{:S(2)}, u32[]{:S(2)}) async-start(bf16[8,48,384]{2,1,0:T(8,128)(2,1)} %bitcast.6), calls=%async_computation.1 | async-start | bytes 589824 | tf_op jit(solution)/shard_map/all_to_all | solution.py:260
  141.7 57.1 %collective-permute-start.9 = (bf16[192,1664]{1,0:T(8,128)(2,1)S(1)}, bf16[192,1664]{1,0:T(8,128)(2,1)}, u32[]{:S(2)}, u32[]{:S(2)}) collective-permute-start(bf16[192,1664]{1,0:T(8,128)(2,1)S(1)} %bitcast.10), channel_id=1, source_target_pairs={{0,1},{1,0},{2,3},{3,2},{4,5},{5,4},{6,7},{7,6},{8,9},{9,8},{10,11... | collective-permute-start | bytes 1916936 | tf_op jit(solution)/shard_map/ppermute | solution.py:193
  146.6 0.8 copy-start.5
  147.4 50.0 %copy-start.8 = (s32[1,7]{1,0:T(1,128)S(1)}, s32[1,7]{1,0:T(1,128)}, u32[]{:S(2)}) copy-start(s32[1,7]{1,0:T(1,128)} %gm.1) | copy-start | bytes 88
  147.4 50.0 %copy-start.9 = (s32[1,7]{1,0:T(1,128)S(1)}, s32[1,7]{1,0:T(1,128)}, u32[]{:S(2)}) copy-start(s32[1,7]{1,0:T(1,128)} %um.1) | copy-start | bytes 88
  147.4 28.4 %copy-start.6 = (bf16[4,64,896]{2,1,0:T(8,128)(2,1)S(1)}, bf16[4,64,896]{2,1,0:T(8,128)(2,1)}, u32[]{:S(2)}) copy-start(bf16[4,64,896]{2,1,0:T(8,128)(2,1)} %copy-done.5) | copy-start | bytes 1376260
  147.4 20.2 %collective-permute-start.11 = (bf16[4,64,896]{2,1,0:T(8,128)(2,1)}, bf16[4,64,896]{2,1,0:T(8,128)(2,1)S(1)}, u32[]{:S(2)}, u32[]{:S(2)}) collective-permute-start(bf16[4,64,896]{2,1,0:T(8,128)(2,1)} %get-tuple-element.33), channel_id=1, source_target_pairs={{0,32},{32,64},{64,96},{96,0},{1,33},{33,65},{65,97},{97,1},{2,34}... | collective-permute-start | bytes 1376264 | tf_op jit(solution)/shard_map/ppermute | solution.py:197
  150.0 17.6 %collective-permute-start.12 = (bf16[4,64,896]{2,1,0:T(8,128)(2,1)}, bf16[4,64,896]{2,1,0:T(8,128)(2,1)S(1)}, u32[]{:S(2)}, u32[]{:S(2)}) collective-permute-start(bf16[4,64,896]{2,1,0:T(8,128)(2,1)} %get-tuple-element.34), channel_id=1, source_target_pairs={{0,64},{32,96},{64,0},{96,32},{1,65},{33,97},{65,1},{97,33},{2,66}... | collective-permute-start | bytes 1376264 | tf_op jit(solution)/shard_map/ppermute | solution.py:197
  151.9 24.0 %collective-permute-start.13 = (bf16[4,64,896]{2,1,0:T(8,128)(2,1)}, bf16[4,64,896]{2,1,0:T(8,128)(2,1)S(1)}, u32[]{:S(2)}, u32[]{:S(2)}) collective-permute-start(bf16[4,64,896]{2,1,0:T(8,128)(2,1)} %get-tuple-element.35), channel_id=1, source_target_pairs={{0,96},{32,0},{64,32},{96,64},{1,97},{33,1},{65,33},{97,65},{2,98}... | collective-permute-start | bytes 1376264 | tf_op jit(solution)/shard_map/ppermute | solution.py:197
  154.8 5.5 %collective-permute-start.7 = (bf16[48,384]{1,0:T(8,128)(2,1)S(1)}, bf16[48,384]{1,0:T(8,128)(2,1)S(1)}, u32[]{:S(2)}, u32[]{:S(2)}) collective-permute-start(bf16[48,384]{1,0:T(8,128)(2,1)S(1)} %shard_map.96.first), channel_id=1, source_target_pairs={{0,1},{1,0},{2,3},{3,2},{4,5},{5,4},{6,7},{7,6},{8,9},{9,8},{10,11... | collective-permute-start | bytes 110600 | tf_op jit(solution)/shard_map/ppermute | solution.py:193
  161.1 39.9 %all-to-all-start.2 = ((bf16[8,48,384]{2,1,0:T(8,128)(2,1)}), bf16[8,48,384]{2,1,0:T(8,128)(2,1)S(1)}, u32[]{:S(2)}, u32[]{:S(2)}) async-start(bf16[8,48,384]{2,1,0:T(8,128)(2,1)} %shard_map.97), calls=%async_computation.2 | async-start | bytes 589824 | tf_op jit(solution)/shard_map/all_to_all | solution.py:292
  176.1 8.7 %collective-permute-start.14 = (bf16[64,896]{1,0:T(8,128)(2,1)S(1)}, bf16[64,896]{1,0:T(8,128)(2,1)S(1)}, u32[]{:S(2)}, u32[]{:S(2)}) collective-permute-start(bf16[64,896]{1,0:T(8,128)(2,1)S(1)} %get-tuple-element.37), channel_id=1, source_target_pairs={{0,128},{128,256},{256,384},{384,0},{1,129},{129,257},{257,385},{3... | collective-permute-start | bytes 344072 | tf_op jit(solution)/shard_map/ppermute | solution.py:197
  178.3 9.9 %collective-permute-start.15 = (bf16[64,896]{1,0:T(8,128)(2,1)S(1)}, bf16[64,896]{1,0:T(8,128)(2,1)S(1)}, u32[]{:S(2)}, u32[]{:S(2)}) collective-permute-start(bf16[64,896]{1,0:T(8,128)(2,1)S(1)} %get-tuple-element.38), channel_id=1, source_target_pairs={{0,256},{128,384},{256,0},{384,128},{1,257},{129,385},{257,1},{385... | collective-permute-start | bytes 344072 | tf_op jit(solution)/shard_map/ppermute | solution.py:197
  182.7 14.8 %collective-permute-start.16 = (bf16[64,896]{1,0:T(8,128)(2,1)S(1)}, bf16[64,896]{1,0:T(8,128)(2,1)S(1)}, u32[]{:S(2)}, u32[]{:S(2)}) collective-permute-start(bf16[64,896]{1,0:T(8,128)(2,1)S(1)} %get-tuple-element.39), channel_id=1, source_target_pairs={{0,384},{128,0},{256,128},{384,256},{1,385},{129,1},{257,129},{385... | collective-permute-start | bytes 344072 | tf_op jit(solution)/shard_map/ppermute | solution.py:197
